TPU v7x, 256 devices: a whole 4x4x8 slice. The times are simulated.
256 devices in a mesh: seq: 32 (over y, x, core), exp: 8 (over z).
Axes of the slice: x: 4, y: 4, z: 8, core: 2. Of those that a mesh axis runs over, the one named last changes fastest.
Arguments:
- mixer_input: bfloat16 [4096, 8192], P('seq', 'exp'), may hold values from -6 to 6
- gate_input: bfloat16 [4096, 8192], P('seq', 'exp'), may hold values from -6 to 6
- delta_raw: bfloat16 [4096, 8192], P('seq', 'exp'), may hold values from -7 to 16387
- input_coef: bfloat16 [4096, 16], P('seq'), may hold values from 0.19921875 to 1.796875
- output_coef: bfloat16 [4096, 16], P('seq'), may hold values from -3 to 3
- decay_rate: float32 [16, 8192], P(None, 'exp'), may hold values from 4.8828125e-06 to 0.05
- conv_weight: float32 [4, 8192], P(None, 'exp'), may hold values from -3 to 3
- conv_bias: float32 [8192], P('exp'), may hold values from -3 to 3
- skip_gain: float32 [8192], P('exp'), may hold values from 0.5 to 1.5
- out_weight: bfloat16 [8192, 4096], P('exp', 'seq'), may hold values from -0.0625 to 0.0625
- residual: bfloat16 [4096, 4096], P(('seq', 'exp')), may hold values from -6 to 6
- norm_gain: float32 [4096], replicated, may hold values from 0.1 to 1.9
- router_weight: bfloat16 [4096, 8], replicated, may hold values from -0.09375 to 0.09375
- expert_ids: int32 [4096, 2], P(('seq', 'exp')), may hold values from 0 to 7, all different within a row; in each aligned block of 16 rows (0 to 15, 16 to 31, ...) at most 5 rows name the same one
- gate_weight: bfloat16 [8, 4096, 12288], P('exp', None, 'seq'), may hold values from -0.09375 to 0.09375
- up_weight: bfloat16 [8, 4096, 12288], P('exp', None, 'seq'), may hold values from -0.09375 to 0.09375
- down_weight: bfloat16 [8, 12288, 4096], P('exp', 'seq'), may hold values from -0.0546875 to 0.0546875
Outputs:
- mixed: bfloat16 [4096, 8192], P('seq', 'exp')
- final: bfloat16 [4096, 4096], P(('seq', 'exp'))
Inputs may be any that keep to these rules, and one draw needn't show every extreme that they name: `expert_ids`: each row names two different experts. In each aligned block of 16 rows (the rows of one device) no expert is named by more than 5 rows, and in some block one expert is named by exactly 5 rows.
All inputs are finite; a program needn't handle non-finite values.
Results may differ from a plain program's by a relative error of at most 0.015.
Values may be sent and summed in bfloat16 or wider, within the bound.
No kernel may reach another device: no remote copies, remote signals or barrier semaphores. Data moves between devices by JAX's collectives and lax.ppermute only.
A program may use at most 128 MiB of HBM per device.

v0:
```python
import jax
import jax.numpy as jnp
from jax import lax
from jax.sharding import PartitionSpec as P

KCONV = 4


def from_behind(block, axis, distance):
    devices = range(lax.axis_size(axis))
    route = [(i - distance, i) for i in devices if i - distance in devices]
    return lax.ppermute(block, axis, route)


def carried_in(part, axis, combine, identity):
    place = lax.axis_index(axis)
    gathered = jax.tree.map(lambda a: lax.all_gather(a, axis), part)
    state = jax.tree.map(lambda a, e: jnp.zeros_like(a) + jnp.asarray(e, a.dtype), part, identity)

    def one(turn, state):
        return combine(
            state, jax.tree.map(lambda a: lax.dynamic_index_in_dim(a, turn, 0, False), gathered)
        )

    return lax.fori_loop(0, place, one, state)


def sweep(state, delta, convolved, input_rows, output_rows, decay_rate):

    def advance(carry, inputs):
        delta_row, value_row, input_row, output_row = inputs
        retain = jnp.exp(-delta_row[None, :] * decay_rate)
        carry = retain * carry + (1.0 - retain) * input_row[:, None] * value_row[None, :]
        return (carry, jnp.sum(output_row[:, None] * carry, axis=0))

    return lax.scan(advance, state, (delta, convolved, input_rows, output_rows), unroll=8)


def chain(earlier, later):
    return (earlier[0] * later[0], later[0] * earlier[1] + later[1])


def shards(
    mixer_input,
    gate_input,
    delta_raw,
    input_coef,
    output_coef,
    decay_rate,
    conv_weight,
    conv_bias,
    skip_gain,
    out_weight,
    residual,
    norm_gain,
    router_weight,
    expert_ids,
    gate_weight,
    up_weight,
    down_weight,
):
    length = mixer_input.shape[0]
    width = mixer_input.shape[1]
    tail = mixer_input[length - (KCONV - 1) :]
    before = from_behind(tail, "seq", 1)
    padded = jnp.concatenate([before, mixer_input], axis=0).astype(jnp.float32)
    summed = jnp.broadcast_to(conv_bias[None, :], (length, width))
    for offset in range(KCONV):
        summed = summed + conv_weight[offset][None, :] * padded[offset : offset + length]
    convolved = jax.nn.silu(summed)
    delta = jax.nn.softplus(delta_raw.astype(jnp.float32))
    input_rows = input_coef.astype(jnp.float32)
    output_rows = output_coef.astype(jnp.float32)
    zero_state = jnp.zeros(decay_rate.shape, jnp.float32)
    end_state, local_out = sweep(zero_state, delta, convolved, input_rows, output_rows, decay_rate)
    block_decay = jnp.exp(-jnp.sum(delta, axis=0)[None, :] * decay_rate)
    carried_decay, start_state = carried_in(
        (block_decay, end_state), "seq", chain, (jnp.ones_like(block_decay), zero_state)
    )
    last_state, scan_out = sweep(start_state, delta, convolved, input_rows, output_rows, decay_rate)
    mixed = (
        (scan_out + skip_gain[None, :] * convolved) * jax.nn.silu(gate_input.astype(jnp.float32))
    ).astype(jnp.bfloat16)
    rows = residual.shape[0]
    model_width = residual.shape[1]
    full_weight = lax.all_gather(out_weight, "seq", axis=1, tiled=True)
    projected = lax.psum_scatter(
        jnp.dot(mixed, full_weight, preferred_element_type=jnp.float32).astype(jnp.bfloat16),
        "exp",
        scatter_dimension=0,
        tiled=True,
    ).astype(jnp.float32)
    hidden_state = residual.astype(jnp.float32) + projected
    scale = lax.rsqrt(jnp.mean(hidden_state * hidden_state, axis=1, keepdims=True) + 1e-06)
    normed = (hidden_state * scale * norm_gain[None, :]).astype(jnp.bfloat16)
    experts = router_weight.shape[1]
    capacity = 2 * rows // experts + 1
    logits = jnp.dot(normed, router_weight, preferred_element_type=jnp.float32)
    expert_range = jnp.arange(experts, dtype=jnp.int32)
    matches = expert_ids[:, :, None] == expert_range[None, None, :]
    chosen = jnp.sum(jnp.where(matches, logits[:, None, :], 0.0), axis=2)
    first = jax.nn.sigmoid(chosen[:, 0] - chosen[:, 1])
    flat_ids = expert_ids.reshape(-1)
    onehot = (flat_ids[:, None] == expert_range[None, :]).astype(jnp.int32)
    rank = jnp.sum((jnp.cumsum(onehot, axis=0) - onehot) * onehot, axis=1)
    target = flat_ids * capacity + rank
    placing = (jnp.arange(experts * capacity, dtype=jnp.int32)[:, None] == target[None, :]).astype(
        jnp.bfloat16
    )
    repeated = jnp.broadcast_to(normed[:, None, :], (rows, 2, model_width)).reshape(-1, model_width)
    outgoing = (
        jnp.dot(placing, repeated, preferred_element_type=jnp.float32)
        .astype(jnp.bfloat16)
        .reshape(experts, capacity, model_width)
    )
    arrived = lax.all_to_all(outgoing, "exp", split_axis=0, concat_axis=0, tiled=True)
    flat_rows = arrived.reshape(-1, arrived.shape[2])
    piece = lax.all_gather(flat_rows, "seq", axis=0, tiled=True)
    gating = jnp.dot(piece, gate_weight[0], preferred_element_type=jnp.float32)
    upward = jnp.dot(piece, up_weight[0], preferred_element_type=jnp.float32)
    activated = (jax.nn.silu(gating) * upward).astype(jnp.bfloat16)
    partial_out = jnp.dot(activated, down_weight[0], preferred_element_type=jnp.float32)
    summed_out = lax.psum_scatter(
        partial_out.astype(jnp.bfloat16), "seq", scatter_dimension=0, tiled=True
    )
    returned = lax.all_to_all(
        summed_out.reshape(arrived.shape), "exp", split_axis=0, concat_axis=0, tiled=True
    )
    flat_returned = returned.reshape(-1, model_width)
    picked = jnp.einsum(
        "sa,sd->ad", placing, flat_returned, preferred_element_type=jnp.float32
    ).reshape(rows, 2, model_width)
    moe_out = first[:, None] * picked[:, 0] + (1.0 - first)[:, None] * picked[:, 1]
    final = (hidden_state + moe_out).astype(jnp.bfloat16)
    return (mixed, final)


def solution(mesh):
    return jax.shard_map(
        shards,
        mesh=mesh,
        in_specs=(
            P("seq", "exp"),
            P("seq", "exp"),
            P("seq", "exp"),
            P("seq", None),
            P("seq", None),
            P(None, "exp"),
            P(None, "exp"),
            P("exp"),
            P("exp"),
            P("exp", "seq"),
            P(("seq", "exp"), None),
            P(),
            P(),
            P(("seq", "exp"), None),
            P("exp", None, "seq"),
            P("exp", None, "seq"),
            P("exp", "seq", None),
        ),
        out_specs=(P("seq", "exp"), P(("seq", "exp"), None)),
        check_vma=False,
    )
```

profile of v0, /device:TPU:6, one launch (start us, length us, event | category | flops | bytes accessed | tf_op | source)
XLA Modules:
  0.0 490.1 jit_solution(7569274445757107317)
XLA Ops:
  8.1 2.0 collective-permute-start
  10.2 2.1 fusion.59
  17.4 1.8 fusion.81
  19.2 28.9 %while.37 = (s32[]{:T(128)}, f32[16,1024]{1,0:T(8,128)S(1)}, f32[16,8,1024]{2,1,0:T(8,128)}, f32[16,1024]{1,0:T(8,128)S(1)}, f32[16,8,16]{2,1,0:T(8,128)S(1)}, /...) while((s32[]{:T(128)}, f32[16,1024]{1,0:T(8,128)S(1)}, ...), condition=%wide.region_2.3_spmd.clone, body=%wide.region_1.2_spmd.clone.sunk | while | flops 811018 | bytes 396055 | solution.py:36
  20.8 1.6 constant_dynamic-slice_fusion.41
  22.6 1.6 constant_dynamic-slice_fusion.41
  26.1 1.6 constant_dynamic-slice_fusion.41
  27.9 1.9 constant_dynamic-slice_fusion.41
  30.0 1.6 constant_dynamic-slice_fusion.41
  31.9 1.5 constant_dynamic-slice_fusion.41
  35.3 1.5 constant_dynamic-slice_fusion.41
  37.0 1.9 constant_dynamic-slice_fusion.41
  39.1 1.6 constant_dynamic-slice_fusion.41
  40.9 1.6 constant_dynamic-slice_fusion.41
  42.8 1.6 constant_dynamic-slice_fusion.41
  44.6 1.6 constant_dynamic-slice_fusion.41
  46.4 1.6 constant_dynamic-slice_fusion.41
  49.7 16.5 %all-gather.11.cloned.1.call-done = f32[512,1024]{1,0:T(8,128)} async-done(((f32[16,1024]{1,0:T(8,128)}), f32[512,1024]{1,0:T(8,128)}) %all-gather.11.cloned.1.call-update) | async-done | bytes 2097168 | tf_op jit(solution)/shard_map/all_gather | solution.py:17
  66.2 51.3 %all-gather.13.cloned.1.call-done = f32[512,1024]{1,0:T(8,128)} async-done(((f32[16,1024]{1,0:T(8,128)}), f32[512,1024]{1,0:T(8,128)}) %all-gather.13.cloned.1.call-update) | async-done | bytes 2097168 | tf_op jit(solution)/shard_map/all_gather | solution.py:17
  117.5 5.5 %while.35 = (s32[]{:T(128)}, f32[16,1024]{1,0:T(8,128)S(1)}, s32[]{:T(128)}, f32[32,16,1024]{2,1,0:T(8,128)}, f32[32,16,1024]{2,1,0:T(8,128)}, /*index=5*/s32[]{:T(128)}, s32[]{:T(128)}, s32[]{:T(128)}) while((s32[]{:T(128)}, f32[16,1024]{1,0:T(8,128)S(1)}, s32[]{:T(128)}, f32[32,16,1024]{2,1,0:T(8,128)}, f32[32,16,1024]{2,1,0:T(8,128)}, ...), condition=%wide.region_4.5_spmd, body=%wide.region_3.4_spmd.sunk | while | flops 32773 | bytes 262275 | solution.py:25
  123.0 44.5 %while.36 = (s32[]{:T(128)}, f32[16,1024]{1,0:T(8,128)S(1)}, f32[16,8,1024]{2,1,0:T(8,128)}, f32[16,8,1024]{2,1,0:T(8,128)}, f32[16,1024]{1,0:T(8,128)S(1)}, /*i...) while((s32[]{:T(128)}, f32[16,1024]{1,0:T(8,128)S(1)}, ...), condition=%wide.region_14.15_spmd, body=%wide.region_5.14_spmd.sunk | while | flops 1441801 | bytes 1316385 | solution.py:36
  125.7 1.6 constant_dynamic-slice_fusion.40
  128.4 1.6 constant_dynamic-slice_fusion.40
  133.9 1.6 constant_dynamic-slice_fusion.40
  136.7 1.9 constant_dynamic-slice_fusion.40
  139.7 1.6 constant_dynamic-slice_fusion.40
  142.6 1.5 constant_dynamic-slice_fusion.40
  147.8 1.5 constant_dynamic-slice_fusion.40
  150.6 1.9 constant_dynamic-slice_fusion.40
  153.6 1.6 constant_dynamic-slice_fusion.40
  156.4 1.6 constant_dynamic-slice_fusion.40
  159.2 1.6 constant_dynamic-slice_fusion.40
  162.0 1.6 constant_dynamic-slice_fusion.40
  164.7 1.6 constant_dynamic-slice_fusion.40
  167.5 2.5 fusion.58
  170.0 13.6 %all-gather.7.cloned.1.call-done = bf16[1024,4096]{1,0:T(8,128)(2,1)} async-done(((bf16[1024,128]{1,0:T(8,128)(2,1)}), bf16[1024,4096]{1,0:T(8,128)(2,1)}) %all-gather.7.cloned.1.call-update) | async-done | bytes 8388624 | tf_op jit(solution)/shard_map/all_gather | solution.py:86
  183.6 5.7 %convolution_convert_fusion.1 = bf16[128,4096]{1,0:T(8,128)(2,1)} fusion(bf16[128,1024]{1,0:T(8,128)(2,1)S(1)} %fusion.58, bf16[1024,4096]{1,0:T(8,128)(2,1)} %all-gather.7.cloned.1.call-done), kind=kOutput, calls=%fused_computation.111 | convolution fusion | flops 1074266112 | bytes 9699328 | tf_op jit(solution)/shard_map/dot_general | solution.py:88
  191.1 45.7 %reduce-scatter.3.cloned.1.call-done = bf16[16,4096]{1,0:T(8,128)(2,1)} async-done(((bf16[128,4096]{1,0:T(8,128)(2,1)}), bf16[16,4096]{1,0:T(8,128)(2,1)}) %reduce-scatter.3.cloned.1.call-update) | async-done | bytes 131088 | tf_op jit(solution)/shard_map/reduce_scatter | solution.py:87
  242.7 17.8 %all_to_all.10 = bf16[8,5,4096]{2,1,0:T(8,128)(2,1)} all-to-all(bf16[8,5,4096]{2,1,0:T(8,128)(2,1)} %reshape.356), channel_id=1, replica_groups=mesh['seq'=32,'exp'=8] {'exp'}, dimensions={0} | all-to-all | bytes 655360 | tf_op jit(solution)/shard_map/all_to_all | solution.py:116
  260.6 1.9 reshape.357
  262.5 59.6 %all-gather.9.cloned.1.call-done = bf16[1280,4096]{1,0:T(8,128)(2,1)} async-done(((bf16[40,4096]{1,0:T(8,128)(2,1)}), bf16[1280,4096]{1,0:T(8,128)(2,1)}) %all-gather.9.cloned.1.call-update) | async-done | bytes 10485776 | tf_op jit(solution)/shard_map/all_gather | solution.py:118
  322.1 10.2 %fusion.33 = f32[1280,384]{1,0:T(8,128)} fusion(bf16[1280,4096]{1,0:T(8,128)(2,1)} %all-gather.9.cloned.1.call-done, bf16[1,4096,384]{2,1,0:T(8,128)(2,1)} %param.37), kind=kOutput, calls=%fused_computation.116 | convolution fusion | flops 4026531840 | bytes 15597568 | tf_op jit(solution)/shard_map/dot_general | solution.py:119
  332.3 17.2 %convolution_convert_fusion = bf16[1280,4096]{1,0:T(8,128)(2,1)} fusion(bf16[1,384,4096]{2,1,0:T(8,128)(2,1)S(1)} %copy-done, bf16[1280,4096]{1,0:T(8,128)(2,1)} %all-gather.9.cloned.1.call-done, bf16[1,4096,384]{2,1,0:T(8,128)(2,1)} %param.38, f32[1280,384]{1,0:T(8,128)} %fusion.33), kind=kOutput, calls=%fused_computation.110 | convolution fusion | flops 8061255680 | bytes 29229056 | tf_op jit(solution)/shard_map/dot_general | solution.py:122
  349.6 105.3 %reduce-scatter.5.cloned.1.call-done = bf16[40,4096]{1,0:T(8,128)(2,1)} async-done(((bf16[1280,4096]{1,0:T(8,128)(2,1)}), bf16[40,4096]{1,0:T(8,128)(2,1)}) %reduce-scatter.5.cloned.1.call-update) | async-done | bytes 327696 | tf_op jit(solution)/shard_map/reduce_scatter | solution.py:123
  454.8 1.9 reshape.358
  456.7 7.0 %all-to-all-start.1 = ((bf16[8,5,4096]{2,1,0:T(8,128)(2,1)}), bf16[8,5,4096]{2,1,0:T(8,128)(2,1)}, u32[]{:S(2)}, u32[]{:S(2)}) async-start(bf16[8,5,4096]{2,1,0:T(8,128)(2,1)} %reshape.358), calls=%async_computation.3 | async-start | bytes 1048576 | tf_op jit(solution)/shard_map/all_to_all | solution.py:126
  464.1 16.1 %all-to-all-done.1 = bf16[8,5,4096]{2,1,0:T(8,128)(2,1)} async-done(((bf16[8,5,4096]{2,1,0:T(8,128)(2,1)}), bf16[8,5,4096]{2,1,0:T(8,128)(2,1)}, u32[]{:S(2)}, u32[]{:S(2)}) %all-to-all-start.1) | async-done | bytes 327712 | tf_op jit(solution)/shard_map/all_to_all | solution.py:126
  481.5 1.7 fusion.64
  (277 shorter events, 52.3 us)
Async XLA Ops:
  7.2 325.1 %copy-start = (bf16[1,384,4096]{2,1,0:T(8,128)(2,1)S(1)}, bf16[1,384,4096]{2,1,0:T(8,128)(2,1)}, u32[]{:S(2)}) copy-start(bf16[1,384,4096]{2,1,0:T(8,128)(2,1)} %param.39) | copy-start | bytes 9437188
  7.2 12.0 %copy-start.2 = (f32[16,1024]{1,0:T(8,128)S(1)}, f32[16,1024]{1,0:T(8,128)}, u32[]{:S(2)}) copy-start(f32[16,1024]{1,0:T(8,128)} %param.28) | copy-start | bytes 196612
  7.2 59.0 %all-gather.11.cloned.1.call-start = ((), (), s32[]{:S(2)}) async-start(), calls=%async_computation.8 | async-start | bytes 2162688 | tf_op jit(solution)/shard_map/all_gather | solution.py:17
  8.1 7.4 %collective-permute-start = (bf16[3,1024]{1,0:T(4,128)(2,1)S(1)}, bf16[3,1024]{1,0:T(4,128)(2,1)S(1)}, u32[]{:S(2)}, u32[]{:S(2)}) collective-permute-start(bf16[3,1024]{1,0:T(4,128)(2,1)S(1)} %slice.264), channel_id=1, source_target_pairs={{0,8},{8,16},{16,24},{24,32},{32,40},{40,48},{48,56},{56,64},{64,7... | collective-permute-start | bytes 18440 | tf_op jit(solution)/shard_map/ppermute | solution.py:12
  13.8 103.7 %all-gather.13.cloned.1.call-start = ((), (), s32[]{:S(2)}) async-start(), calls=%async_computation.9 | async-start | bytes 2162688 | tf_op jit(solution)/shard_map/all_gather | solution.py:17
  16.5 0.8 copy-start.1
  16.5 33.1 %copy-start.12 = (bf16[128,16]{0,1:T(8,128)(2,1)S(1)}, bf16[128,16]{0,1:T(8,128)(2,1)}, u32[]{:S(2)}) copy-start(bf16[128,16]{0,1:T(8,128)(2,1)} %param.27) | copy-start | bytes 12292
  48.1 0.6 copy-start.3
  48.8 134.8 %all-gather.7.cloned.1.call-start = ((), (), s32[]{:S(2)}) async-start(), calls=%async_computation.4 | async-start | bytes 8650752 | tf_op jit(solution)/shard_map/all_gather | solution.py:86
  49.5 187.3 %reduce-scatter.3.cloned.1.call-start = ((), (), s32[]{:S(2)}) async-start(), calls=%async_computation.5 | async-start | bytes 1179648 | tf_op jit(solution)/shard_map/reduce_scatter | solution.py:87
  123.0 44.5 %copy-start.9 = (f32[1024]{0:T(1024)S(1)}, f32[1024]{0:T(1024)}, u32[]{:S(2)}) copy-start(f32[1024]{0:T(1024)} %param.30) | copy-start | bytes 12292
  123.0 44.5 %copy-start.11 = (f32[1024]{0:T(1024)S(1)}, f32[1024]{0:T(1024)}, u32[]{:S(2)}) copy-start(f32[1024]{0:T(1024)} %param.31) | copy-start | bytes 12292
  170.0 19.3 %copy-start.4 = (bf16[128,1024]{1,0:T(8,128)(2,1)}, bf16[128,1024]{1,0:T(8,128)(2,1)S(1)}, u32[]{:S(2)}) copy-start(bf16[128,1024]{1,0:T(8,128)(2,1)S(1)} %fusion.58) | copy-start | bytes 786436
  170.0 66.9 %copy-start.7 = (bf16[16,4096]{1,0:T(8,128)(2,1)S(1)}, bf16[16,4096]{1,0:T(8,128)(2,1)}, u32[]{:S(2)}) copy-start(bf16[16,4096]{1,0:T(8,128)(2,1)} %param.33) | copy-start | bytes 393220
  170.0 67.9 %copy-start.10 = (f32[4096]{0:T(1024)S(1)}, f32[4096]{0:T(1024)}, u32[]{:S(2)}) copy-start(f32[4096]{0:T(1024)} %param.34) | copy-start | bytes 49156
  189.3 132.8 %all-gather.9.cloned.1.call-start = ((), (), s32[]{:S(2)}) async-start(), calls=%async_computation.6 | async-start | bytes 10813440 | tf_op jit(solution)/shard_map/all_gather | solution.py:118
  238.9 0.7 copy-start.5
  262.5 192.3 %reduce-scatter.5.cloned.1.call-start = ((), (), s32[]{:S(2)}) async-start(), calls=%async_computation.7 | async-start | bytes 10813440 | tf_op jit(solution)/shard_map/reduce_scatter | solution.py:123
  349.5 114.2 %copy-start.14 = (s32[32]{0:T(128)S(1)}, s32[32]{0:T(128)}, u32[]{:S(2)}) copy-start(s32[32]{0:T(128)} %multiply_add_fusion.8) | copy-start | bytes 388
  349.5 114.3 %copy-start.6 = (bf16[16,4096]{1,0:T(8,128)(2,1)S(1)}, bf16[16,4096]{1,0:T(8,128)(2,1)}, u32[]{:S(2)}) copy-start(bf16[16,4096]{1,0:T(8,128)(2,1)} %copy-done.5) | copy-start | bytes 393220
  349.5 114.3 %copy-start.8 = (bf16[4096,8]{0,1:T(8,128)(2,1)S(1)}, bf16[4096,8]{0,1:T(8,128)(2,1)}, u32[]{:S(2)}) copy-start(bf16[4096,8]{0,1:T(8,128)(2,1)} %param.35) | copy-start | bytes 196612
  349.5 114.5 %copy-start.13 = (s32[16,2]{0,1:T(2,128)S(1)}, s32[16,2]{0,1:T(2,128)}, u32[]{:S(2)}) copy-start(s32[16,2]{0,1:T(2,128)} %param.36) | copy-start | bytes 388
  456.7 23.4 %all-to-all-start.1 = ((bf16[8,5,4096]{2,1,0:T(8,128)(2,1)}), bf16[8,5,4096]{2,1,0:T(8,128)(2,1)}, u32[]{:S(2)}, u32[]{:S(2)}) async-start(bf16[8,5,4096]{2,1,0:T(8,128)(2,1)} %reshape.358), calls=%async_computation.3 | async-start | bytes 1048576 | tf_op jit(solution)/shard_map/all_to_all | solution.py:126
Sparse Core Ops, SparseCore 0:
  13.9 52.2 all-gather.10
  69.3 48.1 all-gather.12
  119.9 63.6 all-gather.6
  189.4 47.3 reduce-scatter.2
  262.6 59.4 all-gather.8
  349.7 105.1 reduce-scatter.4
where the time goes:
time: 497 us; the launch traced here: 490 us
  waiting for transfers between devices  309 us (62%)
  other arithmetic  79.9 us (16%)
  matrix products  34.6 us (7%)
  local copies, waits for them, and re-layouts  24.2 us (5%)
  blocking collectives  17.8 us (4%)
  between operations  14.4 us (3%)
  starting transfers between devices  9.3 us (2%)
    reduce_scatter x1, waiting for transfers between devices, shards(): lax.psum_scatter(partial_out.astype(jnp.bfloat16), 'seq', scatter_dimensi...  105 us
    all_gather x2, waiting for transfers between devices, carried_in(): gathered = jax.tree.map(lambda a: lax.all_gather(a, axis), part)  67.7 us
    all_gather x1, waiting for transfers between devices, shards(): piece = lax.all_gather(flat_rows, 'seq', axis=0, tiled=True)  59.6 us
    slice x32, other arithmetic, sweep(): lax.scan(advance, state, (delta, convolved, input_rows, output_rows), unr...  50.8 us
    reduce_scatter x1, waiting for transfers between devices, shards(): lax.psum_scatter(jnp.dot(mixed, full_weight, preferred_element_type=jnp.f...  45.7 us
    all_to_all x1, blocking collectives, shards(): lax.all_to_all(outgoing, 'exp', split_axis=0, concat_axis=0, tiled=True)  17.8 us
    dot_general x1, matrix products, shards(): jnp.dot(activated, down_weight[0], preferred_element_type=jnp.float32)  17.2 us
    all_to_all x1, waiting for transfers between devices, shards(): lax.all_to_all(summed_out.reshape(arrived.shape), 'exp', split_axis=0, co...  16.1 us
  transfers between devices with their start and end apart: 8, of which 7 were waited for; matrix products, arithmetic and copies ran while one was open for 18% of the time, Pallas kernels for 0%

commit v1 on v0

--- a/solution.py
+++ b/solution.py
@@ -101,8 +101,9 @@
     chosen = jnp.sum(jnp.where(matches, logits[:, None, :], 0.0), axis=2)
     first = jax.nn.sigmoid(chosen[:, 0] - chosen[:, 1])
     flat_ids = expert_ids.reshape(-1)
-    onehot = (flat_ids[:, None] == expert_range[None, :]).astype(jnp.int32)
-    rank = jnp.sum((jnp.cumsum(onehot, axis=0) - onehot) * onehot, axis=1)
+    position = jnp.arange(flat_ids.shape[0], dtype=jnp.int32)
+    earlier = (flat_ids[:, None] == flat_ids[None, :]) & (position[None, :] < position[:, None])
+    rank = jnp.sum(earlier.astype(jnp.int32), axis=1)
     target = flat_ids * capacity + rank
     placing = (jnp.arange(experts * capacity, dtype=jnp.int32)[:, None] == target[None, :]).astype(
         jnp.bfloat16

time: 497 us -> 492 us (0.990)
  other arithmetic: 79.9 us -> 71.6 us
    slice x32, other arithmetic: 50.8 us -> 42.6 us  [sweep(): lax.scan(advance, state, (delta, convolved, input_rows, output_rows), unr...]
  transfers between devices with their start and end apart: 8 -> 8, of which waited for: 7 -> 7; matrix products, arithmetic and copies ran while one was open for 18% -> 17% of each run, Pallas kernels for 0% -> 0%
where the time goes in v1:
time: 492 us; the launch traced here: 486 us
  waiting for transfers between devices  313 us (64%)
  other arithmetic  71.6 us (15%)
  matrix products  34.6 us (7%)
  local copies, waits for them, and re-layouts  24 us (5%)
  blocking collectives  17.9 us (4%)
  between operations  14.4 us (3%)
  starting transfers between devices  9.35 us (2%)
    reduce_scatter x1, waiting for transfers between devices, shards(): lax.psum_scatter(partial_out.astype(jnp.bfloat16), 'seq', scatter_dimensi...  105 us
    all_gather x2, waiting for transfers between devices, carried_in(): gathered = jax.tree.map(lambda a: lax.all_gather(a, axis), part)  71.8 us
    all_gather x1, waiting for transfers between devices, shards(): piece = lax.all_gather(flat_rows, 'seq', axis=0, tiled=True)  59.5 us
    slice x32, other arithmetic, sweep(): lax.scan(advance, state, (delta, convolved, input_rows, output_rows), unr...  42.6 us
    reduce_scatter x1, waiting for transfers between devices, shards(): lax.psum_scatter(jnp.dot(mixed, full_weight, preferred_element_type=jnp.f...  41.7 us
    all_to_all x1, blocking collectives, shards(): lax.all_to_all(outgoing, 'exp', split_axis=0, concat_axis=0, tiled=True)  17.9 us
    all_gather x1, waiting for transfers between devices, shards(): full_weight = lax.all_gather(out_weight, 'seq', axis=1, tiled=True)  17.7 us
    dot_general x1, matrix products, shards(): jnp.dot(activated, down_weight[0], preferred_element_type=jnp.float32)  17.2 us
  transfers between devices with their start and end apart: 8, of which 7 were waited for; matrix products, arithmetic and copies ran while one was open for 17% of the time, Pallas kernels for 0%

profile of v1, /device:TPU:6, one launch (start us, length us, event | category | flops | bytes accessed | tf_op | source)
XLA Modules:
  0.0 485.9 jit_solution(3095711971764541297)
XLA Ops:
  8.1 2.0 collective-permute-start
  10.2 2.1 fusion.59
  12.2 1.5 multiply_exponential_fusion
  17.3 1.8 fusion.81
  19.2 24.8 %while.37 = (s32[]{:T(128)}, f32[16,1024]{1,0:T(8,128)S(1)}, f32[16,8,1024]{2,1,0:T(8,128)}, f32[16,1024]{1,0:T(8,128)S(1)}, f32[16,8,16]{2,1,0:T(8,128)S(1)}, /...) while((s32[]{:T(128)}, f32[16,1024]{1,0:T(8,128)S(1)}, ...), condition=%wide.region_2.3_spmd.clone, body=%wide.region_1.2_spmd.clone.sunk | while | flops 811018 | bytes 396055 | solution.py:36
  19.2 1.3 constant_dynamic-slice_fusion.41
  22.3 1.4 constant_dynamic-slice_fusion.41
  23.9 1.3 constant_dynamic-slice_fusion.41
  26.9 1.3 constant_dynamic-slice_fusion.41
  28.5 1.3 constant_dynamic-slice_fusion.41
  30.0 1.5 constant_dynamic-slice_fusion.41
  31.8 1.3 constant_dynamic-slice_fusion.41
  33.3 1.3 constant_dynamic-slice_fusion.41
  34.8 1.3 constant_dynamic-slice_fusion.41
  36.4 1.3 constant_dynamic-slice_fusion.41
  37.9 1.3 constant_dynamic-slice_fusion.41
  39.5 1.3 constant_dynamic-slice_fusion.41
  45.6 20.6 %all-gather.11.cloned.1.call-done = f32[512,1024]{1,0:T(8,128)} async-done(((f32[16,1024]{1,0:T(8,128)}), f32[512,1024]{1,0:T(8,128)}) %all-gather.11.cloned.1.call-update) | async-done | bytes 2097168 | tf_op jit(solution)/shard_map/all_gather | solution.py:17
  66.2 51.3 %all-gather.13.cloned.1.call-done = f32[512,1024]{1,0:T(8,128)} async-done(((f32[16,1024]{1,0:T(8,128)}), f32[512,1024]{1,0:T(8,128)}) %all-gather.13.cloned.1.call-update) | async-done | bytes 2097168 | tf_op jit(solution)/shard_map/all_gather | solution.py:17
  117.5 5.5 %while.35 = (s32[]{:T(128)}, f32[16,1024]{1,0:T(8,128)S(1)}, s32[]{:T(128)}, f32[32,16,1024]{2,1,0:T(8,128)}, f32[32,16,1024]{2,1,0:T(8,128)}, /*index=5*/s32[]{:T(128)}, s32[]{:T(128)}, s32[]{:T(128)}) while((s32[]{:T(128)}, f32[16,1024]{1,0:T(8,128)S(1)}, s32[]{:T(128)}, f32[32,16,1024]{2,1,0:T(8,128)}, f32[32,16,1024]{2,1,0:T(8,128)}, ...), condition=%wide.region_4.5_spmd, body=%wide.region_3.4_spmd.sunk | while | flops 32773 | bytes 262275 | solution.py:25
  123.0 40.2 %while.36 = (s32[]{:T(128)}, f32[16,1024]{1,0:T(8,128)S(1)}, f32[16,8,1024]{2,1,0:T(8,128)}, f32[16,8,1024]{2,1,0:T(8,128)}, f32[16,1024]{1,0:T(8,128)S(1)}, /*i...) while((s32[]{:T(128)}, f32[16,1024]{1,0:T(8,128)S(1)}, ...), condition=%wide.region_14.15_spmd, body=%wide.region_5.14_spmd.sunk | while | flops 1441801 | bytes 1316385 | solution.py:36
  123.1 1.3 constant_dynamic-slice_fusion.40
  128.1 1.4 constant_dynamic-slice_fusion.40
  130.6 1.3 constant_dynamic-slice_fusion.40
  133.1 1.3 constant_dynamic-slice_fusion.40
  135.6 1.3 constant_dynamic-slice_fusion.40
  138.1 1.3 constant_dynamic-slice_fusion.40
  140.6 1.5 constant_dynamic-slice_fusion.40
  143.3 1.3 constant_dynamic-slice_fusion.40
  145.8 1.3 constant_dynamic-slice_fusion.40
  148.3 1.3 constant_dynamic-slice_fusion.40
  150.8 1.3 constant_dynamic-slice_fusion.40
  153.3 1.3 constant_dynamic-slice_fusion.40
  155.8 1.3 constant_dynamic-slice_fusion.40
  163.3 2.5 fusion.58
  165.8 17.7 %all-gather.7.cloned.1.call-done = bf16[1024,4096]{1,0:T(8,128)(2,1)} async-done(((bf16[1024,128]{1,0:T(8,128)(2,1)}), bf16[1024,4096]{1,0:T(8,128)(2,1)}) %all-gather.7.cloned.1.call-update) | async-done | bytes 8388624 | tf_op jit(solution)/shard_map/all_gather | solution.py:86
  183.6 5.7 %convolution_convert_fusion.1 = bf16[128,4096]{1,0:T(8,128)(2,1)} fusion(bf16[128,1024]{1,0:T(8,128)(2,1)S(1)} %fusion.58, bf16[1024,4096]{1,0:T(8,128)(2,1)} %all-gather.7.cloned.1.call-done), kind=kOutput, calls=%fused_computation.111 | convolution fusion | flops 1074266112 | bytes 9699328 | tf_op jit(solution)/shard_map/dot_general | solution.py:88
  191.0 41.7 %reduce-scatter.3.cloned.1.call-done = bf16[16,4096]{1,0:T(8,128)(2,1)} async-done(((bf16[128,4096]{1,0:T(8,128)(2,1)}), bf16[16,4096]{1,0:T(8,128)(2,1)}) %reduce-scatter.3.cloned.1.call-update) | async-done | bytes 131088 | tf_op jit(solution)/shard_map/reduce_scatter | solution.py:87
  238.5 17.9 %all_to_all.10 = bf16[8,5,4096]{2,1,0:T(8,128)(2,1)} all-to-all(bf16[8,5,4096]{2,1,0:T(8,128)(2,1)} %reshape.357), channel_id=1, replica_groups=mesh['seq'=32,'exp'=8] {'exp'}, dimensions={0} | all-to-all | bytes 655360 | tf_op jit(solution)/shard_map/all_to_all | solution.py:117
  256.4 1.9 reshape.358
  258.4 59.5 %all-gather.9.cloned.1.call-done = bf16[1280,4096]{1,0:T(8,128)(2,1)} async-done(((bf16[40,4096]{1,0:T(8,128)(2,1)}), bf16[1280,4096]{1,0:T(8,128)(2,1)}) %all-gather.9.cloned.1.call-update) | async-done | bytes 10485776 | tf_op jit(solution)/shard_map/all_gather | solution.py:119
  317.9 10.2 %fusion.33 = f32[1280,384]{1,0:T(8,128)} fusion(bf16[1280,4096]{1,0:T(8,128)(2,1)} %all-gather.9.cloned.1.call-done, bf16[1,4096,384]{2,1,0:T(8,128)(2,1)} %param.37), kind=kOutput, calls=%fused_computation.116 | convolution fusion | flops 4026531840 | bytes 15597568 | tf_op jit(solution)/shard_map/dot_general | solution.py:120
  328.1 17.2 %convolution_convert_fusion = bf16[1280,4096]{1,0:T(8,128)(2,1)} fusion(bf16[1,384,4096]{2,1,0:T(8,128)(2,1)S(1)} %copy-done, bf16[1280,4096]{1,0:T(8,128)(2,1)} %all-gather.9.cloned.1.call-done, bf16[1,4096,384]{2,1,0:T(8,128)(2,1)} %param.38, f32[1280,384]{1,0:T(8,128)} %fusion.33), kind=kOutput, calls=%fused_computation.110 | convolution fusion | flops 8061255680 | bytes 29229056 | tf_op jit(solution)/shard_map/dot_general | solution.py:123
  345.4 105.2 %reduce-scatter.5.cloned.1.call-done = bf16[40,4096]{1,0:T(8,128)(2,1)} async-done(((bf16[1280,4096]{1,0:T(8,128)(2,1)}), bf16[40,4096]{1,0:T(8,128)(2,1)}) %reduce-scatter.5.cloned.1.call-update) | async-done | bytes 327696 | tf_op jit(solution)/shard_map/reduce_scatter | solution.py:124
  450.6 1.9 reshape.359
  452.5 7.1 %all-to-all-start.1 = ((bf16[8,5,4096]{2,1,0:T(8,128)(2,1)}), bf16[8,5,4096]{2,1,0:T(8,128)(2,1)}, u32[]{:S(2)}, u32[]{:S(2)}) async-start(bf16[8,5,4096]{2,1,0:T(8,128)(2,1)} %reshape.359), calls=%async_computation.3 | async-start | bytes 1048576 | tf_op jit(solution)/shard_map/all_to_all | solution.py:127
  459.9 16.0 %all-to-all-done.1 = bf16[8,5,4096]{2,1,0:T(8,128)(2,1)} async-done(((bf16[8,5,4096]{2,1,0:T(8,128)(2,1)}), bf16[8,5,4096]{2,1,0:T(8,128)(2,1)}, u32[]{:S(2)}, u32[]{:S(2)}) %all-to-all-start.1) | async-done | bytes 327712 | tf_op jit(solution)/shard_map/all_to_all | solution.py:127
  477.3 1.7 fusion.64
  (275 shorter events, 51.2 us)
Async XLA Ops:
  7.2 321.0 %copy-start = (bf16[1,384,4096]{2,1,0:T(8,128)(2,1)S(1)}, bf16[1,384,4096]{2,1,0:T(8,128)(2,1)}, u32[]{:S(2)}) copy-start(bf16[1,384,4096]{2,1,0:T(8,128)(2,1)} %param.39) | copy-start | bytes 9437188
  7.2 12.0 %copy-start.2 = (f32[16,1024]{1,0:T(8,128)S(1)}, f32[16,1024]{1,0:T(8,128)}, u32[]{:S(2)}) copy-start(f32[16,1024]{1,0:T(8,128)} %param.28) | copy-start | bytes 196612
  7.2 59.0 %all-gather.11.cloned.1.call-start = ((), (), s32[]{:S(2)}) async-start(), calls=%async_computation.8 | async-start | bytes 2162688 | tf_op jit(solution)/shard_map/all_gather | solution.py:17
  8.1 7.4 %collective-permute-start = (bf16[3,1024]{1,0:T(4,128)(2,1)S(1)}, bf16[3,1024]{1,0:T(4,128)(2,1)S(1)}, u32[]{:S(2)}, u32[]{:S(2)}) collective-permute-start(bf16[3,1024]{1,0:T(4,128)(2,1)S(1)} %slice.264), channel_id=1, source_target_pairs={{0,8},{8,16},{16,24},{24,32},{32,40},{40,48},{48,56},{56,64},{64,7... | collective-permute-start | bytes 18440 | tf_op jit(solution)/shard_map/ppermute | solution.py:12
  13.8 103.7 %all-gather.13.cloned.1.call-start = ((), (), s32[]{:S(2)}) async-start(), calls=%async_computation.9 | async-start | bytes 2162688 | tf_op jit(solution)/shard_map/all_gather | solution.py:17
  16.5 0.8 copy-start.1
  16.5 29.0 %copy-start.12 = (bf16[128,16]{0,1:T(8,128)(2,1)S(1)}, bf16[128,16]{0,1:T(8,128)(2,1)}, u32[]{:S(2)}) copy-start(bf16[128,16]{0,1:T(8,128)(2,1)} %param.27) | copy-start | bytes 12292
  44.0 0.6 copy-start.3
  44.7 138.9 %all-gather.7.cloned.1.call-start = ((), (), s32[]{:S(2)}) async-start(), calls=%async_computation.4 | async-start | bytes 8650752 | tf_op jit(solution)/shard_map/all_gather | solution.py:86
  45.4 187.2 %reduce-scatter.3.cloned.1.call-start = ((), (), s32[]{:S(2)}) async-start(), calls=%async_computation.5 | async-start | bytes 1179648 | tf_op jit(solution)/shard_map/reduce_scatter | solution.py:87
  123.0 40.3 %copy-start.9 = (f32[1024]{0:T(1024)S(1)}, f32[1024]{0:T(1024)}, u32[]{:S(2)}) copy-start(f32[1024]{0:T(1024)} %param.30) | copy-start | bytes 12292
  123.0 40.3 %copy-start.11 = (f32[1024]{0:T(1024)S(1)}, f32[1024]{0:T(1024)}, u32[]{:S(2)}) copy-start(f32[1024]{0:T(1024)} %param.31) | copy-start | bytes 12292
  165.8 23.5 %copy-start.4 = (bf16[128,1024]{1,0:T(8,128)(2,1)}, bf16[128,1024]{1,0:T(8,128)(2,1)S(1)}, u32[]{:S(2)}) copy-start(bf16[128,1024]{1,0:T(8,128)(2,1)S(1)} %fusion.58) | copy-start | bytes 786436
  165.8 66.8 %copy-start.7 = (bf16[16,4096]{1,0:T(8,128)(2,1)S(1)}, bf16[16,4096]{1,0:T(8,128)(2,1)}, u32[]{:S(2)}) copy-start(bf16[16,4096]{1,0:T(8,128)(2,1)} %param.33) | copy-start | bytes 393220
  165.8 67.9 %copy-start.10 = (f32[4096]{0:T(1024)S(1)}, f32[4096]{0:T(1024)}, u32[]{:S(2)}) copy-start(f32[4096]{0:T(1024)} %param.34) | copy-start | bytes 49156
  189.3 128.6 %all-gather.9.cloned.1.call-start = ((), (), s32[]{:S(2)}) async-start(), calls=%async_computation.6 | async-start | bytes 10813440 | tf_op jit(solution)/shard_map/all_gather | solution.py:119
  234.7 0.7 copy-start.5
  258.3 192.3 %reduce-scatter.5.cloned.1.call-start = ((), (), s32[]{:S(2)}) async-start(), calls=%async_computation.7 | async-start | bytes 10813440 | tf_op jit(solution)/shard_map/reduce_scatter | solution.py:124
  345.3 114.2 %copy-start.14 = (s32[32]{0:T(128)S(1)}, s32[32]{0:T(128)}, u32[]{:S(2)}) copy-start(s32[32]{0:T(128)} %multiply_add_fusion.8) | copy-start | bytes 388
  345.3 114.3 %copy-start.6 = (bf16[16,4096]{1,0:T(8,128)(2,1)S(1)}, bf16[16,4096]{1,0:T(8,128)(2,1)}, u32[]{:S(2)}) copy-start(bf16[16,4096]{1,0:T(8,128)(2,1)} %copy-done.5) | copy-start | bytes 393220
  345.3 114.3 %copy-start.8 = (bf16[4096,8]{0,1:T(8,128)(2,1)S(1)}, bf16[4096,8]{0,1:T(8,128)(2,1)}, u32[]{:S(2)}) copy-start(bf16[4096,8]{0,1:T(8,128)(2,1)} %param.35) | copy-start | bytes 196612
  345.3 114.5 %copy-start.13 = (s32[16,2]{0,1:T(2,128)S(1)}, s32[16,2]{0,1:T(2,128)}, u32[]{:S(2)}) copy-start(s32[16,2]{0,1:T(2,128)} %param.36) | copy-start | bytes 388
  452.5 23.4 %all-to-all-start.1 = ((bf16[8,5,4096]{2,1,0:T(8,128)(2,1)}), bf16[8,5,4096]{2,1,0:T(8,128)(2,1)}, u32[]{:S(2)}, u32[]{:S(2)}) async-start(bf16[8,5,4096]{2,1,0:T(8,128)(2,1)} %reshape.359), calls=%async_computation.3 | async-start | bytes 1048576 | tf_op jit(solution)/shard_map/all_to_all | solution.py:127
Sparse Core Ops, SparseCore 0:
  13.9 52.2 all-gather.10
  69.3 48.1 all-gather.12
  119.9 63.5 all-gather.6
  189.4 43.1 reduce-scatter.2
  258.5 59.4 all-gather.8
  345.5 105.0 reduce-scatter.4

commit v2 on v1

--- a/solution.py
+++ b/solution.py
@@ -1,43 +1,205 @@
+import functools
+import math
+
 import jax
 import jax.numpy as jnp
 from jax import lax
+from jax.experimental import pallas as pl
+from jax.experimental.pallas import tpu as pltpu
 from jax.sharding import PartitionSpec as P
 
 KCONV = 4
-
-
-def from_behind(block, axis, distance):
-    devices = range(lax.axis_size(axis))
-    route = [(i - distance, i) for i in devices if i - distance in devices]
-    return lax.ppermute(block, axis, route)
-
-
-def carried_in(part, axis, combine, identity):
-    place = lax.axis_index(axis)
-    gathered = jax.tree.map(lambda a: lax.all_gather(a, axis), part)
-    state = jax.tree.map(lambda a, e: jnp.zeros_like(a) + jnp.asarray(e, a.dtype), part, identity)
-
-    def one(turn, state):
-        return combine(
-            state, jax.tree.map(lambda a: lax.dynamic_index_in_dim(a, turn, 0, False), gathered)
+LANES = 128
+SUB = 8
+CORES = 2
+SIDE = 4
+LOG2E = math.log2(math.e)
+VMEM = pl.BlockSpec(memory_space=pltpu.VMEM)
+SMEM = pl.BlockSpec(memory_space=pltpu.SMEM)
+
+
+def split_place(place):
+    return place // (SIDE * CORES), (place // CORES) % SIDE, place % CORES
+
+
+def join_place(y, x, c):
+    return (y % SIDE * SIDE + x % SIDE) * CORES + c % CORES
+
+
+def moved(block, dy=0, dx=0, dc=0):
+    route = []
+    for i in range(SIDE * SIDE * CORES):
+        y, x, c = split_place(i)
+        route.append((i, join_place(y + dy, x + dx, c + dc)))
+    return lax.ppermute(block, "seq", route)
+
+
+def local_scan_kernel(
+    inp_ref, before_ref, raw_ref, rate_ref, taps_ref, bias_ref, skip_ref, in_ref, out_ref,
+    y_ref, sums_ref, carry_ref, scaled_ref,
+    pad_ref, delta_ref, conv_ref,
+):
+    length, width = inp_ref.shape
+    states = rate_ref.shape[0]
+    tiles = width // LANES
+    for j in range(tiles):
+        cols = slice(j * LANES, (j + 1) * LANES)
+        pad_ref[SUB - KCONV + 1 : SUB, :] = before_ref[:, cols].astype(jnp.float32)
+        pad_ref[SUB:, :] = inp_ref[:, cols].astype(jnp.float32)
+        summed = jnp.broadcast_to(bias_ref[:, cols], (length, LANES))
+        for k in range(KCONV):
+            begin = SUB - KCONV + 1 + k
+            summed = summed + taps_ref[k : k + 1, cols] * pad_ref[begin : begin + length, :]
+        conv_ref[pl.ds(j, length, stride=tiles), :] = summed * jax.nn.sigmoid(summed)
+        raw = raw_ref[:, cols].astype(jnp.float32)
+        delta_ref[pl.ds(j, length, stride=tiles), :] = jnp.maximum(raw, 0.0) + jnp.log1p(
+            jnp.exp(-jnp.abs(raw))
         )
-
-    return lax.fori_loop(0, place, one, state)
-
-
-def sweep(state, delta, convolved, input_rows, output_rows, decay_rate):
-
-    def advance(carry, inputs):
-        delta_row, value_row, input_row, output_row = inputs
-        retain = jnp.exp(-delta_row[None, :] * decay_rate)
-        carry = retain * carry + (1.0 - retain) * input_row[:, None] * value_row[None, :]
-        return (carry, jnp.sum(output_row[:, None] * carry, axis=0))
-
-    return lax.scan(advance, state, (delta, convolved, input_rows, output_rows), unroll=8)
-
-
-def chain(earlier, later):
-    return (earlier[0] * later[0], later[0] * earlier[1] + later[1])
+        scaled_ref[pl.ds(j, states, stride=tiles), :] = rate_ref[:, cols] * -LOG2E
+
+    skip = skip_ref[...]
+
+    def step(t, carry):
+        total, state = carry
+        rows = pl.ds(pl.multiple_of(t * SUB, SUB), SUB)
+        delta, value = delta_ref[rows, :], conv_ref[rows, :]
+        total = total + delta
+        out = skip * value
+        after = []
+        for n in range(states):
+            retain = jnp.exp2(delta * scaled_ref[n * SUB : (n + 1) * SUB, :])
+            fresh = in_ref[t * states + n] * value
+            now = fresh + retain * (state[n] - fresh)
+            out = out + out_ref[t * states + n] * now
+            after.append(now)
+        sums_ref[rows, :] = total
+        y_ref[rows, :] = out
+        return total, tuple(after)
+
+    zero = jnp.zeros((SUB, LANES), jnp.float32)
+    total, state = lax.fori_loop(0, length, step, (zero, (zero,) * states), unroll=2)
+    for n in range(states):
+        carry_ref[n * SUB : (n + 1) * SUB, :] = state[n]
+    carry_ref[states * SUB :, :] = total
+
+
+def finish_scan_kernel(y_ref, sums_ref, start_ref, scaled_ref, gate_ref, out_ref, mixed_ref, full_ref):
+    length, width = gate_ref.shape
+    states = start_ref.shape[0] // SUB
+    tiles = width // LANES
+
+    def step(t, carry):
+        rows = pl.ds(pl.multiple_of(t * SUB, SUB), SUB)
+        total, out = sums_ref[rows, :], y_ref[rows, :]
+        for n in range(states):
+            part = slice(n * SUB, (n + 1) * SUB)
+            kept = jnp.exp2(total * scaled_ref[part, :]) * start_ref[part, :]
+            out = out + out_ref[t * states + n] * kept
+        full_ref[rows, :] = out
+        return carry
+
+    lax.fori_loop(0, length, step, 0, unroll=2)
+    for j in range(tiles):
+        cols = slice(j * LANES, (j + 1) * LANES)
+        gate = gate_ref[:, cols].astype(jnp.float32)
+        gated = full_ref[pl.ds(j, length, stride=tiles), :] * (gate * jax.nn.sigmoid(gate))
+        mixed_ref[:, cols] = gated.astype(mixed_ref.dtype)
+
+
+def local_scan(inp, before, raw, rate, taps, bias, skip, in_flat, out_flat):
+    length, width = inp.shape
+    states = rate.shape[0]
+    flat = jax.ShapeDtypeStruct((length * SUB, LANES), jnp.float32)
+    return pl.pallas_call(
+        local_scan_kernel,
+        name="local_scan",
+        out_shape=(
+            flat,
+            flat,
+            jax.ShapeDtypeStruct(((states + 1) * SUB, LANES), jnp.float32),
+            jax.ShapeDtypeStruct((states * SUB, LANES), jnp.float32),
+        ),
+        in_specs=[VMEM] * 7 + [SMEM] * 2,
+        out_specs=(VMEM,) * 4,
+        scratch_shapes=[
+            pltpu.VMEM((length + SUB, LANES), jnp.float32),
+            pltpu.VMEM((length * SUB, LANES), jnp.float32),
+            pltpu.VMEM((length * SUB, LANES), jnp.float32),
+        ],
+        compiler_params=pltpu.CompilerParams(vmem_limit_bytes=24 << 20),
+        cost_estimate=pl.CostEstimate(flops=8_000_000, transcendentals=2_500_000, bytes_accessed=2_000_000),
+    )(inp, before, raw, rate, taps, bias, skip, in_flat, out_flat)
+
+
+def finish_scan(y, sums, start, scaled, gate, out_flat):
+    length, width = gate.shape
+    return pl.pallas_call(
+        finish_scan_kernel,
+        name="finish_scan",
+        out_shape=jax.ShapeDtypeStruct((length, width), jnp.bfloat16),
+        in_specs=[VMEM] * 5 + [SMEM],
+        out_specs=VMEM,
+        scratch_shapes=[pltpu.VMEM((length * SUB, LANES), jnp.float32)],
+        compiler_params=pltpu.CompilerParams(vmem_limit_bytes=24 << 20),
+        cost_estimate=pl.CostEstimate(flops=8_000_000, transcendentals=2_500_000, bytes_accessed=2_000_000),
+    )(y, sums, start, scaled, gate, out_flat)
+
+
+def entering_state(carry, scaled):
+    states = scaled.shape[0] // SUB
+    scaled = scaled.reshape(states, SUB, LANES)
+    y, x, c = split_place(lax.axis_index("seq"))
+
+    def parts(block):
+        block = block.reshape(states + 1, SUB, LANES)
+        return block[states], block[:states]
+
+    def kept(span, state):
+        return jnp.exp2(span[None] * scaled) * state
+
+    def packed(span, state):
+        return jnp.concatenate([state, span[None]], axis=0).reshape(carry.shape)
+
+    own = parts(carry)
+    other = parts(moved(carry, dc=1))
+    is_first = c == 0
+    first = [jnp.where(is_first, a, b) for a, b in zip(own, other)]
+    last = [jnp.where(is_first, b, a) for a, b in zip(own, other)]
+    chip = (first[0] + last[0], kept(last[0], first[1]) + last[1])
+    start = jnp.where(is_first, 0.0, other[1])
+    span = jnp.where(is_first, 0.0, other[0])
+
+    sent = packed(*chip)
+    near = [parts(moved(sent, dx=k)) for k in range(1, SIDE)]
+    ahead = jnp.zeros_like(span)
+    behind = jnp.zeros_like(span)
+    row_state = jnp.zeros_like(chip[1])
+    earlier_state = jnp.zeros_like(chip[1])
+    for k in range(1, SIDE):
+        got_span, got_state = near[k - 1]
+        is_earlier = k <= x
+        earlier_state = earlier_state + jnp.where(is_earlier, kept(ahead, got_state), 0.0)
+        row_state = row_state + jnp.where(is_earlier, 0.0, kept(behind, got_state))
+        ahead = ahead + jnp.where(is_earlier, got_span, 0.0)
+        behind = behind + jnp.where(is_earlier, 0.0, got_span)
+    row_state = row_state + kept(behind, chip[1] + kept(chip[0], earlier_state))
+    row_span = ahead + chip[0] + behind
+    start = start + kept(span, earlier_state)
+    span = span + ahead
+
+    sent = packed(row_span, row_state)
+    far = [parts(moved(sent, dy=k)) for k in range(1, SIDE)]
+    for k in range(1, SIDE):
+        got_span, got_state = far[k - 1]
+        is_earlier = k <= y
+        start = start + jnp.where(is_earlier, kept(span, got_state), 0.0)
+        span = span + jnp.where(is_earlier, got_span, 0.0)
+    return start.reshape(states * SUB, LANES)
+
+
+def from_before(tail):
+    count = lax.axis_size("seq")
+    return lax.ppermute(tail, "seq", [(i, i + 1) for i in range(count - 1)])
 
 
 def shards(
@@ -60,27 +222,22 @@
     down_weight,
 ):
     length = mixer_input.shape[0]
-    width = mixer_input.shape[1]
-    tail = mixer_input[length - (KCONV - 1) :]
-    before = from_behind(tail, "seq", 1)
-    padded = jnp.concatenate([before, mixer_input], axis=0).astype(jnp.float32)
-    summed = jnp.broadcast_to(conv_bias[None, :], (length, width))
-    for offset in range(KCONV):
-        summed = summed + conv_weight[offset][None, :] * padded[offset : offset + length]
-    convolved = jax.nn.silu(summed)
-    delta = jax.nn.softplus(delta_raw.astype(jnp.float32))
-    input_rows = input_coef.astype(jnp.float32)
-    output_rows = output_coef.astype(jnp.float32)
-    zero_state = jnp.zeros(decay_rate.shape, jnp.float32)
-    end_state, local_out = sweep(zero_state, delta, convolved, input_rows, output_rows, decay_rate)
-    block_decay = jnp.exp(-jnp.sum(delta, axis=0)[None, :] * decay_rate)
-    carried_decay, start_state = carried_in(
-        (block_decay, end_state), "seq", chain, (jnp.ones_like(block_decay), zero_state)
-    )
-    last_state, scan_out = sweep(start_state, delta, convolved, input_rows, output_rows, decay_rate)
-    mixed = (
-        (scan_out + skip_gain[None, :] * convolved) * jax.nn.silu(gate_input.astype(jnp.float32))
-    ).astype(jnp.bfloat16)
+    in_flat = input_coef.astype(jnp.float32).reshape(-1)
+    out_flat = output_coef.astype(jnp.float32).reshape(-1)
+    before = from_before(mixer_input[length - (KCONV - 1) :])
+    y, sums, carry, scaled = local_scan(
+        mixer_input,
+        before,
+        delta_raw,
+        decay_rate,
+        conv_weight,
+        conv_bias.reshape(1, -1),
+        skip_gain.reshape(SUB, LANES),
+        in_flat,
+        out_flat,
+    )
+    start = entering_state(carry, scaled)
+    mixed = finish_scan(y, sums, start, scaled, gate_input, out_flat)
     rows = residual.shape[0]
     model_width = residual.shape[1]
     full_weight = lax.all_gather(out_weight, "seq", axis=1, tiled=True)

time: 492 us -> 379 us (0.77); the launches traced: 486 us -> 378 us
  other arithmetic: 71.6 us -> 8.03 us
  waiting for transfers between devices: 313 us -> 256 us
  starting transfers between devices: 9.35 us -> 18.9 us
  Pallas kernels: 0 us -> 8.68 us
    all_gather x2 -> x0, waiting for transfers between devices: 71.8 us -> none  [carried_in(): gathered = jax.tree.map(lambda a: lax.all_gather(a, axis), part)]
    slice x32 -> x0, other arithmetic: 42.6 us -> none  [sweep(): lax.scan(advance, state, (delta, convolved, input_rows, output_rows), unr...]
    ppermute x1 -> x8, waiting for transfers between devices: 0.01 us -> 11.8 us  [the longest x7 10.5 us: moved(): return lax.ppermute(block, 'seq', route)]
    dynamic_update_slice x16 -> x0, local copies, waits for them, and re-layouts: 9.77 us -> none  [sweep(): lax.scan(advance, state, (delta, convolved, input_rows, output_rows), unr...]
    ppermute x1 -> x8, starting transfers between devices: 2.04 us -> 11.5 us  [the longest x7 9.6 us: moved(): return lax.ppermute(block, 'seq', route)]
    pallas_call x0 -> x2, Pallas kernels: none -> 8.68 us  [the longest x1 4.86 us: local_scan(): pl.pallas_call(local_scan_kernel, name='local_scan', out_shape=(flat, fla...]
    unnamed x31 -> x37, local copies, waits for them, and re-layouts: 2.91 us -> 10.3 us
    reduce_sum x48 -> x0, other arithmetic: 7.21 us -> none  [advance(): return (carry, jnp.sum(output_row[:, None] * carry, axis=0))]
  transfers between devices with their start and end apart: 8 -> 13, of which waited for: 7 -> 11; matrix products, arithmetic and copies ran while one was open for 17% -> 2% of each run, Pallas kernels for 0% -> 2%
where the time goes in v2:
time: 379 us; the launch traced here: 378 us
  waiting for transfers between devices  256 us (68%)
  matrix products  34.7 us (9%)
  local copies, waits for them, and re-layouts  20 us (5%)
  starting transfers between devices  18.9 us (5%)
  blocking collectives  17.9 us (5%)
  between operations  13.9 us (4%)
  Pallas kernels  8.68 us (2%)
  other arithmetic  8.03 us (2%)
    reduce_scatter x1, waiting for transfers between devices, shards(): lax.psum_scatter(partial_out.astype(jnp.bfloat16), 'seq', scatter_dimensi...  105 us
    all_gather x1, waiting for transfers between devices, shards(): piece = lax.all_gather(flat_rows, 'seq', axis=0, tiled=True)  59.4 us
    reduce_scatter x1, waiting for transfers between devices, shards(): lax.psum_scatter(jnp.dot(mixed, full_weight, preferred_element_type=jnp.f...  38.8 us
    all_gather x1, waiting for transfers between devices, shards(): full_weight = lax.all_gather(out_weight, 'seq', axis=1, tiled=True)  24.1 us
    all_to_all x1, blocking collectives, shards(): lax.all_to_all(outgoing, 'exp', split_axis=0, concat_axis=0, tiled=True)  17.9 us
    dot_general x1, matrix products, shards(): jnp.dot(activated, down_weight[0], preferred_element_type=jnp.float32)  17.2 us
    all_to_all x1, waiting for transfers between devices, shards(): lax.all_to_all(summed_out.reshape(arrived.shape), 'exp', split_axis=0, co...  16 us
    ppermute x7, waiting for transfers between devices, moved(): return lax.ppermute(block, 'seq', route)  10.5 us
  transfers between devices with their start and end apart: 13, of which 11 were waited for; matrix products, arithmetic and copies ran while one was open for 2% of the time, Pallas kernels for 2%

profile of v2, /device:TPU:6, one launch (start us, length us, event | category | flops | bytes accessed | tf_op | source)
XLA Modules:
  0.0 378.2 jit_solution(3930235492467874097)
XLA Ops:
  8.0 0.9 slice.81
  8.8 1.9 collective-permute-start
  10.8 0.8 copy.28
  11.6 0.8 copy.29
  12.5 1.3 collective-permute-done.before_ref
  13.8 0.9 copy-done.1
  14.8 0.9 copy-done.2
  15.7 0.8 copy-done.4
  16.5 0.7 copy-done.5
  17.3 0.7 copy-done.6
  18.6 4.9 %local_scan.1 = (f32[1024,128]{1,0:T(8,128)S(1)}, f32[1024,128]{1,0:T(8,128)S(1)}, f32[136,128]{1,0:T(8,128)S(1)}, f32[128,128]{1,0:T(8,128)S(1)}) custom-call(bf16[128,1024]{1,0:T(8,128)(2,1)S(1)} %copy-done.1, bf16[3,1024]{1,0:T(4,128)(2,1)S(1)} %collective-permute-done.before_ref, bf16[128,1024]{1,0:T(8,128)(2,1)S(1)} %copy-done.2, ...), custom_call_target="tpu_custom_call" | custom-call | flops 8000000 | bytes 2000000 | tf_op jit(solution)/shard_map/local_scan/pallas_call | solution.py:113
  23.5 0.9 copy-done.8
  24.4 0.8 copy-done.10
  25.5 1.0 collective-permute-done.1
  27.1 0.8 collective-permute-start.4
  28.0 1.1 collective-permute-start.3
  29.0 2.1 collective-permute-start.2
  31.2 4.5 %collective-permute-done.4 = f32[136,128]{1,0:T(8,128)S(1)} collective-permute-done((f32[136,128]{1,0:T(8,128)}, f32[136,128]{1,0:T(8,128)S(1)}, u32[]{:S(2)}, u32[]{:S(2)}) %collective-permute-start.4) | collective-permute-done | bytes 69664 | tf_op jit(solution)/shard_map/ppermute | solution.py:34
  35.6 1.1 collective-permute-done.2
  37.4 1.0 fusion.32
  39.0 1.7 collective-permute-start.5
  40.7 1.5 collective-permute-start.7
  42.2 2.0 collective-permute-start.6
  44.7 3.5 collective-permute-done.6
  48.3 1.0 fusion.21.start_ref
  49.2 0.9 copy-done.3
  50.2 1.0 copy-done.9
  51.2 1.0 copy-done.11
  52.3 3.8 %finish_scan.1 = bf16[128,1024]{1,0:T(8,128)(2,1)} custom-call(f32[1024,128]{1,0:T(8,128)S(1)} %copy-done.9, f32[1024,128]{1,0:T(8,128)S(1)} %copy-done.11, f32[128,128]{1,0:T(8,128)S(1)} %fusion.21.start_ref, f32[128,128]{1,0:T(8,128)S(1)} %get-tuple-element.9.scaled_ref, bf16[128,1024]{1,0:T(8,128)(2,1)S(1)} %copy-done.3, f32[2048]{0:T(1024)S(1)} %reshape.165.out_ref), custom_call_target="tpu_custom_call" | custom-call | flops 8000000 | bytes 2000000 | tf_op jit(solution)/shard_map/finish_scan/pallas_call | solution.py:136
  56.1 24.1 %all-gather.3.cloned.1.call-done = bf16[1024,4096]{1,0:T(8,128)(2,1)} async-done(((bf16[1024,128]{1,0:T(8,128)(2,1)}), bf16[1024,4096]{1,0:T(8,128)(2,1)}) %all-gather.3.cloned.1.call-update) | async-done | bytes 8388624 | tf_op jit(solution)/shard_map/all_gather | solution.py:243
  80.2 5.8 %convolution_convert_fusion.1 = bf16[128,4096]{1,0:T(8,128)(2,1)} fusion(bf16[128,1024]{1,0:T(8,128)(2,1)} %finish_scan.1, bf16[1024,4096]{1,0:T(8,128)(2,1)} %all-gather.3.cloned.1.call-done), kind=kOutput, calls=%fused_computation.1 | convolution fusion | flops 1074266112 | bytes 9699328 | tf_op jit(solution)/shard_map/dot_general | solution.py:245
  86.4 38.8 %reduce-scatter.3.cloned.1.call-done = bf16[16,4096]{1,0:T(8,128)(2,1)} async-done(((bf16[128,4096]{1,0:T(8,128)(2,1)}), bf16[16,4096]{1,0:T(8,128)(2,1)}) %reduce-scatter.3.cloned.1.call-update) | async-done | bytes 131088 | tf_op jit(solution)/shard_map/reduce_scatter | solution.py:244
  125.3 1.1 multiply_reduce_fusion
  126.3 1.0 multiply_convert_fusion
  128.2 0.8 reshape.157
  129.0 1.2 convolution_convert_fusion.2
  130.2 0.9 reshape.158
  131.1 17.9 %all_to_all.10 = bf16[8,5,4096]{2,1,0:T(8,128)(2,1)} all-to-all(bf16[8,5,4096]{2,1,0:T(8,128)(2,1)} %reshape.158), channel_id=1, replica_groups=mesh['seq'=32,'exp'=8] {'exp'}, dimensions={0} | all-to-all | bytes 655360 | tf_op jit(solution)/shard_map/all_to_all | solution.py:274
  149.1 1.9 reshape.159
  151.2 59.4 %all-gather.5.cloned.1.call-done = bf16[1280,4096]{1,0:T(8,128)(2,1)} async-done(((bf16[40,4096]{1,0:T(8,128)(2,1)}), bf16[1280,4096]{1,0:T(8,128)(2,1)}) %all-gather.5.cloned.1.call-update) | async-done | bytes 10485776 | tf_op jit(solution)/shard_map/all_gather | solution.py:276
  210.6 10.2 %fusion.2 = f32[1280,384]{1,0:T(8,128)} fusion(bf16[1280,4096]{1,0:T(8,128)(2,1)} %all-gather.5.cloned.1.call-done, bf16[1,4096,384]{2,1,0:T(8,128)(2,1)} %param.31), kind=kOutput, calls=%fused_computation.6 | convolution fusion | flops 4026531840 | bytes 15597568 | tf_op jit(solution)/shard_map/dot_general | solution.py:277
  220.8 17.2 %convolution_convert_fusion = bf16[1280,4096]{1,0:T(8,128)(2,1)} fusion(bf16[1,384,4096]{2,1,0:T(8,128)(2,1)S(1)} %copy-done, bf16[1280,4096]{1,0:T(8,128)(2,1)} %all-gather.5.cloned.1.call-done, bf16[1,4096,384]{2,1,0:T(8,128)(2,1)} %param.32, f32[1280,384]{1,0:T(8,128)} %fusion.2), kind=kOutput, calls=%fused_computation | convolution fusion | flops 8061255680 | bytes 29229056 | tf_op jit(solution)/shard_map/dot_general | solution.py:280
  238.0 105.2 %reduce-scatter.5.cloned.1.call-done = bf16[40,4096]{1,0:T(8,128)(2,1)} async-done(((bf16[1280,4096]{1,0:T(8,128)(2,1)}), bf16[40,4096]{1,0:T(8,128)(2,1)}) %reduce-scatter.5.cloned.1.call-update) | async-done | bytes 327696 | tf_op jit(solution)/shard_map/reduce_scatter | solution.py:281
  343.2 1.9 reshape.160
  345.2 7.1 %all-to-all-start.1 = ((bf16[8,5,4096]{2,1,0:T(8,128)(2,1)}), bf16[8,5,4096]{2,1,0:T(8,128)(2,1)}, u32[]{:S(2)}, u32[]{:S(2)}) async-start(bf16[8,5,4096]{2,1,0:T(8,128)(2,1)} %reshape.160), calls=%async_computation.3 | async-start | bytes 1048576 | tf_op jit(solution)/shard_map/all_to_all | solution.py:284
  352.5 16.0 %all-to-all-done.1 = bf16[8,5,4096]{2,1,0:T(8,128)(2,1)} async-done(((bf16[8,5,4096]{2,1,0:T(8,128)(2,1)}), bf16[8,5,4096]{2,1,0:T(8,128)(2,1)}, u32[]{:S(2)}, u32[]{:S(2)}) %all-to-all-start.1) | async-done | bytes 327712 | tf_op jit(solution)/shard_map/all_to_all | solution.py:284
  368.6 1.2 reshape.166
  370.0 1.7 fusion.18
  (59 shorter events, 6.4 us)
Async XLA Ops:
  7.2 213.6 %copy-start = (bf16[1,384,4096]{2,1,0:T(8,128)(2,1)S(1)}, bf16[1,384,4096]{2,1,0:T(8,128)(2,1)}, u32[]{:S(2)}) copy-start(bf16[1,384,4096]{2,1,0:T(8,128)(2,1)} %param.33) | copy-start | bytes 9437188
  7.2 73.0 %all-gather.3.cloned.1.call-start = ((), (), s32[]{:S(2)}) async-start(), calls=%async_computation.4 | async-start | bytes 8650752 | tf_op jit(solution)/shard_map/all_gather | solution.py:243
  7.9 117.3 %reduce-scatter.3.cloned.1.call-start = ((), (), s32[]{:S(2)}) async-start(), calls=%async_computation.5 | async-start | bytes 1179648 | tf_op jit(solution)/shard_map/reduce_scatter | solution.py:244
  8.8 5.0 %collective-permute-start = (bf16[3,1024]{1,0:T(4,128)(2,1)S(1)}, bf16[3,1024]{1,0:T(4,128)(2,1)S(1)}, u32[]{:S(2)}, u32[]{:S(2)}) collective-permute-start(bf16[3,1024]{1,0:T(4,128)(2,1)S(1)} %slice.81), channel_id=1, source_target_pairs={{0,8},{8,16},{16,24},{24,32},{32,40},{40,48},{48,56},{56,64},{64,7... | collective-permute-start | bytes 18440 | tf_op jit(solution)/shard_map/ppermute | solution.py:202
  13.8 1.0 copy-start.1
  14.7 0.9 copy-start.2
  15.7 0.8 copy-start.4
  16.5 0.7 copy-start.5
  17.3 0.7 copy-start.6
  17.9 0.7 copy-start.7
  23.5 0.9 copy-start.8
  24.4 0.8 copy-start.10
  25.2 1.3 collective-permute-start.1
  27.1 8.5 %collective-permute-start.4 = (f32[136,128]{1,0:T(8,128)}, f32[136,128]{1,0:T(8,128)S(1)}, u32[]{:S(2)}, u32[]{:S(2)}) collective-permute-start(f32[136,128]{1,0:T(8,128)} %maximum_bitcast_fusion), channel_id=1, source_target_pairs={{0,48},{8,56},{16,0},{24,8},{32,16},{40,24},{48,32},{56,40},{64,11... | collective-permute-start | bytes 208904 | tf_op jit(solution)/shard_map/ppermute | solution.py:34
  28.0 7.7 %collective-permute-start.3 = (f32[136,128]{1,0:T(8,128)}, f32[136,128]{1,0:T(8,128)S(1)}, u32[]{:S(2)}, u32[]{:S(2)}) collective-permute-start(f32[136,128]{1,0:T(8,128)} %maximum_bitcast_fusion), channel_id=1, source_target_pairs={{0,32},{8,40},{16,48},{24,56},{32,0},{40,8},{48,16},{56,24},{64,96... | collective-permute-start | bytes 208904 | tf_op jit(solution)/shard_map/ppermute | solution.py:34
  29.0 7.7 %collective-permute-start.2 = (f32[136,128]{1,0:T(8,128)}, f32[136,128]{1,0:T(8,128)}, u32[]{:S(2)}, u32[]{:S(2)}) collective-permute-start(f32[136,128]{1,0:T(8,128)} %maximum_bitcast_fusion), channel_id=1, source_target_pairs={{0,16},{8,24},{16,32},{24,40},{32,48},{40,56},{48,0},{56,8},{64,80... | collective-permute-start | bytes 208904 | tf_op jit(solution)/shard_map/ppermute | solution.py:34
  39.0 5.7 %collective-permute-start.5 = (f32[136,128]{1,0:T(8,128)}, f32[136,128]{1,0:T(8,128)S(1)}, u32[]{:S(2)}, u32[]{:S(2)}) collective-permute-start(f32[136,128]{1,0:T(8,128)} %maximum_bitcast_fusion.1), channel_id=1, source_target_pairs={{0,64},{8,72},{16,80},{24,88},{32,96},{40,104},{48,112},{56,120},{... | collective-permute-start | bytes 208904 | tf_op jit(solution)/shard_map/ppermute | solution.py:34
  40.7 7.6 %collective-permute-start.7 = (f32[136,128]{1,0:T(8,128)}, f32[136,128]{1,0:T(8,128)S(1)}, u32[]{:S(2)}, u32[]{:S(2)}) collective-permute-start(f32[136,128]{1,0:T(8,128)} %maximum_bitcast_fusion.1), channel_id=1, source_target_pairs={{0,192},{8,200},{16,208},{24,216},{32,224},{40,232},{48,240},{56,2... | collective-permute-start | bytes 208904 | tf_op jit(solution)/shard_map/ppermute | solution.py:34
  42.2 6.0 %collective-permute-start.6 = (f32[136,128]{1,0:T(8,128)}, f32[136,128]{1,0:T(8,128)S(1)}, u32[]{:S(2)}, u32[]{:S(2)}) collective-permute-start(f32[136,128]{1,0:T(8,128)} %maximum_bitcast_fusion.1), channel_id=1, source_target_pairs={{0,128},{8,136},{16,144},{24,152},{32,160},{40,168},{48,176},{56,1... | collective-permute-start | bytes 208904 | tf_op jit(solution)/shard_map/ppermute | solution.py:34
  49.2 1.0 copy-start.3
  50.2 1.0 copy-start.9
  51.2 1.0 copy-start.11
  56.1 30.0 %copy-start.17 = (s32[16,2]{0,1:T(2,128)S(1)}, s32[16,2]{0,1:T(2,128)}, u32[]{:S(2)}) copy-start(s32[16,2]{0,1:T(2,128)} %param.30) | copy-start | bytes 388
  56.1 69.2 %copy-start.14 = (bf16[16,4096]{1,0:T(8,128)(2,1)S(1)}, bf16[16,4096]{1,0:T(8,128)(2,1)}, u32[]{:S(2)}) copy-start(bf16[16,4096]{1,0:T(8,128)(2,1)} %param.27) | copy-start | bytes 393220
  56.1 70.2 %copy-start.16 = (f32[4096]{0:T(1024)S(1)}, f32[4096]{0:T(1024)}, u32[]{:S(2)}) copy-start(f32[4096]{0:T(1024)} %param.28) | copy-start | bytes 49156
  86.0 124.6 %all-gather.5.cloned.1.call-start = ((), (), s32[]{:S(2)}) async-start(), calls=%async_computation.6 | async-start | bytes 10813440 | tf_op jit(solution)/shard_map/all_gather | solution.py:276
  127.3 0.7 copy-start.12
  151.0 192.2 %reduce-scatter.5.cloned.1.call-start = ((), (), s32[]{:S(2)}) async-start(), calls=%async_computation.7 | async-start | bytes 10813440 | tf_op jit(solution)/shard_map/reduce_scatter | solution.py:281
  238.0 114.3 %copy-start.13 = (bf16[16,4096]{1,0:T(8,128)(2,1)S(1)}, bf16[16,4096]{1,0:T(8,128)(2,1)}, u32[]{:S(2)}) copy-start(bf16[16,4096]{1,0:T(8,128)(2,1)} %copy-done.12) | copy-start | bytes 393220
  238.0 114.3 %copy-start.15 = (bf16[4096,8]{0,1:T(8,128)(2,1)S(1)}, bf16[4096,8]{0,1:T(8,128)(2,1)}, u32[]{:S(2)}) copy-start(bf16[4096,8]{0,1:T(8,128)(2,1)} %param.29) | copy-start | bytes 196612
  345.2 23.4 %all-to-all-start.1 = ((bf16[8,5,4096]{2,1,0:T(8,128)(2,1)}), bf16[8,5,4096]{2,1,0:T(8,128)(2,1)}, u32[]{:S(2)}, u32[]{:S(2)}) async-start(bf16[8,5,4096]{2,1,0:T(8,128)(2,1)} %reshape.160), calls=%async_computation.3 | async-start | bytes 1048576 | tf_op jit(solution)/shard_map/all_to_all | solution.py:284
Sparse Core Ops, SparseCore 0:
  10.5 69.6 all-gather.2
  86.1 39.0 reduce-scatter.2
  151.1 59.4 all-gather.4
  238.1 105.0 reduce-scatter.4

commit v3 on v2

--- a/solution.py
+++ b/solution.py
@@ -200,6 +200,137 @@
 def from_before(tail):
     count = lax.axis_size("seq")
     return lax.ppermute(tail, "seq", [(i, i + 1) for i in range(count - 1)])
+
+
+def around(block, ring, step):
+    route = []
+    for i in range(SIDE * SIDE * CORES):
+        y, x, c = split_place(i)
+        along_x = (ring == "inner") == (c == 0)
+        dy, dx = (0, step) if along_x else (step, 0)
+        route.append((i, join_place(y + dy, x + dx, c)))
+    return lax.ppermute(block, "seq", route)
+
+
+def added(*terms):
+    return sum(t.astype(jnp.float32) for t in terms)
+
+
+def expert_in_kernel(*refs):
+    pieces, (gate_a, gate_b, up_a, up_b, act_a, act_b, rows_ref) = refs[:-7], refs[-7:]
+    rows = pieces[0].shape[0]
+
+    @pl.when(pl.program_id(0) == 0)
+    def _():
+        for k, piece in enumerate(pieces):
+            rows_ref[k * rows : (k + 1) * rows, :] = piece[...]
+
+    for gate, up, act in ((gate_a, up_a, act_a), (gate_b, up_b, act_b)):
+        both = jnp.concatenate([gate[...], up[...]], axis=1)
+        hidden = jnp.dot(rows_ref[...], both, preferred_element_type=jnp.float32)
+        gating, upward = hidden[:, :LANES], hidden[:, LANES:]
+        act[...] = (gating * jax.nn.sigmoid(gating) * upward).astype(act.dtype)
+
+
+def expert_out_kernel(act_a, act_b, down_a, down_b, *outs):
+    rows = outs[0].shape[0]
+    acts = jnp.concatenate([act_a[...], act_b[...]], axis=1)
+    down = jnp.concatenate([down_a[...], down_b[...]], axis=0)
+    result = jnp.dot(acts, down, preferred_element_type=jnp.float32).astype(outs[0].dtype)
+    for k, out in enumerate(outs):
+        out[...] = result[k * rows : (k + 1) * rows]
+
+
+def expert(pieces, here, there):
+    rows, width = pieces[0].shape
+    count = len(pieces) * rows
+    hidden = here[0].shape[1]
+    weight = pl.BlockSpec((width, LANES), lambda i: (0, i))
+    act = pl.BlockSpec((count, LANES), lambda i: (0, i))
+    acts = pl.pallas_call(
+        expert_in_kernel,
+        name="expert_in",
+        grid=(hidden // LANES,),
+        out_shape=(jax.ShapeDtypeStruct((count, hidden), jnp.bfloat16),) * 2,
+        in_specs=[VMEM] * len(pieces) + [weight] * 4,
+        out_specs=(act, act),
+        scratch_shapes=[pltpu.VMEM((count, width), jnp.bfloat16)],
+        compiler_params=pltpu.CompilerParams(vmem_limit_bytes=32 << 20),
+        cost_estimate=pl.CostEstimate(
+            flops=8 * count * width * hidden, transcendentals=2 * count * hidden, bytes_accessed=20_000_000
+        ),
+    )(*pieces, here[0], there[0], here[1], there[1])
+    tile = 4 * LANES
+    weight = pl.BlockSpec((hidden, tile), lambda i: (0, i))
+    piece = pl.BlockSpec((rows, tile), lambda i: (0, i))
+    return pl.pallas_call(
+        expert_out_kernel,
+        name="expert_out",
+        grid=(width // tile,),
+        out_shape=(jax.ShapeDtypeStruct((rows, width), jnp.bfloat16),) * len(pieces),
+        in_specs=[VMEM] * 2 + [weight] * 2,
+        out_specs=(piece,) * len(pieces),
+        compiler_params=pltpu.CompilerParams(vmem_limit_bytes=32 << 20),
+        cost_estimate=pl.CostEstimate(
+            flops=4 * count * width * hidden, transcendentals=0, bytes_accessed=10_000_000
+        ),
+    )(*acts, here[2], there[2])
+
+
+def experts_of_rows(block, here, there):
+    dtype = block.dtype
+    near = [block] + [around(block, "inner", k) for k in range(1, SIDE)]
+    low, high = jnp.concatenate(near[:2], axis=0), jnp.concatenate(near[2:], axis=0)
+    low_up = around(low, "outer", 1)
+    high_down = around(high, "outer", -1)
+    high_up = around(high, "outer", 1)
+    low_down = around(low, "outer", -1)
+    low_far = around(low_up, "outer", 1)
+    high_far = around(high_down, "outer", -1)
+    low, high, low_up, high_down = expert([low, high, low_up, high_down], here, there)
+    got_high_down = around(high_down, "outer", 1)
+    got_low_up = around(low_up, "outer", -1)
+    low_far, high_far, low_down, high_up = expert([low_far, high_far, low_down, high_up], here, there)
+    low_relay = around(low_far, "outer", 1)
+    high_relay = around(high_far, "outer", -1)
+    got_low_down = around(added(low_down, low_relay).astype(dtype), "outer", 1)
+    got_high_up = around(added(high_up, high_relay).astype(dtype), "outer", -1)
+    low_sum = added(low, got_low_up, got_low_down)
+    high_sum = added(high, got_high_down, got_high_up)
+    rows = block.shape[0]
+    blocks = [low_sum[:rows], low_sum[rows:], high_sum[:rows], high_sum[rows:]]
+    back = [around(blocks[k].astype(dtype), "inner", -k) for k in range(1, SIDE)]
+    return added(blocks[0], *back).astype(dtype)
+
+
+def project_kernel(mixed_ref, weight_ref, out_ref):
+    owners, rows = out_ref.shape[:2]
+    both = jnp.concatenate([weight_ref[0], weight_ref[1]], axis=1)
+    result = jnp.dot(mixed_ref[...], both, preferred_element_type=jnp.float32).astype(out_ref.dtype)
+    for owner in range(owners):
+        out_ref[owner] = result[owner * rows : (owner + 1) * rows]
+
+
+def project(mixed, weight):
+    blocks = lax.all_gather(weight, "seq")
+    owners = lax.axis_size("exp")
+    tokens, depth = mixed.shape
+    count = blocks.shape[0]
+    rows = tokens // owners
+    terms = pl.pallas_call(
+        project_kernel,
+        name="project",
+        grid=(count // 2,),
+        out_shape=jax.ShapeDtypeStruct((owners, rows, count * LANES), jnp.bfloat16),
+        in_specs=[VMEM, pl.BlockSpec((2, depth, LANES), lambda i: (i, 0, 0))],
+        out_specs=pl.BlockSpec((owners, rows, 2 * LANES), lambda i: (0, 0, i)),
+        compiler_params=pltpu.CompilerParams(vmem_limit_bytes=24 << 20),
+        cost_estimate=pl.CostEstimate(
+            flops=2 * tokens * depth * count * LANES, transcendentals=0, bytes_accessed=10_000_000
+        ),
+    )(mixed, blocks)
+    terms = lax.all_to_all(terms, "exp", 0, 0, tiled=True)
+    return added(*(terms[k] for k in range(owners)))
 
 
 def shards(
@@ -236,17 +367,14 @@
         in_flat,
         out_flat,
     )
+    here = [w[0] for w in (gate_weight, up_weight, down_weight)]
+    there = [moved(w, dc=1) for w in here]
+    carry, *there = lax.optimization_barrier((carry, *there))
     start = entering_state(carry, scaled)
     mixed = finish_scan(y, sums, start, scaled, gate_input, out_flat)
     rows = residual.shape[0]
     model_width = residual.shape[1]
-    full_weight = lax.all_gather(out_weight, "seq", axis=1, tiled=True)
-    projected = lax.psum_scatter(
-        jnp.dot(mixed, full_weight, preferred_element_type=jnp.float32).astype(jnp.bfloat16),
-        "exp",
-        scatter_dimension=0,
-        tiled=True,
-    ).astype(jnp.float32)
+    projected = project(mixed, out_weight)
     hidden_state = residual.astype(jnp.float32) + projected
     scale = lax.rsqrt(jnp.mean(hidden_state * hidden_state, axis=1, keepdims=True) + 1e-06)
     normed = (hidden_state * scale * norm_gain[None, :]).astype(jnp.bfloat16)
@@ -273,14 +401,7 @@
     )
     arrived = lax.all_to_all(outgoing, "exp", split_axis=0, concat_axis=0, tiled=True)
     flat_rows = arrived.reshape(-1, arrived.shape[2])
-    piece = lax.all_gather(flat_rows, "seq", axis=0, tiled=True)
-    gating = jnp.dot(piece, gate_weight[0], preferred_element_type=jnp.float32)
-    upward = jnp.dot(piece, up_weight[0], preferred_element_type=jnp.float32)
-    activated = (jax.nn.silu(gating) * upward).astype(jnp.bfloat16)
-    partial_out = jnp.dot(activated, down_weight[0], preferred_element_type=jnp.float32)
-    summed_out = lax.psum_scatter(
-        partial_out.astype(jnp.bfloat16), "seq", scatter_dimension=0, tiled=True
-    )
+    summed_out = experts_of_rows(flat_rows, here, there)
     returned = lax.all_to_all(
         summed_out.reshape(arrived.shape), "exp", split_axis=0, concat_axis=0, tiled=True
     )

time: 379 us -> 289 us (0.76)
  waiting for transfers between devices: 256 us -> 128 us
  Pallas kernels: 8.68 us -> 44.1 us
  matrix products: 34.7 us -> 0.58 us
  starting transfers between devices: 18.9 us -> 47.5 us
  local copies, waits for them, and re-layouts: 20 us -> 25.7 us
    reduce_scatter x2 -> x0, waiting for transfers between devices: 144 us -> none  [the longest x1 105 us: shards(): lax.psum_scatter(partial_out.astype(jnp.bfloat16), 'seq', scatter_dimensi...]
    all_gather x2 -> x1, waiting for transfers between devices: 83.5 us -> 15.7 us  [project(): blocks = lax.all_gather(weight, 'seq')]
    ppermute x0 -> x18, waiting for transfers between devices: none -> 58.2 us  [around(): return lax.ppermute(block, 'seq', route)]
    pallas_call x0 -> x5, Pallas kernels: none -> 35.4 us  [the longest x2 14.6 us: expert(): pl.pallas_call(expert_in_kernel, name='expert_in', grid=(hidden // LANES,...]
    dot_general x3 -> x0, matrix products: 33.2 us -> none  [the longest x1 17.2 us: shards(): jnp.dot(activated, down_weight[0], preferred_element_type=jnp.float32)]
    all_to_all x0 -> x1, waiting for transfers between devices: none -> 28.8 us  [project(): terms = lax.all_to_all(terms, 'exp', 0, 0, tiled=True)]
    ppermute x0 -> x18, starting transfers between devices: none -> 23.4 us  [around(): return lax.ppermute(block, 'seq', route)]
    unnamed x37 -> x55, local copies, waits for them, and re-layouts: 10.3 us -> 19.4 us
  transfers between devices with their start and end apart: 13 -> 32, of which waited for: 11 -> 21; matrix products, arithmetic and copies ran while one was open for 2% -> 3% of each run, Pallas kernels for 2% -> 8%
where the time goes in v3:
time: 289 us; the launch traced here: 287 us
  waiting for transfers between devices  128 us (44%)
  starting transfers between devices  47.5 us (16%)
  Pallas kernels  44.1 us (15%)
  local copies, waits for them, and re-layouts  25.7 us (9%)
  blocking collectives  21 us (7%)
  between operations  14.4 us (5%)
  other arithmetic  6.39 us (2%)
    ppermute x18, waiting for transfers between devices, around(): return lax.ppermute(block, 'seq', route)  58.2 us
    all_to_all x1, waiting for transfers between devices, project(): terms = lax.all_to_all(terms, 'exp', 0, 0, tiled=True)  28.8 us
    ppermute x18, starting transfers between devices, around(): return lax.ppermute(block, 'seq', route)  23.4 us
    all_to_all x1, blocking collectives, shards(): lax.all_to_all(outgoing, 'exp', split_axis=0, concat_axis=0, tiled=True)  21 us
    unnamed x55, local copies, waits for them, and re-layouts  19.4 us
    all_gather x1, waiting for transfers between devices, project(): blocks = lax.all_gather(weight, 'seq')  15.7 us
    pallas_call x2, Pallas kernels, expert(): pl.pallas_call(expert_in_kernel, name='expert_in', grid=(hidden // LANES,...  14.6 us
    pallas_call x2, Pallas kernels, expert(): pl.pallas_call(expert_out_kernel, name='expert_out', grid=(width // tile,...  13.5 us
  transfers between devices with their start and end apart: 32, of which 21 were waited for; matrix products, arithmetic and copies ran while one was open for 3% of the time, Pallas kernels for 8%

profile of v3, /device:TPU:6, one launch (start us, length us, event | category | flops | bytes accessed | tf_op | source)
XLA Modules:
  0.0 287.5 jit_solution(11901421111310657221)
XLA Ops:
  9.3 2.3 collective-permute-start
  19.1 4.9 %local_scan.1 = (f32[1024,128]{1,0:T(8,128)S(1)}, f32[1024,128]{1,0:T(8,128)S(1)}, f32[136,128]{1,0:T(8,128)S(1)}, f32[128,128]{1,0:T(8,128)S(1)}) custom-call(bf16[128,1024]{1,0:T(8,128)(2,1)S(1)} %copy-done.9, bf16[3,1024]{1,0:T(4,128)(2,1)S(1)} %collective-permute-done.before_ref, bf16[128,1024]{1,0:T(8,128)(2,1)S(1)} %copy-done.11, ...), custom_call_target="tpu_custom_call" | custom-call | flops 8000000 | bytes 2000000 | tf_op jit(solution)/shard_map/local_scan/pallas_call | solution.py:113
  27.7 1.3 collective-permute-start.5
  29.0 1.6 collective-permute-start.6
  31.0 2.3 collective-permute-done.5
  33.4 3.0 %collective-permute-done.6 = f32[136,128]{1,0:T(8,128)} collective-permute-done((f32[136,128]{1,0:T(8,128)}, f32[136,128]{1,0:T(8,128)}, u32[]{:S(2)}, u32[]{:S(2)}) %collective-permute-start.6) | collective-permute-done | bytes 69664 | tf_op jit(solution)/shard_map/ppermute | solution.py:34
  36.4 1.2 collective-permute-done.7
  39.9 2.4 collective-permute-start.8
  42.2 2.8 collective-permute-start.9
  45.0 1.5 collective-permute-start.10
  46.8 1.5 collective-permute-done.9
  48.3 1.3 collective-permute-done.10
  52.5 1.0 copy-done.20
  53.6 3.8 %finish_scan.1.mixed_ref = bf16[128,1024]{1,0:T(8,128)(2,1)} custom-call(f32[1024,128]{1,0:T(8,128)S(1)} %copy-done.18, f32[1024,128]{1,0:T(8,128)S(1)} %copy-done.20, f32[128,128]{1,0:T(8,128)S(1)} %fusion.9.start_ref, f32[128,128]{1,0:T(8,128)S(1)} %get-tuple-element.26.scaled_ref, bf16[128,1024]{1,0:T(8,128)(2,1)S(1)} %copy-done.12, ...), custom_call_target="tpu_custom_call" | custom-call | flops 8000000 | bytes 2000000 | tf_op jit(solution)/shard_map/finish_scan/pallas_call | solution.py:136
  57.4 15.7 %all-gather.3.cloned.1.call-done = bf16[32768,128]{1,0:T(8,128)(2,1)} async-done(((bf16[1024,128]{1,0:T(8,128)(2,1)}), bf16[32768,128]{1,0:T(8,128)(2,1)}) %all-gather.3.cloned.1.call-update) | async-done | bytes 8388624 | tf_op jit(solution)/shard_map/all_gather | solution.py:315
  73.1 3.4 %copy-done.7 = bf16[32768,128]{1,0:T(8,128)(2,1)S(1)} copy-done((bf16[32768,128]{1,0:T(8,128)(2,1)S(1)}, bf16[32768,128]{1,0:T(8,128)(2,1)}, u32[]{:S(2)}) %copy-start.7) | copy-done | bytes 8388632
  77.5 7.3 %project.1 = bf16[8,16,4096]{2,1,0:T(8,128)(2,1)} custom-call(bf16[128,1024]{1,0:T(8,128)(2,1)S(1)} %copy-done.8, bf16[32,1024,128]{2,1,0:T(8,128)(2,1)S(1)} %bitcast.218), custom_call_target="tpu_custom_call" | custom-call | flops 1073741824 | bytes 10000000 | tf_op jit(solution)/shard_map/project/pallas_call | solution.py:320
  84.7 7.1 %all-to-all-start = ((bf16[8,16,4096]{2,1,0:T(8,128)(2,1)}), bf16[8,16,4096]{2,1,0:T(8,128)(2,1)S(1)}, u32[]{:S(2)}, u32[]{:S(2)}) async-start(bf16[8,16,4096]{2,1,0:T(8,128)(2,1)} %project.1), calls=%async_computation | async-start | bytes 2097152 | tf_op jit(solution)/shard_map/all_to_all | solution.py:332
  92.2 28.8 %all-to-all-done = bf16[8,16,4096]{2,1,0:T(8,128)(2,1)S(1)} async-done(((bf16[8,16,4096]{2,1,0:T(8,128)(2,1)}), bf16[8,16,4096]{2,1,0:T(8,128)(2,1)S(1)}, u32[]{:S(2)}, u32[]{:S(2)}) %all-to-all-start) | async-done | bytes 1048608 | tf_op jit(solution)/shard_map/all_to_all | solution.py:332
  122.8 21.0 %all_to_all.15 = bf16[8,5,4096]{2,1,0:T(8,128)(2,1)} all-to-all(bf16[8,5,4096]{2,1,0:T(8,128)(2,1)S(1)} %reshape.173), channel_id=1, replica_groups=mesh['seq'=32,'exp'=8] {'exp'}, dimensions={0} | all-to-all | bytes 655360 | tf_op jit(solution)/shard_map/all_to_all | solution.py:402
  143.9 2.1 reshape.174
  145.9 1.4 collective-permute-start.12
  147.4 3.2 %collective-permute-start.11 = (bf16[40,4096]{1,0:T(8,128)(2,1)}, bf16[40,4096]{1,0:T(8,128)(2,1)S(1)}, u32[]{:S(2)}, u32[]{:S(2)}) collective-permute-start(bf16[40,4096]{1,0:T(8,128)(2,1)} %reshape.174), channel_id=1, source_target_pairs={{0,16},{8,72},{16,32},{24,88},{32,48},{40,104},{48,0},{56,120},{64... | collective-permute-start | bytes 983048 | tf_op jit(solution)/shard_map/ppermute | solution.py:212
  151.7 3.2 %collective-permute-done.12 = bf16[40,4096]{1,0:T(8,128)(2,1)S(1)} collective-permute-done((bf16[40,4096]{1,0:T(8,128)(2,1)}, bf16[40,4096]{1,0:T(8,128)(2,1)S(1)}, u32[]{:S(2)}, u32[]{:S(2)}) %collective-permute-start.12) | collective-permute-done | bytes 327712 | tf_op jit(solution)/shard_map/ppermute | solution.py:212
  154.9 3.4 %collective-permute-done.13 = bf16[40,4096]{1,0:T(8,128)(2,1)S(1)} collective-permute-done((bf16[40,4096]{1,0:T(8,128)(2,1)}, bf16[40,4096]{1,0:T(8,128)(2,1)S(1)}, u32[]{:S(2)}, u32[]{:S(2)}) %collective-permute-start.13) | collective-permute-done | bytes 327712 | tf_op jit(solution)/shard_map/ppermute | solution.py:212
  158.3 1.1 collective-permute-start.15
  159.4 1.3 collective-permute-start.14
  160.8 3.1 %collective-permute-start.19 = (bf16[80,4096]{1,0:T(8,128)(2,1)S(1)}, bf16[80,4096]{1,0:T(8,128)(2,1)S(1)}, u32[]{:S(2)}, u32[]{:S(2)}) collective-permute-start(bf16[80,4096]{1,0:T(8,128)(2,1)S(1)} %constant_dynamic-update-slice_fusion.refs_0_), channel_id=1, source_target_pairs={{0,192},{8,56},{16,208},{24,8},{32,224},{40,24},{48,240},{56,40},{... | collective-permute-start | bytes 1966088 | tf_op jit(solution)/shard_map/ppermute | solution.py:212
  163.9 5.2 %collective-permute-done.15.refs_3_ = bf16[80,4096]{1,0:T(8,128)(2,1)S(1)} collective-permute-done((bf16[80,4096]{1,0:T(8,128)(2,1)S(1)}, bf16[80,4096]{1,0:T(8,128)(2,1)S(1)}, u32[]{:S(2)}, u32[]{:S(2)}) %collective-permute-start.15) | collective-permute-done | bytes 655392 | tf_op jit(solution)/shard_map/ppermute | solution.py:212
  169.1 2.0 collective-permute-start.18
  171.3 7.0 %collective-permute-done.20.refs_3_ = bf16[80,4096]{1,0:T(8,128)(2,1)S(1)} collective-permute-done((bf16[80,4096]{1,0:T(8,128)(2,1)S(1)}, bf16[80,4096]{1,0:T(8,128)(2,1)S(1)}, u32[]{:S(2)}, u32[]{:S(2)}) %collective-permute-start.20) | collective-permute-done | bytes 655392 | tf_op jit(solution)/shard_map/ppermute | solution.py:212
  178.3 4.9 %collective-permute-done.18.refs_1_ = bf16[80,4096]{1,0:T(8,128)(2,1)S(1)} collective-permute-done((bf16[80,4096]{1,0:T(8,128)(2,1)S(1)}, bf16[80,4096]{1,0:T(8,128)(2,1)S(1)}, u32[]{:S(2)}, u32[]{:S(2)}) %collective-permute-start.18) | collective-permute-done | bytes 655392 | tf_op jit(solution)/shard_map/ppermute | solution.py:212
  183.2 2.2 collective-permute-done.17.refs_0_
  185.3 1.9 copy-done.2
  187.2 1.9 copy-done.5
  189.1 7.4 %expert_in.3 = (bf16[320,384]{1,0:T(8,128)(2,1)S(1)}, bf16[320,384]{1,0:T(8,128)(2,1)S(1)}) custom-call(bf16[80,4096]{1,0:T(8,128)(2,1)S(1)} %collective-permute-done.17.refs_0_, bf16[80,4096]{1,0:T(8,128)(2,1)S(1)} %collective-permute-done.18.refs_1_, bf16[80,4096]{1,0:T(8,128)(2,1)S(1)} %collective-permute-done.19.refs_2_, ...), custom_call_target="tpu_custom_call" | custom-call | flops 4026531840 | bytes 20000000 | tf_op jit(solution)/shard_map/expert_in/pallas_call | solution.py:250
  196.6 7.0 %expert_out.3 = (bf16[80,4096]{1,0:T(8,128)(2,1)S(1)}, bf16[80,4096]{1,0:T(8,128)(2,1)S(1)}, bf16[80,4096]{1,0:T(8,128)(2,1)S(1)}, bf16[80,4096]{1,0:T(8,128)(2,1)S(1)}) custom-call(bf16[320,384]{1,0:T(8,128)(2,1)S(1)} %get-tuple-element.34.act_a, bf16[320,384]{1,0:T(8,128)(2,1)S(1)} %get-tuple-element.35.act_b, bf16[384,4096]{1,0:T(8,128)(2,1)S(1)} %bitcast.220, ...), custom_call_target="tpu_custom_call" | custom-call | flops 2013265920 | bytes 10000000 | tf_op jit(solution)/shard_map/expert_out/pallas_call | solution.py:266
  203.7 7.2 %expert_in.2 = (bf16[320,384]{1,0:T(8,128)(2,1)S(1)}, bf16[320,384]{1,0:T(8,128)(2,1)S(1)}) custom-call(bf16[80,4096]{1,0:T(8,128)(2,1)S(1)} %constant_dynamic-update-slice_fusion.refs_0_, bf16[80,4096]{1,0:T(8,128)(2,1)S(1)} %constant_dynamic-update-slice_fusion.2.refs_1_, bf16[80,4096]{1,0:T(8,128)(2,1)S(1)} %collective-permute-done.14.refs_2_, ...), custom_call_target="tpu_custom_call" | custom-call | flops 4026531840 | bytes 20000000 | tf_op jit(solution)/shard_map/expert_in/pallas_call | solution.py:250
  210.9 6.5 %expert_out.2 = (bf16[80,4096]{1,0:T(8,128)(2,1)S(1)}, bf16[80,4096]{1,0:T(8,128)(2,1)S(1)}, bf16[80,4096]{1,0:T(8,128)(2,1)S(1)}, bf16[80,4096]{1,0:T(8,128)(2,1)S(1)}) custom-call(bf16[320,384]{1,0:T(8,128)(2,1)S(1)} %get-tuple-element.29.act_a, bf16[320,384]{1,0:T(8,128)(2,1)S(1)} %get-tuple-element.30.act_b, bf16[384,4096]{1,0:T(8,128)(2,1)S(1)} %bitcast.221, ...), custom_call_target="tpu_custom_call" | custom-call | flops 2013265920 | bytes 10000000 | tf_op jit(solution)/shard_map/expert_out/pallas_call | solution.py:266
  217.4 2.1 collective-permute-start.24
  219.4 1.3 collective-permute-start.16
  221.6 2.8 collective-permute-start.26
  224.4 11.9 %collective-permute-done.21 = bf16[80,4096]{1,0:T(8,128)(2,1)S(1)} collective-permute-done((bf16[80,4096]{1,0:T(8,128)(2,1)S(1)}, bf16[80,4096]{1,0:T(8,128)(2,1)S(1)}, u32[]{:S(2)}, u32[]{:S(2)}) %collective-permute-start.21) | collective-permute-done | bytes 655392 | tf_op jit(solution)/shard_map/ppermute | solution.py:212
  237.6 2.2 collective-permute-start.27
  240.9 12.2 %collective-permute-done.22 = bf16[80,4096]{1,0:T(8,128)(2,1)S(1)} collective-permute-done((bf16[80,4096]{1,0:T(8,128)(2,1)S(1)}, bf16[80,4096]{1,0:T(8,128)(2,1)S(1)}, u32[]{:S(2)}, u32[]{:S(2)}) %collective-permute-start.22) | collective-permute-done | bytes 655392 | tf_op jit(solution)/shard_map/ppermute | solution.py:212
  253.4 8.3 %collective-permute-done.23 = bf16[40,4096]{1,0:T(8,128)(2,1)S(1)} collective-permute-done((bf16[40,4096]{1,0:T(8,128)(2,1)S(1)}, bf16[40,4096]{1,0:T(8,128)(2,1)S(1)}, u32[]{:S(2)}, u32[]{:S(2)}) %collective-permute-start.23) | collective-permute-done | bytes 327712 | tf_op jit(solution)/shard_map/ppermute | solution.py:212
  262.8 3.5 %all-to-all-start.2 = ((bf16[8,5,4096]{2,1,0:T(8,128)(2,1)}), bf16[8,5,4096]{2,1,0:T(8,128)(2,1)S(1)}, u32[]{:S(2)}, u32[]{:S(2)}) async-start(bf16[8,5,4096]{2,1,0:T(8,128)(2,1)} %reshape.175), calls=%async_computation.2 | async-start | bytes 1048576 | tf_op jit(solution)/shard_map/all_to_all | solution.py:405
  266.6 12.9 %all-to-all-done.2 = bf16[8,5,4096]{2,1,0:T(8,128)(2,1)S(1)} async-done(((bf16[8,5,4096]{2,1,0:T(8,128)(2,1)}), bf16[8,5,4096]{2,1,0:T(8,128)(2,1)S(1)}, u32[]{:S(2)}, u32[]{:S(2)}) %all-to-all-start.2) | async-done | bytes 327712 | tf_op jit(solution)/shard_map/all_to_all | solution.py:405
  (123 shorter events, 29.9 us)
Async XLA Ops:
  7.2 259.2 %copy-start = (bf16[4096,8]{0,1:T(8,128)(2,1)S(1)}, bf16[4096,8]{0,1:T(8,128)(2,1)}, u32[]{:S(2)}) copy-start(bf16[4096,8]{0,1:T(8,128)(2,1)} %param.29) | copy-start | bytes 196612
  7.2 65.9 %all-gather.3.cloned.1.call-start = ((), (), s32[]{:S(2)}) async-start(), calls=%async_computation.3 | async-start | bytes 8650752 | tf_op jit(solution)/shard_map/all_gather | solution.py:315
  7.9 17.7 %collective-permute-start.1 = (bf16[4096,384]{1,0:T(8,128)(2,1)}, bf16[4096,384]{1,0:T(8,128)(2,1)S(1)}, u32[]{:S(2)}, u32[]{:S(2)}) collective-permute-start(bf16[4096,384]{1,0:T(8,128)(2,1)} %bitcast.212), channel_id=1, source_target_pairs={{0,8},{8,0},{16,24},{24,16},{32,40},{40,32},{48,56},{56,48},{64,72... | collective-permute-start | bytes 9437192 | tf_op jit(solution)/shard_map/ppermute | solution.py:34
  8.0 17.6 %collective-permute-start.2 = (bf16[4096,384]{1,0:T(8,128)(2,1)}, bf16[4096,384]{1,0:T(8,128)(2,1)}, u32[]{:S(2)}, u32[]{:S(2)}) collective-permute-start(bf16[4096,384]{1,0:T(8,128)(2,1)} %bitcast.215), channel_id=1, source_target_pairs={{0,8},{8,0},{16,24},{24,16},{32,40},{40,32},{48,56},{56,48},{64,72... | collective-permute-start | bytes 9437192 | tf_op jit(solution)/shard_map/ppermute | solution.py:34
  8.5 17.1 %collective-permute-start.3 = (bf16[384,4096]{1,0:T(8,128)(2,1)}, bf16[384,4096]{1,0:T(8,128)(2,1)}, u32[]{:S(2)}, u32[]{:S(2)}) collective-permute-start(bf16[384,4096]{1,0:T(8,128)(2,1)} %bitcast.219), channel_id=1, source_target_pairs={{0,8},{8,0},{16,24},{24,16},{32,40},{40,32},{48,56},{56,48},{64,72... | collective-permute-start | bytes 9437192 | tf_op jit(solution)/shard_map/ppermute | solution.py:34
  9.3 5.0 %collective-permute-start = (bf16[3,1024]{1,0:T(4,128)(2,1)S(1)}, bf16[3,1024]{1,0:T(4,128)(2,1)S(1)}, u32[]{:S(2)}, u32[]{:S(2)}) collective-permute-start(bf16[3,1024]{1,0:T(4,128)(2,1)S(1)} %slice.120), channel_id=1, source_target_pairs={{0,8},{8,16},{16,24},{24,32},{32,40},{40,48},{48,56},{56,64},{64,7... | collective-permute-start | bytes 18440 | tf_op jit(solution)/shard_map/ppermute | solution.py:202
  25.6 31.8 %copy-start.4 = (bf16[4096,384]{1,0:T(8,128)(2,1)}, bf16[4096,384]{1,0:T(8,128)(2,1)S(1)}, u32[]{:S(2)}) copy-start(bf16[4096,384]{1,0:T(8,128)(2,1)S(1)} %collective-permute-done.1.refs_5_) | copy-start | bytes 9437188
  25.6 1.3 collective-permute-start.4
  27.7 5.7 %collective-permute-start.5 = (f32[136,128]{1,0:T(8,128)}, f32[136,128]{1,0:T(8,128)}, u32[]{:S(2)}, u32[]{:S(2)}) collective-permute-start(f32[136,128]{1,0:T(8,128)} %maximum_bitcast_fusion), channel_id=1, source_target_pairs={{0,16},{8,24},{16,32},{24,40},{32,48},{40,56},{48,0},{56,8},{64,80... | collective-permute-start | bytes 208904 | tf_op jit(solution)/shard_map/ppermute | solution.py:34
  29.0 7.4 %collective-permute-start.6 = (f32[136,128]{1,0:T(8,128)}, f32[136,128]{1,0:T(8,128)}, u32[]{:S(2)}, u32[]{:S(2)}) collective-permute-start(f32[136,128]{1,0:T(8,128)} %maximum_bitcast_fusion), channel_id=1, source_target_pairs={{0,32},{8,40},{16,48},{24,56},{32,0},{40,8},{48,16},{56,24},{64,96... | collective-permute-start | bytes 208904 | tf_op jit(solution)/shard_map/ppermute | solution.py:34
  30.6 7.0 %collective-permute-start.7 = (f32[136,128]{1,0:T(8,128)}, f32[136,128]{1,0:T(8,128)S(1)}, u32[]{:S(2)}, u32[]{:S(2)}) collective-permute-start(f32[136,128]{1,0:T(8,128)} %maximum_bitcast_fusion), channel_id=1, source_target_pairs={{0,48},{8,56},{16,0},{24,8},{32,16},{40,24},{48,32},{56,40},{64,11... | collective-permute-start | bytes 208904 | tf_op jit(solution)/shard_map/ppermute | solution.py:34
  39.9 6.9 %collective-permute-start.8 = (f32[136,128]{1,0:T(8,128)}, f32[136,128]{1,0:T(8,128)S(1)}, u32[]{:S(2)}, u32[]{:S(2)}) collective-permute-start(f32[136,128]{1,0:T(8,128)} %maximum_bitcast_fusion.1), channel_id=1, source_target_pairs={{0,64},{8,72},{16,80},{24,88},{32,96},{40,104},{48,112},{56,120},{... | collective-permute-start | bytes 208904 | tf_op jit(solution)/shard_map/ppermute | solution.py:34
  42.2 6.0 %collective-permute-start.9 = (f32[136,128]{1,0:T(8,128)}, f32[136,128]{1,0:T(8,128)S(1)}, u32[]{:S(2)}, u32[]{:S(2)}) collective-permute-start(f32[136,128]{1,0:T(8,128)} %maximum_bitcast_fusion.1), channel_id=1, source_target_pairs={{0,128},{8,136},{16,144},{24,152},{32,160},{40,168},{48,176},{56,1... | collective-permute-start | bytes 208904 | tf_op jit(solution)/shard_map/ppermute | solution.py:34
  45.0 4.5 %collective-permute-start.10 = (f32[136,128]{1,0:T(8,128)}, f32[136,128]{1,0:T(8,128)S(1)}, u32[]{:S(2)}, u32[]{:S(2)}) collective-permute-start(f32[136,128]{1,0:T(8,128)} %maximum_bitcast_fusion.1), channel_id=1, source_target_pairs={{0,192},{8,200},{16,208},{24,216},{32,224},{40,232},{48,240},{56,2... | collective-permute-start | bytes 208904 | tf_op jit(solution)/shard_map/ppermute | solution.py:34
  50.5 1.0 copy-start.12
  51.5 1.0 copy-start.18
  52.5 1.0 copy-start.20
  73.1 3.4 %copy-start.7 = (bf16[32768,128]{1,0:T(8,128)(2,1)S(1)}, bf16[32768,128]{1,0:T(8,128)(2,1)}, u32[]{:S(2)}) copy-start(bf16[32768,128]{1,0:T(8,128)(2,1)} %all-gather.3.cloned.1.call-done) | copy-start | bytes 25165828
  84.7 7.2 %copy-start.25 = (s32[16,2]{0,1:T(2,128)S(1)}, s32[16,2]{0,1:T(2,128)}, u32[]{:S(2)}) copy-start(s32[16,2]{0,1:T(2,128)} %param.30) | copy-start | bytes 388
  84.7 36.4 %copy-start.23 = (bf16[16,4096]{1,0:T(8,128)(2,1)S(1)}, bf16[16,4096]{1,0:T(8,128)(2,1)}, u32[]{:S(2)}) copy-start(bf16[16,4096]{1,0:T(8,128)(2,1)} %param.27) | copy-start | bytes 393220
  84.7 36.6 %copy-start.24 = (f32[4096]{0:T(1024)S(1)}, f32[4096]{0:T(1024)}, u32[]{:S(2)}) copy-start(f32[4096]{0:T(1024)} %param.28) | copy-start | bytes 49156
  84.7 36.3 %all-to-all-start = ((bf16[8,16,4096]{2,1,0:T(8,128)(2,1)}), bf16[8,16,4096]{2,1,0:T(8,128)(2,1)S(1)}, u32[]{:S(2)}, u32[]{:S(2)}) async-start(bf16[8,16,4096]{2,1,0:T(8,128)(2,1)} %project.1), calls=%async_computation | async-start | bytes 2097152 | tf_op jit(solution)/shard_map/all_to_all | solution.py:332
  143.9 41.4 %copy-start.1 = (bf16[1,4096,384]{2,1,0:T(8,128)(2,1)S(1)}, bf16[1,4096,384]{2,1,0:T(8,128)(2,1)}, u32[]{:S(2)}) copy-start(bf16[1,4096,384]{2,1,0:T(8,128)(2,1)} %param.31) | copy-start | bytes 9437188
  145.9 8.9 %collective-permute-start.12 = (bf16[40,4096]{1,0:T(8,128)(2,1)}, bf16[40,4096]{1,0:T(8,128)(2,1)S(1)}, u32[]{:S(2)}, u32[]{:S(2)}) collective-permute-start(bf16[40,4096]{1,0:T(8,128)(2,1)} %reshape.174), channel_id=1, source_target_pairs={{0,32},{8,136},{16,48},{24,152},{32,0},{40,168},{48,16},{56,184},{... | collective-permute-start | bytes 983048 | tf_op jit(solution)/shard_map/ppermute | solution.py:212
  147.4 10.8 %collective-permute-start.13 = (bf16[40,4096]{1,0:T(8,128)(2,1)}, bf16[40,4096]{1,0:T(8,128)(2,1)S(1)}, u32[]{:S(2)}, u32[]{:S(2)}) collective-permute-start(bf16[40,4096]{1,0:T(8,128)(2,1)} %reshape.174), channel_id=1, source_target_pairs={{0,48},{8,200},{16,0},{24,216},{32,16},{40,232},{48,32},{56,248},{... | collective-permute-start | bytes 983048 | tf_op jit(solution)/shard_map/ppermute | solution.py:212
  147.4 12.0 %collective-permute-start.11 = (bf16[40,4096]{1,0:T(8,128)(2,1)}, bf16[40,4096]{1,0:T(8,128)(2,1)S(1)}, u32[]{:S(2)}, u32[]{:S(2)}) collective-permute-start(bf16[40,4096]{1,0:T(8,128)(2,1)} %reshape.174), channel_id=1, source_target_pairs={{0,16},{8,72},{16,32},{24,88},{32,48},{40,104},{48,0},{56,120},{64... | collective-permute-start | bytes 983048 | tf_op jit(solution)/shard_map/ppermute | solution.py:212
  158.3 10.8 %collective-permute-start.15 = (bf16[80,4096]{1,0:T(8,128)(2,1)S(1)}, bf16[80,4096]{1,0:T(8,128)(2,1)S(1)}, u32[]{:S(2)}, u32[]{:S(2)}) collective-permute-start(bf16[80,4096]{1,0:T(8,128)(2,1)S(1)} %constant_dynamic-update-slice_fusion.2.refs_1_), channel_id=1, source_target_pairs={{0,192},{8,56},{16,208},{24,8},{32,224},{40,24},{48,240},{56,40},{... | collective-permute-start | bytes 1966088 | tf_op jit(solution)/shard_map/ppermute | solution.py:212
  159.4 11.9 %collective-permute-start.14 = (bf16[80,4096]{1,0:T(8,128)(2,1)S(1)}, bf16[80,4096]{1,0:T(8,128)(2,1)S(1)}, u32[]{:S(2)}, u32[]{:S(2)}) collective-permute-start(bf16[80,4096]{1,0:T(8,128)(2,1)S(1)} %constant_dynamic-update-slice_fusion.refs_0_), channel_id=1, source_target_pairs={{0,64},{8,24},{16,80},{24,40},{32,96},{40,56},{48,112},{56,8},{64,... | collective-permute-start | bytes 1966088 | tf_op jit(solution)/shard_map/ppermute | solution.py:212
  160.7 17.6 %collective-permute-start.20 = (bf16[80,4096]{1,0:T(8,128)(2,1)S(1)}, bf16[80,4096]{1,0:T(8,128)(2,1)S(1)}, u32[]{:S(2)}, u32[]{:S(2)}) collective-permute-start(bf16[80,4096]{1,0:T(8,128)(2,1)S(1)} %constant_dynamic-update-slice_fusion.2.refs_1_), channel_id=1, source_target_pairs={{0,64},{8,24},{16,80},{24,40},{32,96},{40,56},{48,112},{56,8},{64,... | collective-permute-start | bytes 1966088 | tf_op jit(solution)/shard_map/ppermute | solution.py:212
  160.8 17.5 %collective-permute-start.19 = (bf16[80,4096]{1,0:T(8,128)(2,1)S(1)}, bf16[80,4096]{1,0:T(8,128)(2,1)S(1)}, u32[]{:S(2)}, u32[]{:S(2)}) collective-permute-start(bf16[80,4096]{1,0:T(8,128)(2,1)S(1)} %constant_dynamic-update-slice_fusion.refs_0_), channel_id=1, source_target_pairs={{0,192},{8,56},{16,208},{24,8},{32,224},{40,24},{48,240},{56,40},{... | collective-permute-start | bytes 1966088 | tf_op jit(solution)/shard_map/ppermute | solution.py:212
  169.1 14.0 %collective-permute-start.18 = (bf16[80,4096]{1,0:T(8,128)(2,1)S(1)}, bf16[80,4096]{1,0:T(8,128)(2,1)S(1)}, u32[]{:S(2)}, u32[]{:S(2)}) collective-permute-start(bf16[80,4096]{1,0:T(8,128)(2,1)S(1)} %collective-permute-done.15.refs_3_), channel_id=1, source_target_pairs={{0,192},{8,56},{16,208},{24,8},{32,224},{40,24},{48,240},{56,40},{... | collective-permute-start | bytes 1966088 | tf_op jit(solution)/shard_map/ppermute | solution.py:212
  171.3 14.0 %collective-permute-start.17 = (bf16[80,4096]{1,0:T(8,128)(2,1)S(1)}, bf16[80,4096]{1,0:T(8,128)(2,1)S(1)}, u32[]{:S(2)}, u32[]{:S(2)}) collective-permute-start(bf16[80,4096]{1,0:T(8,128)(2,1)S(1)} %collective-permute-done.14.refs_2_), channel_id=1, source_target_pairs={{0,64},{8,24},{16,80},{24,40},{32,96},{40,56},{48,112},{56,8},{64,... | collective-permute-start | bytes 1966088 | tf_op jit(solution)/shard_map/ppermute | solution.py:212
  185.3 1.9 copy-start.2
  187.2 1.9 copy-start.5
  189.1 7.5 %copy-start.10 = (bf16[1,384,4096]{2,1,0:T(8,128)(2,1)S(1)}, bf16[1,384,4096]{2,1,0:T(8,128)(2,1)}, u32[]{:S(2)}) copy-start(bf16[1,384,4096]{2,1,0:T(8,128)(2,1)} %param.33) | copy-start | bytes 9437188
  196.6 7.1 %copy-start.3 = (bf16[1,4096,384]{2,1,0:T(8,128)(2,1)S(1)}, bf16[1,4096,384]{2,1,0:T(8,128)(2,1)}, u32[]{:S(2)}) copy-start(bf16[1,4096,384]{2,1,0:T(8,128)(2,1)} %param.32) | copy-start | bytes 9437188
  196.6 7.1 %copy-start.6 = (bf16[4096,384]{1,0:T(8,128)(2,1)S(1)}, bf16[4096,384]{1,0:T(8,128)(2,1)}, u32[]{:S(2)}) copy-start(bf16[4096,384]{1,0:T(8,128)(2,1)} %copy-done.4) | copy-start | bytes 9437188
  203.6 17.9 %collective-permute-start.25 = (bf16[80,4096]{1,0:T(8,128)(2,1)S(1)}, bf16[80,4096]{1,0:T(8,128)(2,1)S(1)}, u32[]{:S(2)}, u32[]{:S(2)}) collective-permute-start(bf16[80,4096]{1,0:T(8,128)(2,1)S(1)} %get-tuple-element.41), channel_id=1, source_target_pairs={{0,192},{8,56},{16,208},{24,8},{32,224},{40,24},{48,240},{56,40},{... | collective-permute-start | bytes 1966088 | tf_op jit(solution)/shard_map/ppermute | solution.py:212
  217.4 19.9 %collective-permute-start.24 = (bf16[80,4096]{1,0:T(8,128)(2,1)S(1)}, bf16[80,4096]{1,0:T(8,128)(2,1)S(1)}, u32[]{:S(2)}, u32[]{:S(2)}) collective-permute-start(bf16[80,4096]{1,0:T(8,128)(2,1)S(1)} %get-tuple-element.39), channel_id=1, source_target_pairs={{0,64},{8,24},{16,80},{24,40},{32,96},{40,56},{48,112},{56,8},{64,... | collective-permute-start | bytes 1966088 | tf_op jit(solution)/shard_map/ppermute | solution.py:212
  219.4 21.4 %collective-permute-start.16 = (bf16[80,4096]{1,0:T(8,128)(2,1)S(1)}, bf16[80,4096]{1,0:T(8,128)(2,1)S(1)}, u32[]{:S(2)}, u32[]{:S(2)}) collective-permute-start(bf16[80,4096]{1,0:T(8,128)(2,1)S(1)} %get-tuple-element.33), channel_id=1, source_target_pairs={{0,192},{8,56},{16,208},{24,8},{32,224},{40,24},{48,240},{56,40},{... | collective-permute-start | bytes 1966088 | tf_op jit(solution)/shard_map/ppermute | solution.py:212
  220.7 15.6 %collective-permute-start.21 = (bf16[80,4096]{1,0:T(8,128)(2,1)S(1)}, bf16[80,4096]{1,0:T(8,128)(2,1)S(1)}, u32[]{:S(2)}, u32[]{:S(2)}) collective-permute-start(bf16[80,4096]{1,0:T(8,128)(2,1)S(1)} %get-tuple-element.37), channel_id=1, source_target_pairs={{0,64},{8,24},{16,80},{24,40},{32,96},{40,56},{48,112},{56,8},{64,... | collective-permute-start | bytes 1966088 | tf_op jit(solution)/shard_map/ppermute | solution.py:212
  221.6 15.7 %collective-permute-start.26 = (bf16[80,4096]{1,0:T(8,128)(2,1)S(1)}, bf16[80,4096]{1,0:T(8,128)(2,1)S(1)}, u32[]{:S(2)}, u32[]{:S(2)}) collective-permute-start(bf16[80,4096]{1,0:T(8,128)(2,1)S(1)} %add_convert_fusion.1), channel_id=1, source_target_pairs={{0,192},{8,56},{16,208},{24,8},{32,224},{40,24},{48,240},{56,40},{... | collective-permute-start | bytes 1966088 | tf_op jit(solution)/shard_map/ppermute | solution.py:212
  236.4 16.6 %collective-permute-start.22 = (bf16[80,4096]{1,0:T(8,128)(2,1)S(1)}, bf16[80,4096]{1,0:T(8,128)(2,1)S(1)}, u32[]{:S(2)}, u32[]{:S(2)}) collective-permute-start(bf16[80,4096]{1,0:T(8,128)(2,1)S(1)} %add_convert_fusion.2), channel_id=1, source_target_pairs={{0,64},{8,24},{16,80},{24,40},{32,96},{40,56},{48,112},{56,8},{64,... | collective-permute-start | bytes 1966088 | tf_op jit(solution)/shard_map/ppermute | solution.py:212
  237.6 15.8 %collective-permute-start.27 = (bf16[40,4096]{1,0:T(8,128)(2,1)S(1)}, bf16[40,4096]{1,0:T(8,128)(2,1)S(1)}, u32[]{:S(2)}, u32[]{:S(2)}) collective-permute-start(bf16[40,4096]{1,0:T(8,128)(2,1)S(1)} %get-tuple-element.57), channel_id=1, source_target_pairs={{0,32},{8,136},{16,48},{24,152},{32,0},{40,168},{48,16},{56,184},{... | collective-permute-start | bytes 983048 | tf_op jit(solution)/shard_map/ppermute | solution.py:212
  239.8 13.6 %collective-permute-start.28 = (bf16[40,4096]{1,0:T(8,128)(2,1)S(1)}, bf16[40,4096]{1,0:T(8,128)(2,1)S(1)}, u32[]{:S(2)}, u32[]{:S(2)}) collective-permute-start(bf16[40,4096]{1,0:T(8,128)(2,1)S(1)} %get-tuple-element.58), channel_id=1, source_target_pairs={{0,16},{8,72},{16,32},{24,88},{32,48},{40,104},{48,0},{56,120},{64... | collective-permute-start | bytes 983048 | tf_op jit(solution)/shard_map/ppermute | solution.py:212
  253.3 8.4 %collective-permute-start.23 = (bf16[40,4096]{1,0:T(8,128)(2,1)S(1)}, bf16[40,4096]{1,0:T(8,128)(2,1)S(1)}, u32[]{:S(2)}, u32[]{:S(2)}) collective-permute-start(bf16[40,4096]{1,0:T(8,128)(2,1)S(1)} %slice.265), channel_id=1, source_target_pairs={{0,48},{8,200},{16,0},{24,216},{32,16},{40,232},{48,32},{56,248},{... | collective-permute-start | bytes 983048 | tf_op jit(solution)/shard_map/ppermute | solution.py:212
  261.8 4.6 %copy-start.22 = (bf16[16,4096]{1,0:T(8,128)(2,1)S(1)}, bf16[16,4096]{1,0:T(8,128)(2,1)}, u32[]{:S(2)}) copy-start(bf16[16,4096]{1,0:T(8,128)(2,1)} %copy-done.21) | copy-start | bytes 393220
  262.8 16.7 %all-to-all-start.2 = ((bf16[8,5,4096]{2,1,0:T(8,128)(2,1)}), bf16[8,5,4096]{2,1,0:T(8,128)(2,1)S(1)}, u32[]{:S(2)}, u32[]{:S(2)}) async-start(bf16[8,5,4096]{2,1,0:T(8,128)(2,1)} %reshape.175), calls=%async_computation.2 | async-start | bytes 1048576 | tf_op jit(solution)/shard_map/all_to_all | solution.py:405
  (10 other events, 8.0 us)
Sparse Core Ops, SparseCore 0:
  10.6 62.5 all-gather.2

commit v4 on v3

--- a/solution.py
+++ b/solution.py
@@ -16,6 +16,7 @@
 LOG2E = math.log2(math.e)
 VMEM = pl.BlockSpec(memory_space=pltpu.VMEM)
 SMEM = pl.BlockSpec(memory_space=pltpu.SMEM)
+HBM = pl.BlockSpec(memory_space=pltpu.MemorySpace.HBM)
 
 
 def split_place(place):
@@ -35,10 +36,20 @@
 
 
 def local_scan_kernel(
-    inp_ref, before_ref, raw_ref, rate_ref, taps_ref, bias_ref, skip_ref, in_ref, out_ref,
+    inp_hbm, raw_hbm, rate_hbm, taps_hbm, bias_hbm, skip_hbm, before_ref, in_ref, out_ref,
     y_ref, sums_ref, carry_ref, scaled_ref,
-    pad_ref, delta_ref, conv_ref,
+    inp_ref, raw_ref, rate_ref, taps_ref, bias_ref, skip_ref, pad_ref, delta_ref, conv_ref, sems,
 ):
+    sources = (inp_hbm, raw_hbm, rate_hbm, taps_hbm, bias_hbm, skip_hbm)
+    places = (inp_ref, raw_ref, rate_ref, taps_ref, bias_ref, skip_ref)
+    copies = [
+        pltpu.make_async_copy(source, place, sems.at[k])
+        for k, (source, place) in enumerate(zip(sources, places))
+    ]
+    for copy in copies:
+        copy.start()
+    for copy in copies:
+        copy.wait()
     length, width = inp_ref.shape
     states = rate_ref.shape[0]
     tiles = width // LANES
@@ -83,7 +94,11 @@
     carry_ref[states * SUB :, :] = total
 
 
-def finish_scan_kernel(y_ref, sums_ref, start_ref, scaled_ref, gate_ref, out_ref, mixed_ref, full_ref):
+def finish_scan_kernel(
+    y_ref, sums_ref, start_ref, scaled_ref, gate_hbm, out_ref, mixed_ref, full_ref, gate_ref, sem
+):
+    copy = pltpu.make_async_copy(gate_hbm, gate_ref, sem)
+    copy.start()
     length, width = gate_ref.shape
     states = start_ref.shape[0] // SUB
     tiles = width // LANES
@@ -99,6 +114,7 @@
         return carry
 
     lax.fori_loop(0, length, step, 0, unroll=2)
+    copy.wait()
     for j in range(tiles):
         cols = slice(j * LANES, (j + 1) * LANES)
         gate = gate_ref[:, cols].astype(jnp.float32)
@@ -110,6 +126,7 @@
     length, width = inp.shape
     states = rate.shape[0]
     flat = jax.ShapeDtypeStruct((length * SUB, LANES), jnp.float32)
+    arrays = (inp, raw, rate, taps, bias, skip)
     return pl.pallas_call(
         local_scan_kernel,
         name="local_scan",
@@ -119,16 +136,18 @@
             jax.ShapeDtypeStruct(((states + 1) * SUB, LANES), jnp.float32),
             jax.ShapeDtypeStruct((states * SUB, LANES), jnp.float32),
         ),
-        in_specs=[VMEM] * 7 + [SMEM] * 2,
+        in_specs=[HBM] * 6 + [VMEM] + [SMEM] * 2,
         out_specs=(VMEM,) * 4,
-        scratch_shapes=[
+        scratch_shapes=[pltpu.VMEM(a.shape, a.dtype) for a in arrays]
+        + [
             pltpu.VMEM((length + SUB, LANES), jnp.float32),
             pltpu.VMEM((length * SUB, LANES), jnp.float32),
             pltpu.VMEM((length * SUB, LANES), jnp.float32),
+            pltpu.SemaphoreType.DMA((6,)),
         ],
-        compiler_params=pltpu.CompilerParams(vmem_limit_bytes=24 << 20),
+        compiler_params=pltpu.CompilerParams(vmem_limit_bytes=58 << 20),
         cost_estimate=pl.CostEstimate(flops=8_000_000, transcendentals=2_500_000, bytes_accessed=2_000_000),
-    )(inp, before, raw, rate, taps, bias, skip, in_flat, out_flat)
+    )(*arrays, before, in_flat, out_flat)
 
 
 def finish_scan(y, sums, start, scaled, gate, out_flat):
@@ -137,10 +156,14 @@
         finish_scan_kernel,
         name="finish_scan",
         out_shape=jax.ShapeDtypeStruct((length, width), jnp.bfloat16),
-        in_specs=[VMEM] * 5 + [SMEM],
+        in_specs=[VMEM] * 4 + [HBM] + [SMEM],
         out_specs=VMEM,
-        scratch_shapes=[pltpu.VMEM((length * SUB, LANES), jnp.float32)],
-        compiler_params=pltpu.CompilerParams(vmem_limit_bytes=24 << 20),
+        scratch_shapes=[
+            pltpu.VMEM((length * SUB, LANES), jnp.float32),
+            pltpu.VMEM((length, width), jnp.bfloat16),
+            pltpu.SemaphoreType.DMA,
+        ],
+        compiler_params=pltpu.CompilerParams(vmem_limit_bytes=16 << 20),
         cost_estimate=pl.CostEstimate(flops=8_000_000, transcendentals=2_500_000, bytes_accessed=2_000_000),
     )(y, sums, start, scaled, gate, out_flat)
 
@@ -216,65 +239,62 @@
     return sum(t.astype(jnp.float32) for t in terms)
 
 
-def expert_in_kernel(*refs):
-    pieces, (gate_a, gate_b, up_a, up_b, act_a, act_b, rows_ref) = refs[:-7], refs[-7:]
+def expert_kernel(steps, *refs):
+    count = (len(refs) - 8) // 2
+    pieces, outs = refs[:count], refs[count + 6 : -2]
+    gate_a, gate_b, up_a, up_b, down_a, down_b = refs[count : count + 6]
+    rows_ref, acts_ref = refs[-2:]
     rows = pieces[0].shape[0]
-
-    @pl.when(pl.program_id(0) == 0)
+    half = acts_ref.shape[1] // 2
+    i = pl.program_id(0)
+
+    @pl.when(i == 0)
     def _():
         for k, piece in enumerate(pieces):
             rows_ref[k * rows : (k + 1) * rows, :] = piece[...]
 
-    for gate, up, act in ((gate_a, up_a, act_a), (gate_b, up_b, act_b)):
-        both = jnp.concatenate([gate[...], up[...]], axis=1)
-        hidden = jnp.dot(rows_ref[...], both, preferred_element_type=jnp.float32)
-        gating, upward = hidden[:, :LANES], hidden[:, LANES:]
-        act[...] = (gating * jax.nn.sigmoid(gating) * upward).astype(act.dtype)
-
-
-def expert_out_kernel(act_a, act_b, down_a, down_b, *outs):
-    rows = outs[0].shape[0]
-    acts = jnp.concatenate([act_a[...], act_b[...]], axis=1)
-    down = jnp.concatenate([down_a[...], down_b[...]], axis=0)
-    result = jnp.dot(acts, down, preferred_element_type=jnp.float32).astype(outs[0].dtype)
-    for k, out in enumerate(outs):
-        out[...] = result[k * rows : (k + 1) * rows]
+    @pl.when(i < steps)
+    def _():
+        for begin, gate, up in ((0, gate_a, up_a), (half, gate_b, up_b)):
+            both = jnp.concatenate([gate[...], up[...]], axis=1)
+            hidden = jnp.dot(rows_ref[...], both, preferred_element_type=jnp.float32)
+            gating, upward = hidden[:, :LANES], hidden[:, LANES:]
+            act = (gating * jax.nn.sigmoid(gating) * upward).astype(acts_ref.dtype)
+            acts_ref[:, pl.ds(pl.multiple_of(begin + i * LANES, LANES), LANES)] = act
+
+    @pl.when(i >= steps)
+    def _():
+        down = jnp.concatenate([down_a[...], down_b[...]], axis=0)
+        result = jnp.dot(acts_ref[...], down, preferred_element_type=jnp.float32)
+        for k, out in enumerate(outs):
+            out[...] = result[k * rows : (k + 1) * rows].astype(out.dtype)
 
 
 def expert(pieces, here, there):
     rows, width = pieces[0].shape
     count = len(pieces) * rows
     hidden = here[0].shape[1]
-    weight = pl.BlockSpec((width, LANES), lambda i: (0, i))
-    act = pl.BlockSpec((count, LANES), lambda i: (0, i))
-    acts = pl.pallas_call(
-        expert_in_kernel,
-        name="expert_in",
-        grid=(hidden // LANES,),
-        out_shape=(jax.ShapeDtypeStruct((count, hidden), jnp.bfloat16),) * 2,
-        in_specs=[VMEM] * len(pieces) + [weight] * 4,
-        out_specs=(act, act),
-        scratch_shapes=[pltpu.VMEM((count, width), jnp.bfloat16)],
-        compiler_params=pltpu.CompilerParams(vmem_limit_bytes=32 << 20),
+    steps = hidden // LANES
+    tile = 4 * LANES
+    into = pl.BlockSpec((width, LANES), lambda i: (0, jnp.minimum(i, steps - 1)))
+    back = pl.BlockSpec((hidden, tile), lambda i: (0, jnp.maximum(i - steps, 0)))
+    piece = pl.BlockSpec((rows, tile), lambda i: (0, jnp.maximum(i - steps, 0)))
+    return pl.pallas_call(
+        functools.partial(expert_kernel, steps),
+        name="expert",
+        grid=(steps + width // tile,),
+        out_shape=(jax.ShapeDtypeStruct((rows, width), jnp.bfloat16),) * len(pieces),
+        in_specs=[VMEM] * len(pieces) + [into] * 4 + [back] * 2,
+        out_specs=(piece,) * len(pieces),
+        scratch_shapes=[
+            pltpu.VMEM((count, width), jnp.bfloat16),
+            pltpu.VMEM((count, 2 * hidden), jnp.bfloat16),
+        ],
+        compiler_params=pltpu.CompilerParams(vmem_limit_bytes=42 << 20),
         cost_estimate=pl.CostEstimate(
-            flops=8 * count * width * hidden, transcendentals=2 * count * hidden, bytes_accessed=20_000_000
+            flops=12 * count * width * hidden, transcendentals=2 * count * hidden, bytes_accessed=24_000_000
         ),
-    )(*pieces, here[0], there[0], here[1], there[1])
-    tile = 4 * LANES
-    weight = pl.BlockSpec((hidden, tile), lambda i: (0, i))
-    piece = pl.BlockSpec((rows, tile), lambda i: (0, i))
-    return pl.pallas_call(
-        expert_out_kernel,
-        name="expert_out",
-        grid=(width // tile,),
-        out_shape=(jax.ShapeDtypeStruct((rows, width), jnp.bfloat16),) * len(pieces),
-        in_specs=[VMEM] * 2 + [weight] * 2,
-        out_specs=(piece,) * len(pieces),
-        compiler_params=pltpu.CompilerParams(vmem_limit_bytes=32 << 20),
-        cost_estimate=pl.CostEstimate(
-            flops=4 * count * width * hidden, transcendentals=0, bytes_accessed=10_000_000
-        ),
-    )(*acts, here[2], there[2])
+    )(*pieces, here[0], there[0], here[1], there[1], here[2], there[2])
 
 
 def experts_of_rows(block, here, there):
@@ -287,10 +307,11 @@
     low_down = around(low, "outer", -1)
     low_far = around(low_up, "outer", 1)
     high_far = around(high_down, "outer", -1)
-    low, high, low_up, high_down = expert([low, high, low_up, high_down], here, there)
+    low_far, high_far, low, high, low_up, high_down, low_down, high_up = expert(
+        [low_far, high_far, low, high, low_up, high_down, low_down, high_up], here, there
+    )
     got_high_down = around(high_down, "outer", 1)
     got_low_up = around(low_up, "outer", -1)
-    low_far, high_far, low_down, high_up = expert([low_far, high_far, low_down, high_up], here, there)
     low_relay = around(low_far, "outer", 1)
     high_relay = around(high_far, "outer", -1)
     got_low_down = around(added(low_down, low_relay).astype(dtype), "outer", 1)
@@ -311,26 +332,37 @@
         out_ref[owner] = result[owner * rows : (owner + 1) * rows]
 
 
-def project(mixed, weight):
-    blocks = lax.all_gather(weight, "seq")
+def project_part(mixed, blocks, begin, end):
     owners = lax.axis_size("exp")
     tokens, depth = mixed.shape
-    count = blocks.shape[0]
     rows = tokens // owners
-    terms = pl.pallas_call(
+    count = end - begin
+    return pl.pallas_call(
         project_kernel,
         name="project",
         grid=(count // 2,),
         out_shape=jax.ShapeDtypeStruct((owners, rows, count * LANES), jnp.bfloat16),
-        in_specs=[VMEM, pl.BlockSpec((2, depth, LANES), lambda i: (i, 0, 0))],
+        in_specs=[VMEM, pl.BlockSpec((2, depth, LANES), lambda i: (i + begin // 2, 0, 0))],
         out_specs=pl.BlockSpec((owners, rows, 2 * LANES), lambda i: (0, 0, i)),
-        compiler_params=pltpu.CompilerParams(vmem_limit_bytes=24 << 20),
+        compiler_params=pltpu.CompilerParams(vmem_limit_bytes=56 << 20),
         cost_estimate=pl.CostEstimate(
-            flops=2 * tokens * depth * count * LANES, transcendentals=0, bytes_accessed=10_000_000
+            flops=2 * tokens * depth * count * LANES,
+            transcendentals=0,
+            bytes_accessed=2 * depth * count * LANES + 4 * tokens * depth,
         ),
     )(mixed, blocks)
-    terms = lax.all_to_all(terms, "exp", 0, 0, tiled=True)
-    return added(*(terms[k] for k in range(owners)))
+
+
+def project(mixed, weight):
+    blocks = lax.all_gather(weight, "seq")
+    count = blocks.shape[0]
+    begin = count * 7 // 16 // 2 * 2
+    first = project_part(mixed, blocks, 0, begin)
+    first = lax.psum_scatter(first, "exp", scatter_dimension=0, tiled=False)
+    second = project_part(mixed, blocks, begin, count)
+    second = lax.all_to_all(second, "exp", 0, 0, tiled=True)
+    second = added(*(second[k] for k in range(second.shape[0])))
+    return jnp.concatenate([first.astype(jnp.float32), second], axis=1)
 
 
 def shards(

time: 289 us -> 280 us (0.969)
  local copies, waits for them, and re-layouts: 25.7 us -> 6.32 us
  starting transfers between devices: 47.5 us -> 58.3 us
    all_to_all x1, waiting for transfers between devices: 28.8 us -> 0.01 us  [project(): second = lax.all_to_all(second, 'exp', 0, 0, tiled=True)]
    reduce_scatter x0 -> x1, waiting for transfers between devices: none -> 24.5 us  [project(): first = lax.psum_scatter(first, 'exp', scatter_dimension=0, tiled=False)]
    unnamed x55 -> x23, local copies, waits for them, and re-layouts: 19.4 us -> 0.77 us
    ppermute x18, starting transfers between devices: 23.4 us -> 34.3 us  [around(): return lax.ppermute(block, 'seq', route)]
    all_gather x1, waiting for transfers between devices: 15.7 us -> 23.6 us  [project(): blocks = lax.all_gather(weight, 'seq')]
    ppermute x18, waiting for transfers between devices: 58.2 us -> 54.8 us  [around(): return lax.ppermute(block, 'seq', route)]
    pallas_call x5 -> x3, Pallas kernels: 35.4 us -> 32.7 us  [the longest x1 19.3 us: expert(): pl.pallas_call(functools.partial(expert_kernel, steps), name='expert', gr...]
  transfers between devices with their start and end apart: 32 -> 33, of which waited for: 21 -> 23; matrix products, arithmetic and copies ran while one was open for 3% -> 3% of each run, Pallas kernels for 8% -> 7%
where the time goes in v4:
time: 280 us; the launch traced here: 276 us
  waiting for transfers between devices  127 us (45%)
  starting transfers between devices  58.3 us (21%)
  Pallas kernels  43.8 us (16%)
  blocking collectives  19.8 us (7%)
  between operations  14.5 us (5%)
  local copies, waits for them, and re-layouts  6.32 us (2%)
  other arithmetic  5.9 us (2%)
    ppermute x18, waiting for transfers between devices, around(): return lax.ppermute(block, 'seq', route)  54.8 us
    ppermute x18, starting transfers between devices, around(): return lax.ppermute(block, 'seq', route)  34.3 us
    reduce_scatter x1, waiting for transfers between devices, project(): first = lax.psum_scatter(first, 'exp', scatter_dimension=0, tiled=False)  24.5 us
    all_gather x1, waiting for transfers between devices, project(): blocks = lax.all_gather(weight, 'seq')  23.6 us
    all_to_all x1, blocking collectives, shards(): lax.all_to_all(outgoing, 'exp', split_axis=0, concat_axis=0, tiled=True)  19.8 us
    pallas_call x1, Pallas kernels, expert(): pl.pallas_call(functools.partial(expert_kernel, steps), name='expert', gr...  19.3 us
    pallas_call x2, Pallas kernels, project_part(): pl.pallas_call(project_kernel, name='project', grid=(count // 2,), out_sh...  13.4 us
    all_to_all x1, waiting for transfers between devices, shards(): lax.all_to_all(summed_out.reshape(arrived.shape), 'exp', split_axis=0, co...  12.9 us
  transfers between devices with their start and end apart: 33, of which 23 were waited for; matrix products, arithmetic and copies ran while one was open for 3% of the time, Pallas kernels for 7%

profile of v4, /device:TPU:6, one launch (start us, length us, event | category | flops | bytes accessed | tf_op | source)
XLA Modules:
  0.0 276.2 jit_solution(1829589887113734350)
XLA Ops:
  9.4 2.3 collective-permute-start
  15.2 7.2 %local_scan.1 = (f32[1024,128]{1,0:T(8,128)}, f32[1024,128]{1,0:T(8,128)}, f32[136,128]{1,0:T(8,128)}, f32[128,128]{1,0:T(8,128)}) custom-call(bf16[128,1024]{1,0:T(8,128)(2,1)} %inp_hbm.1, bf16[128,1024]{1,0:T(8,128)(2,1)} %raw_hbm.1, f32[16,1024]{1,0:T(8,128)} %rate_hbm.1, f32[4,1024]{1,0:T(4,128)} %taps_hbm.1, f32[1,1024]{1,0:T(1,128)} %bitcast.224, ...), custom_call_target="tpu_custom_call" | custom-call | flops 8000000 | bytes 2000000 | tf_op jit(solution)/shard_map/local_scan/pallas_call | solution.py:130
  23.8 1.1 collective-permute-done.4
  25.7 0.9 bitcast_add_fusion
  27.2 2.7 collective-permute-start.6
  30.7 4.2 %collective-permute-done.7 = f32[136,128]{1,0:T(8,128)S(1)} collective-permute-done((f32[136,128]{1,0:T(8,128)S(1)}, f32[136,128]{1,0:T(8,128)S(1)}, u32[]{:S(2)}, u32[]{:S(2)}) %collective-permute-start.7) | collective-permute-done | bytes 69664 | tf_op jit(solution)/shard_map/ppermute | solution.py:35
  35.1 0.9 collective-permute-done.5
  36.0 1.0 fusion.20
  37.0 1.8 collective-permute-start.8
  38.8 1.5 collective-permute-start.10
  40.3 2.1 collective-permute-start.9
  42.6 3.5 %collective-permute-done.9 = f32[136,128]{1,0:T(8,128)S(1)} collective-permute-done((f32[136,128]{1,0:T(8,128)S(1)}, f32[136,128]{1,0:T(8,128)S(1)}, u32[]{:S(2)}, u32[]{:S(2)}) %collective-permute-start.9) | collective-permute-done | bytes 69664 | tf_op jit(solution)/shard_map/ppermute | solution.py:35
  46.3 3.9 %finish_scan.1.mixed_ref = bf16[128,1024]{1,0:T(8,128)(2,1)} custom-call(f32[1024,128]{1,0:T(8,128)S(1)} %copy-done.4, f32[1024,128]{1,0:T(8,128)S(1)} %copy-done.5, f32[128,128]{1,0:T(8,128)S(1)} %fusion.9.start_ref, f32[128,128]{1,0:T(8,128)S(1)} %copy-done.1, bf16[128,1024]{1,0:T(8,128)(2,1)S(1)} %copy-done.3, f32[2048]{0:T(1024)S(1)} %copy-done.2), custom_call_target="tpu_custom_call" | custom-call | flops 8000000 | bytes 2000000 | tf_op jit(solution)/shard_map/finish_scan/pallas_call | solution.py:155
  50.2 23.6 %all-gather.3.cloned.1.call-done = bf16[32768,128]{1,0:T(8,128)(2,1)} async-done(((bf16[1024,128]{1,0:T(8,128)(2,1)}), bf16[32768,128]{1,0:T(8,128)(2,1)}) %all-gather.3.cloned.1.call-update) | async-done | bytes 8388624 | tf_op jit(solution)/shard_map/all_gather | solution.py:357
  73.7 6.0 %project.2 = bf16[8,16,1792]{2,1,0:T(8,128)(2,1)} custom-call(bf16[128,1024]{1,0:T(8,128)(2,1)} %finish_scan.1.mixed_ref, bf16[32,1024,128]{2,1,0:T(8,128)(2,1)} %bitcast.214), custom_call_target="tpu_custom_call" | custom-call | flops 469762048 | bytes 4194304 | tf_op jit(solution)/shard_map/project/pallas_call | solution.py:340
  79.8 7.4 %project.3 = bf16[8,16,2304]{2,1,0:T(8,128)(2,1)} custom-call(bf16[128,1024]{1,0:T(8,128)(2,1)} %finish_scan.1.mixed_ref, bf16[32,1024,128]{2,1,0:T(8,128)(2,1)} %bitcast.215), custom_call_target="tpu_custom_call" | custom-call | flops 603979776 | bytes 5242880 | tf_op jit(solution)/shard_map/project/pallas_call | solution.py:340
  87.2 7.1 %all-to-all-start = ((bf16[8,16,2304]{2,1,0:T(8,128)(2,1)}), bf16[8,16,2304]{2,1,0:T(8,128)(2,1)S(1)}, u32[]{:S(2)}, u32[]{:S(2)}) async-start(bf16[8,16,2304]{2,1,0:T(8,128)(2,1)} %project.3), calls=%async_computation.1 | async-start | bytes 1179648 | tf_op jit(solution)/shard_map/all_to_all | solution.py:363
  94.7 24.5 %reduce-scatter.2.cloned.1.call-done = bf16[1,16,1792]{2,1,0:T(8,128)(2,1)} async-done(((bf16[8,16,1792]{2,1,0:T(8,128)(2,1)}), bf16[1,16,1792]{2,1,0:T(8,128)(2,1)}) %reduce-scatter.2.cloned.1.call-update) | async-done | bytes 57360 | tf_op jit(solution)/shard_map/reduce_scatter | solution.py:361
  121.1 19.8 %all_to_all.15 = bf16[8,5,4096]{2,1,0:T(8,128)(2,1)S(1)} all-to-all(bf16[8,5,4096]{2,1,0:T(8,128)(2,1)S(1)} %reshape.175), channel_id=1, replica_groups=mesh['seq'=32,'exp'=8] {'exp'}, dimensions={0} | all-to-all | bytes 655360 | tf_op jit(solution)/shard_map/all_to_all | solution.py:434
  141.8 1.6 collective-permute-start.14
  143.5 1.7 collective-permute-start.11
  145.2 9.9 %collective-permute-done.11 = bf16[40,4096]{1,0:T(8,128)(2,1)S(1)} collective-permute-done((bf16[40,4096]{1,0:T(8,128)(2,1)S(1)}, bf16[40,4096]{1,0:T(8,128)(2,1)S(1)}, u32[]{:S(2)}, u32[]{:S(2)}) %collective-permute-start.11) | collective-permute-done | bytes 327712 | tf_op jit(solution)/shard_map/ppermute | solution.py:235
  155.1 5.4 %collective-permute-start.12 = (bf16[80,4096]{1,0:T(8,128)(2,1)S(1)}, bf16[80,4096]{1,0:T(8,128)(2,1)S(1)}, u32[]{:S(2)}, u32[]{:S(2)}) collective-permute-start(bf16[80,4096]{1,0:T(8,128)(2,1)S(1)} %constant_dynamic-update-slice_fusion.refs_2_), channel_id=1, source_target_pairs={{0,64},{8,24},{16,80},{24,40},{32,96},{40,56},{48,112},{56,8},{64,... | collective-permute-start | bytes 1966088 | tf_op jit(solution)/shard_map/ppermute | solution.py:235
  160.5 1.1 collective-permute-start.16
  161.6 2.0 collective-permute-start.18
  163.7 6.4 %collective-permute-done.12.refs_4_ = bf16[80,4096]{1,0:T(8,128)(2,1)S(1)} collective-permute-done((bf16[80,4096]{1,0:T(8,128)(2,1)S(1)}, bf16[80,4096]{1,0:T(8,128)(2,1)S(1)}, u32[]{:S(2)}, u32[]{:S(2)}) %collective-permute-start.12) | collective-permute-done | bytes 655392 | tf_op jit(solution)/shard_map/ppermute | solution.py:235
  170.0 1.0 collective-permute-start.13
  171.2 2.2 collective-permute-start.17
  173.4 4.8 %collective-permute-done.18.refs_6_ = bf16[80,4096]{1,0:T(8,128)(2,1)S(1)} collective-permute-done((bf16[80,4096]{1,0:T(8,128)(2,1)S(1)}, bf16[80,4096]{1,0:T(8,128)(2,1)S(1)}, u32[]{:S(2)}, u32[]{:S(2)}) %collective-permute-start.18) | collective-permute-done | bytes 655392 | tf_op jit(solution)/shard_map/ppermute | solution.py:235
  178.2 5.8 %collective-permute-done.13.refs_0_ = bf16[80,4096]{1,0:T(8,128)(2,1)S(1)} collective-permute-done((bf16[80,4096]{1,0:T(8,128)(2,1)S(1)}, bf16[80,4096]{1,0:T(8,128)(2,1)S(1)}, u32[]{:S(2)}, u32[]{:S(2)}) %collective-permute-start.13) | collective-permute-done | bytes 655392 | tf_op jit(solution)/shard_map/ppermute | solution.py:235
  184.1 1.2 collective-permute-done.17.refs_1_
  185.2 19.3 %expert.1 = (bf16[80,4096]{1,0:T(8,128)(2,1)S(1)}, bf16[80,4096]{1,0:T(8,128)(2,1)S(1)}, bf16[80,4096]{1,0:T(8,128)(2,1)S(1)}, bf16[80,4096]{1,0:T(8,128)(2,1)S(...) custom-call(bf16[80,4096]{1,0:T(8,128)(2,1)S(1)} %collective-permute, ...), custom_call_target="tpu_custom_call" | custom-call | flops 12079595520 | bytes 24000000 | tf_op jit(solution)/shard_map/expert/pallas_call | solution.py:282
  205.0 2.8 %collective-permute-start.20 = (bf16[80,4096]{1,0:T(8,128)(2,1)S(1)}, bf16[80,4096]{1,0:T(8,128)(2,1)S(1)}, u32[]{:S(2)}, u32[]{:S(2)}) collective-permute-start(bf16[80,4096]{1,0:T(8,128)(2,1)S(1)} %get-tuple-element.27), channel_id=1, source_target_pairs={{0,192},{8,56},{16,208},{24,8},{32,224},{40,24},{48,240},{56,40},{... | collective-permute-start | bytes 1966088 | tf_op jit(solution)/shard_map/ppermute | solution.py:235
  207.9 3.2 %collective-permute-start.25 = (bf16[80,4096]{1,0:T(8,128)(2,1)S(1)}, bf16[80,4096]{1,0:T(8,128)(2,1)S(1)}, u32[]{:S(2)}, u32[]{:S(2)}) collective-permute-start(bf16[80,4096]{1,0:T(8,128)(2,1)S(1)} %get-tuple-element.33), channel_id=1, source_target_pairs={{0,192},{8,56},{16,208},{24,8},{32,224},{40,24},{48,240},{56,40},{... | collective-permute-start | bytes 1966088 | tf_op jit(solution)/shard_map/ppermute | solution.py:235
  211.1 5.3 %collective-permute-done.21 = bf16[80,4096]{1,0:T(8,128)(2,1)S(1)} collective-permute-done((bf16[80,4096]{1,0:T(8,128)(2,1)S(1)}, bf16[80,4096]{1,0:T(8,128)(2,1)S(1)}, u32[]{:S(2)}, u32[]{:S(2)}) %collective-permute-start.21) | collective-permute-done | bytes 655392 | tf_op jit(solution)/shard_map/ppermute | solution.py:235
  216.7 6.9 %collective-permute-done.25 = bf16[80,4096]{1,0:T(8,128)(2,1)S(1)} collective-permute-done((bf16[80,4096]{1,0:T(8,128)(2,1)S(1)}, bf16[80,4096]{1,0:T(8,128)(2,1)S(1)}, u32[]{:S(2)}, u32[]{:S(2)}) %collective-permute-start.25) | collective-permute-done | bytes 655392 | tf_op jit(solution)/shard_map/ppermute | solution.py:235
  223.8 3.8 %collective-permute-start.26 = (bf16[80,4096]{1,0:T(8,128)(2,1)S(1)}, bf16[80,4096]{1,0:T(8,128)(2,1)S(1)}, u32[]{:S(2)}, u32[]{:S(2)}) collective-permute-start(bf16[80,4096]{1,0:T(8,128)(2,1)S(1)} %add_convert_fusion.1), channel_id=1, source_target_pairs={{0,192},{8,56},{16,208},{24,8},{32,224},{40,24},{48,240},{56,40},{... | collective-permute-start | bytes 1966088 | tf_op jit(solution)/shard_map/ppermute | solution.py:235
  227.6 3.0 %collective-permute-done.22 = bf16[80,4096]{1,0:T(8,128)(2,1)S(1)} collective-permute-done((bf16[80,4096]{1,0:T(8,128)(2,1)S(1)}, bf16[80,4096]{1,0:T(8,128)(2,1)S(1)}, u32[]{:S(2)}, u32[]{:S(2)}) %collective-permute-start.22) | collective-permute-done | bytes 655392 | tf_op jit(solution)/shard_map/ppermute | solution.py:235
  230.8 4.8 %collective-permute-start.23 = (bf16[40,4096]{1,0:T(8,128)(2,1)S(1)}, bf16[40,4096]{1,0:T(8,128)(2,1)S(1)}, u32[]{:S(2)}, u32[]{:S(2)}) collective-permute-start(bf16[40,4096]{1,0:T(8,128)(2,1)S(1)} %slice.265), channel_id=1, source_target_pairs={{0,48},{8,200},{16,0},{24,216},{32,16},{40,232},{48,32},{56,248},{... | collective-permute-start | bytes 983048 | tf_op jit(solution)/shard_map/ppermute | solution.py:235
  235.7 3.5 %collective-permute-done.26 = bf16[80,4096]{1,0:T(8,128)(2,1)S(1)} collective-permute-done((bf16[80,4096]{1,0:T(8,128)(2,1)S(1)}, bf16[80,4096]{1,0:T(8,128)(2,1)S(1)}, u32[]{:S(2)}, u32[]{:S(2)}) %collective-permute-start.26) | collective-permute-done | bytes 655392 | tf_op jit(solution)/shard_map/ppermute | solution.py:235
  239.5 1.1 collective-permute-start.27
  240.6 2.1 collective-permute-start.28
  242.7 1.1 collective-permute-done.23
  243.8 5.0 %collective-permute-done.27 = bf16[40,4096]{1,0:T(8,128)(2,1)S(1)} collective-permute-done((bf16[40,4096]{1,0:T(8,128)(2,1)S(1)}, bf16[40,4096]{1,0:T(8,128)(2,1)S(1)}, u32[]{:S(2)}, u32[]{:S(2)}) %collective-permute-start.27) | collective-permute-done | bytes 327712 | tf_op jit(solution)/shard_map/ppermute | solution.py:235
  248.8 1.7 collective-permute-done.28
  250.6 0.9 reshape.177
  251.5 3.5 %all-to-all-start.2 = ((bf16[8,5,4096]{2,1,0:T(8,128)(2,1)}), bf16[8,5,4096]{2,1,0:T(8,128)(2,1)S(1)}, u32[]{:S(2)}, u32[]{:S(2)}) async-start(bf16[8,5,4096]{2,1,0:T(8,128)(2,1)} %reshape.177), calls=%async_computation.3 | async-start | bytes 1048576 | tf_op jit(solution)/shard_map/all_to_all | solution.py:437
  255.3 12.9 %all-to-all-done.2 = bf16[8,5,4096]{2,1,0:T(8,128)(2,1)S(1)} async-done(((bf16[8,5,4096]{2,1,0:T(8,128)(2,1)}), bf16[8,5,4096]{2,1,0:T(8,128)(2,1)S(1)}, u32[]{:S(2)}, u32[]{:S(2)}) %all-to-all-start.2) | async-done | bytes 327712 | tf_op jit(solution)/shard_map/all_to_all | solution.py:437
  (94 shorter events, 16.1 us)
Async XLA Ops:
  7.2 247.9 %copy-start = (bf16[4096,8]{0,1:T(8,128)(2,1)S(1)}, bf16[4096,8]{0,1:T(8,128)(2,1)}, u32[]{:S(2)}) copy-start(bf16[4096,8]{0,1:T(8,128)(2,1)} %param.29) | copy-start | bytes 196612
  7.2 66.6 %all-gather.3.cloned.1.call-start = ((), (), s32[]{:S(2)}) async-start(), calls=%async_computation.5 | async-start | bytes 8650752 | tf_op jit(solution)/shard_map/all_gather | solution.py:357
  7.9 111.2 %reduce-scatter.2.cloned.1.call-start = ((), (), s32[]{:S(2)}) async-start(), calls=%async_computation.4 | async-start | bytes 516096 | tf_op jit(solution)/shard_map/reduce_scatter | solution.py:361
  8.0 14.6 %collective-permute-start.1 = (bf16[4096,384]{1,0:T(8,128)(2,1)}, bf16[4096,384]{1,0:T(8,128)(2,1)}, u32[]{:S(2)}, u32[]{:S(2)}) collective-permute-start(bf16[4096,384]{1,0:T(8,128)(2,1)} %bitcast.218), channel_id=1, source_target_pairs={{0,8},{8,0},{16,24},{24,16},{32,40},{40,32},{48,56},{56,48},{64,72... | collective-permute-start | bytes 9437192 | tf_op jit(solution)/shard_map/ppermute | solution.py:35
  8.1 14.5 %collective-permute-start.2 = (bf16[4096,384]{1,0:T(8,128)(2,1)}, bf16[4096,384]{1,0:T(8,128)(2,1)}, u32[]{:S(2)}, u32[]{:S(2)}) collective-permute-start(bf16[4096,384]{1,0:T(8,128)(2,1)} %bitcast.220), channel_id=1, source_target_pairs={{0,8},{8,0},{16,24},{24,16},{32,40},{40,32},{48,56},{56,48},{64,72... | collective-permute-start | bytes 9437192 | tf_op jit(solution)/shard_map/ppermute | solution.py:35
  8.6 14.5 %collective-permute-start.3 = (bf16[384,4096]{1,0:T(8,128)(2,1)}, bf16[384,4096]{1,0:T(8,128)(2,1)}, u32[]{:S(2)}, u32[]{:S(2)}) collective-permute-start(bf16[384,4096]{1,0:T(8,128)(2,1)} %bitcast.222), channel_id=1, source_target_pairs={{0,8},{8,0},{16,24},{24,16},{32,40},{40,32},{48,56},{56,48},{64,72... | collective-permute-start | bytes 9437192 | tf_op jit(solution)/shard_map/ppermute | solution.py:35
  9.4 5.2 %collective-permute-start = (bf16[3,1024]{1,0:T(4,128)(2,1)S(1)}, bf16[3,1024]{1,0:T(4,128)(2,1)S(1)}, u32[]{:S(2)}, u32[]{:S(2)}) collective-permute-start(bf16[3,1024]{1,0:T(4,128)(2,1)S(1)} %slice.120), channel_id=1, source_target_pairs={{0,8},{8,16},{16,24},{24,32},{32,40},{40,48},{48,56},{56,64},{64,7... | collective-permute-start | bytes 18440 | tf_op jit(solution)/shard_map/ppermute | solution.py:225
  14.6 0.6 copy-start.9
  22.5 23.7 %copy-start.1 = (f32[128,128]{1,0:T(8,128)S(1)}, f32[128,128]{1,0:T(8,128)}, u32[]{:S(2)}) copy-start(f32[128,128]{1,0:T(8,128)} %get-tuple-element.22.scaled_ref) | copy-start | bytes 196612
  22.5 23.8 %copy-start.2 = (f32[2048]{0:T(1024)S(1)}, f32[2048]{0:T(1024)}, u32[]{:S(2)}) copy-start(f32[2048]{0:T(1024)} %reshape.182.out_ref) | copy-start | bytes 24580
  22.5 23.8 %copy-start.3 = (bf16[128,1024]{1,0:T(8,128)(2,1)S(1)}, bf16[128,1024]{1,0:T(8,128)(2,1)}, u32[]{:S(2)}) copy-start(bf16[128,1024]{1,0:T(8,128)(2,1)} %gate_hbm.1) | copy-start | bytes 786436
  22.5 23.8 %copy-start.4 = (f32[1024,128]{1,0:T(8,128)S(1)}, f32[1024,128]{1,0:T(8,128)}, u32[]{:S(2)}) copy-start(f32[1024,128]{1,0:T(8,128)} %get-tuple-element.18.y_ref) | copy-start | bytes 1572868
  22.5 23.8 %copy-start.5 = (f32[1024,128]{1,0:T(8,128)S(1)}, f32[1024,128]{1,0:T(8,128)}, u32[]{:S(2)}) copy-start(f32[1024,128]{1,0:T(8,128)} %get-tuple-element.19.sums_ref) | copy-start | bytes 1572868
  23.0 1.9 collective-permute-start.4
  26.6 8.4 %collective-permute-start.7 = (f32[136,128]{1,0:T(8,128)S(1)}, f32[136,128]{1,0:T(8,128)S(1)}, u32[]{:S(2)}, u32[]{:S(2)}) collective-permute-start(f32[136,128]{1,0:T(8,128)S(1)} %maximum_bitcast_fusion), channel_id=1, source_target_pairs={{0,48},{8,56},{16,0},{24,8},{32,16},{40,24},{48,32},{56,40},{64,11... | collective-permute-start | bytes 208904 | tf_op jit(solution)/shard_map/ppermute | solution.py:35
  27.2 7.9 %collective-permute-start.6 = (f32[136,128]{1,0:T(8,128)S(1)}, f32[136,128]{1,0:T(8,128)S(1)}, u32[]{:S(2)}, u32[]{:S(2)}) collective-permute-start(f32[136,128]{1,0:T(8,128)S(1)} %maximum_bitcast_fusion), channel_id=1, source_target_pairs={{0,32},{8,40},{16,48},{24,56},{32,0},{40,8},{48,16},{56,24},{64,96... | collective-permute-start | bytes 208904 | tf_op jit(solution)/shard_map/ppermute | solution.py:35
  29.9 6.1 %collective-permute-start.5 = (f32[136,128]{1,0:T(8,128)S(1)}, f32[136,128]{1,0:T(8,128)S(1)}, u32[]{:S(2)}, u32[]{:S(2)}) collective-permute-start(f32[136,128]{1,0:T(8,128)S(1)} %maximum_bitcast_fusion), channel_id=1, source_target_pairs={{0,16},{8,24},{16,32},{24,40},{32,48},{40,56},{48,0},{56,8},{64,80... | collective-permute-start | bytes 208904 | tf_op jit(solution)/shard_map/ppermute | solution.py:35
  37.0 5.6 %collective-permute-start.8 = (f32[136,128]{1,0:T(8,128)S(1)}, f32[136,128]{1,0:T(8,128)S(1)}, u32[]{:S(2)}, u32[]{:S(2)}) collective-permute-start(f32[136,128]{1,0:T(8,128)S(1)} %maximum_bitcast_fusion.1), channel_id=1, source_target_pairs={{0,64},{8,72},{16,80},{24,88},{32,96},{40,104},{48,112},{56,120},{... | collective-permute-start | bytes 208904 | tf_op jit(solution)/shard_map/ppermute | solution.py:35
  38.8 7.4 %collective-permute-start.10 = (f32[136,128]{1,0:T(8,128)S(1)}, f32[136,128]{1,0:T(8,128)S(1)}, u32[]{:S(2)}, u32[]{:S(2)}) collective-permute-start(f32[136,128]{1,0:T(8,128)S(1)} %maximum_bitcast_fusion.1), channel_id=1, source_target_pairs={{0,192},{8,200},{16,208},{24,216},{32,224},{40,232},{48,240},{56,2... | collective-permute-start | bytes 208904 | tf_op jit(solution)/shard_map/ppermute | solution.py:35
  40.3 5.8 %collective-permute-start.9 = (f32[136,128]{1,0:T(8,128)S(1)}, f32[136,128]{1,0:T(8,128)S(1)}, u32[]{:S(2)}, u32[]{:S(2)}) collective-permute-start(f32[136,128]{1,0:T(8,128)S(1)} %maximum_bitcast_fusion.1), channel_id=1, source_target_pairs={{0,128},{8,136},{16,144},{24,152},{32,160},{40,168},{48,176},{56,1... | collective-permute-start | bytes 208904 | tf_op jit(solution)/shard_map/ppermute | solution.py:35
  79.8 14.6 %copy-start.8 = (s32[16,2]{0,1:T(2,128)S(1)}, s32[16,2]{0,1:T(2,128)}, u32[]{:S(2)}) copy-start(s32[16,2]{0,1:T(2,128)} %param.30) | copy-start | bytes 388
  87.2 32.9 %copy-start.6 = (bf16[16,4096]{1,0:T(8,128)(2,1)S(1)}, bf16[16,4096]{1,0:T(8,128)(2,1)}, u32[]{:S(2)}) copy-start(bf16[16,4096]{1,0:T(8,128)(2,1)} %param.27) | copy-start | bytes 393220
  87.2 33.1 %copy-start.7 = (f32[4096]{0:T(1024)S(1)}, f32[4096]{0:T(1024)}, u32[]{:S(2)}) copy-start(f32[4096]{0:T(1024)} %param.28) | copy-start | bytes 49156
  87.2 32.8 %all-to-all-start = ((bf16[8,16,2304]{2,1,0:T(8,128)(2,1)}), bf16[8,16,2304]{2,1,0:T(8,128)(2,1)S(1)}, u32[]{:S(2)}, u32[]{:S(2)}) async-start(bf16[8,16,2304]{2,1,0:T(8,128)(2,1)} %project.3), calls=%async_computation.1 | async-start | bytes 1179648 | tf_op jit(solution)/shard_map/all_to_all | solution.py:363
  141.0 19.5 %collective-permute-start.15 = (bf16[40,4096]{1,0:T(8,128)(2,1)S(1)}, bf16[40,4096]{1,0:T(8,128)(2,1)S(1)}, u32[]{:S(2)}, u32[]{:S(2)}) collective-permute-start(bf16[40,4096]{1,0:T(8,128)(2,1)S(1)} %reshape.176), channel_id=1, source_target_pairs={{0,48},{8,200},{16,0},{24,216},{32,16},{40,232},{48,32},{56,248},{... | collective-permute-start | bytes 983048 | tf_op jit(solution)/shard_map/ppermute | solution.py:235
  141.8 18.6 %collective-permute-start.14 = (bf16[40,4096]{1,0:T(8,128)(2,1)S(1)}, bf16[40,4096]{1,0:T(8,128)(2,1)S(1)}, u32[]{:S(2)}, u32[]{:S(2)}) collective-permute-start(bf16[40,4096]{1,0:T(8,128)(2,1)S(1)} %reshape.176), channel_id=1, source_target_pairs={{0,32},{8,136},{16,48},{24,152},{32,0},{40,168},{48,16},{56,184},{... | collective-permute-start | bytes 983048 | tf_op jit(solution)/shard_map/ppermute | solution.py:235
  143.5 11.6 %collective-permute-start.11 = (bf16[40,4096]{1,0:T(8,128)(2,1)S(1)}, bf16[40,4096]{1,0:T(8,128)(2,1)S(1)}, u32[]{:S(2)}, u32[]{:S(2)}) collective-permute-start(bf16[40,4096]{1,0:T(8,128)(2,1)S(1)} %reshape.176), channel_id=1, source_target_pairs={{0,16},{8,72},{16,32},{24,88},{32,48},{40,104},{48,0},{56,120},{64... | collective-permute-start | bytes 983048 | tf_op jit(solution)/shard_map/ppermute | solution.py:235
  155.1 14.9 %collective-permute-start.12 = (bf16[80,4096]{1,0:T(8,128)(2,1)S(1)}, bf16[80,4096]{1,0:T(8,128)(2,1)S(1)}, u32[]{:S(2)}, u32[]{:S(2)}) collective-permute-start(bf16[80,4096]{1,0:T(8,128)(2,1)S(1)} %constant_dynamic-update-slice_fusion.refs_2_), channel_id=1, source_target_pairs={{0,64},{8,24},{16,80},{24,40},{32,96},{40,56},{48,112},{56,8},{64,... | collective-permute-start | bytes 1966088 | tf_op jit(solution)/shard_map/ppermute | solution.py:235
  160.5 10.7 %collective-permute-start.16 = (bf16[80,4096]{1,0:T(8,128)(2,1)S(1)}, bf16[80,4096]{1,0:T(8,128)(2,1)S(1)}, u32[]{:S(2)}, u32[]{:S(2)}) collective-permute-start(bf16[80,4096]{1,0:T(8,128)(2,1)S(1)} %constant_dynamic-update-slice_fusion.2.refs_3_), channel_id=1, source_target_pairs={{0,192},{8,56},{16,208},{24,8},{32,224},{40,24},{48,240},{56,40},{... | collective-permute-start | bytes 1966088 | tf_op jit(solution)/shard_map/ppermute | solution.py:235
  161.6 16.6 %collective-permute-start.18 = (bf16[80,4096]{1,0:T(8,128)(2,1)S(1)}, bf16[80,4096]{1,0:T(8,128)(2,1)S(1)}, u32[]{:S(2)}, u32[]{:S(2)}) collective-permute-start(bf16[80,4096]{1,0:T(8,128)(2,1)S(1)} %constant_dynamic-update-slice_fusion.refs_2_), channel_id=1, source_target_pairs={{0,192},{8,56},{16,208},{24,8},{32,224},{40,24},{48,240},{56,40},{... | collective-permute-start | bytes 1966088 | tf_op jit(solution)/shard_map/ppermute | solution.py:235
  163.6 14.6 %collective-permute-start.19 = (bf16[80,4096]{1,0:T(8,128)(2,1)S(1)}, bf16[80,4096]{1,0:T(8,128)(2,1)S(1)}, u32[]{:S(2)}, u32[]{:S(2)}) collective-permute-start(bf16[80,4096]{1,0:T(8,128)(2,1)S(1)} %constant_dynamic-update-slice_fusion.2.refs_3_), channel_id=1, source_target_pairs={{0,64},{8,24},{16,80},{24,40},{32,96},{40,56},{48,112},{56,8},{64,... | collective-permute-start | bytes 1966088 | tf_op jit(solution)/shard_map/ppermute | solution.py:235
  170.0 14.0 %collective-permute-start.13 = (bf16[80,4096]{1,0:T(8,128)(2,1)S(1)}, bf16[80,4096]{1,0:T(8,128)(2,1)S(1)}, u32[]{:S(2)}, u32[]{:S(2)}) collective-permute-start(bf16[80,4096]{1,0:T(8,128)(2,1)S(1)} %collective-permute-done.12.refs_4_), channel_id=1, source_target_pairs={{0,64},{8,24},{16,80},{24,40},{32,96},{40,56},{48,112},{56,8},{64,... | collective-permute-start | bytes 1966088 | tf_op jit(solution)/shard_map/ppermute | solution.py:235
  171.2 14.0 %collective-permute-start.17 = (bf16[80,4096]{1,0:T(8,128)(2,1)S(1)}, bf16[80,4096]{1,0:T(8,128)(2,1)S(1)}, u32[]{:S(2)}, u32[]{:S(2)}) collective-permute-start(bf16[80,4096]{1,0:T(8,128)(2,1)S(1)} %collective-permute-done.16.refs_5_), channel_id=1, source_target_pairs={{0,192},{8,56},{16,208},{24,8},{32,224},{40,24},{48,240},{56,40},{... | collective-permute-start | bytes 1966088 | tf_op jit(solution)/shard_map/ppermute | solution.py:235
  204.6 11.9 %collective-permute-start.21 = (bf16[80,4096]{1,0:T(8,128)(2,1)S(1)}, bf16[80,4096]{1,0:T(8,128)(2,1)S(1)}, u32[]{:S(2)}, u32[]{:S(2)}) collective-permute-start(bf16[80,4096]{1,0:T(8,128)(2,1)S(1)} %get-tuple-element.29), channel_id=1, source_target_pairs={{0,64},{8,24},{16,80},{24,40},{32,96},{40,56},{48,112},{56,8},{64,... | collective-permute-start | bytes 1966088 | tf_op jit(solution)/shard_map/ppermute | solution.py:235
  205.0 22.5 %collective-permute-start.20 = (bf16[80,4096]{1,0:T(8,128)(2,1)S(1)}, bf16[80,4096]{1,0:T(8,128)(2,1)S(1)}, u32[]{:S(2)}, u32[]{:S(2)}) collective-permute-start(bf16[80,4096]{1,0:T(8,128)(2,1)S(1)} %get-tuple-element.27), channel_id=1, source_target_pairs={{0,192},{8,56},{16,208},{24,8},{32,224},{40,24},{48,240},{56,40},{... | collective-permute-start | bytes 1966088 | tf_op jit(solution)/shard_map/ppermute | solution.py:235
  207.9 27.8 %collective-permute-start.24 = (bf16[80,4096]{1,0:T(8,128)(2,1)S(1)}, bf16[80,4096]{1,0:T(8,128)(2,1)S(1)}, u32[]{:S(2)}, u32[]{:S(2)}) collective-permute-start(bf16[80,4096]{1,0:T(8,128)(2,1)S(1)} %get-tuple-element.31), channel_id=1, source_target_pairs={{0,64},{8,24},{16,80},{24,40},{32,96},{40,56},{48,112},{56,8},{64,... | collective-permute-start | bytes 1966088 | tf_op jit(solution)/shard_map/ppermute | solution.py:235
  207.9 15.8 %collective-permute-start.25 = (bf16[80,4096]{1,0:T(8,128)(2,1)S(1)}, bf16[80,4096]{1,0:T(8,128)(2,1)S(1)}, u32[]{:S(2)}, u32[]{:S(2)}) collective-permute-start(bf16[80,4096]{1,0:T(8,128)(2,1)S(1)} %get-tuple-element.33), channel_id=1, source_target_pairs={{0,192},{8,56},{16,208},{24,8},{32,224},{40,24},{48,240},{56,40},{... | collective-permute-start | bytes 1966088 | tf_op jit(solution)/shard_map/ppermute | solution.py:235
  216.6 14.0 %collective-permute-start.22 = (bf16[80,4096]{1,0:T(8,128)(2,1)S(1)}, bf16[80,4096]{1,0:T(8,128)(2,1)S(1)}, u32[]{:S(2)}, u32[]{:S(2)}) collective-permute-start(bf16[80,4096]{1,0:T(8,128)(2,1)S(1)} %add_convert_fusion.2), channel_id=1, source_target_pairs={{0,64},{8,24},{16,80},{24,40},{32,96},{40,56},{48,112},{56,8},{64,... | collective-permute-start | bytes 1966088 | tf_op jit(solution)/shard_map/ppermute | solution.py:235
  223.8 15.4 %collective-permute-start.26 = (bf16[80,4096]{1,0:T(8,128)(2,1)S(1)}, bf16[80,4096]{1,0:T(8,128)(2,1)S(1)}, u32[]{:S(2)}, u32[]{:S(2)}) collective-permute-start(bf16[80,4096]{1,0:T(8,128)(2,1)S(1)} %add_convert_fusion.1), channel_id=1, source_target_pairs={{0,192},{8,56},{16,208},{24,8},{32,224},{40,24},{48,240},{56,40},{... | collective-permute-start | bytes 1966088 | tf_op jit(solution)/shard_map/ppermute | solution.py:235
  230.8 12.9 %collective-permute-start.23 = (bf16[40,4096]{1,0:T(8,128)(2,1)S(1)}, bf16[40,4096]{1,0:T(8,128)(2,1)S(1)}, u32[]{:S(2)}, u32[]{:S(2)}) collective-permute-start(bf16[40,4096]{1,0:T(8,128)(2,1)S(1)} %slice.265), channel_id=1, source_target_pairs={{0,48},{8,200},{16,0},{24,216},{32,16},{40,232},{48,32},{56,248},{... | collective-permute-start | bytes 983048 | tf_op jit(solution)/shard_map/ppermute | solution.py:235
  239.5 9.3 %collective-permute-start.27 = (bf16[40,4096]{1,0:T(8,128)(2,1)S(1)}, bf16[40,4096]{1,0:T(8,128)(2,1)S(1)}, u32[]{:S(2)}, u32[]{:S(2)}) collective-permute-start(bf16[40,4096]{1,0:T(8,128)(2,1)S(1)} %get-tuple-element.47), channel_id=1, source_target_pairs={{0,32},{8,136},{16,48},{24,152},{32,0},{40,168},{48,16},{56,184},{... | collective-permute-start | bytes 983048 | tf_op jit(solution)/shard_map/ppermute | solution.py:235
  240.6 9.8 %collective-permute-start.28 = (bf16[40,4096]{1,0:T(8,128)(2,1)S(1)}, bf16[40,4096]{1,0:T(8,128)(2,1)S(1)}, u32[]{:S(2)}, u32[]{:S(2)}) collective-permute-start(bf16[40,4096]{1,0:T(8,128)(2,1)S(1)} %get-tuple-element.48), channel_id=1, source_target_pairs={{0,16},{8,72},{16,32},{24,88},{32,48},{40,104},{48,0},{56,120},{64... | collective-permute-start | bytes 983048 | tf_op jit(solution)/shard_map/ppermute | solution.py:235
  251.5 16.7 %all-to-all-start.2 = ((bf16[8,5,4096]{2,1,0:T(8,128)(2,1)}), bf16[8,5,4096]{2,1,0:T(8,128)(2,1)S(1)}, u32[]{:S(2)}, u32[]{:S(2)}) async-start(bf16[8,5,4096]{2,1,0:T(8,128)(2,1)} %reshape.177), calls=%async_computation.3 | async-start | bytes 1048576 | tf_op jit(solution)/shard_map/all_to_all | solution.py:437
Sparse Core Ops, SparseCore 0:
  10.6 63.1 all-gather.2
  79.9 39.2 reduce-scatter.1

commit v5 on v4

--- a/solution.py
+++ b/solution.py
@@ -299,7 +299,12 @@
 
 def experts_of_rows(block, here, there):
     dtype = block.dtype
-    near = [block] + [around(block, "inner", k) for k in range(1, SIDE)]
+    half = block.shape[1] // 2
+    after, before = around(block, "inner", 1), around(block, "inner", -1)
+    across = jnp.concatenate(
+        [around(after[:, :half], "inner", 1), around(before[:, half:], "inner", -1)], axis=1
+    )
+    near = [block, after, across, before]
     low, high = jnp.concatenate(near[:2], axis=0), jnp.concatenate(near[2:], axis=0)
     low_up = around(low, "outer", 1)
     high_down = around(high, "outer", -1)
@@ -324,45 +329,37 @@
     return added(blocks[0], *back).astype(dtype)
 
 
-def project_kernel(mixed_ref, weight_ref, out_ref):
+def project_kernel(mixed_ref, *refs):
+    blocks, out_ref = refs[:-1], refs[-1]
     owners, rows = out_ref.shape[:2]
-    both = jnp.concatenate([weight_ref[0], weight_ref[1]], axis=1)
-    result = jnp.dot(mixed_ref[...], both, preferred_element_type=jnp.float32).astype(out_ref.dtype)
+    weight = jnp.concatenate([block[...] for block in blocks], axis=1)
+    result = jnp.dot(mixed_ref[...], weight, preferred_element_type=jnp.float32).astype(out_ref.dtype)
     for owner in range(owners):
         out_ref[owner] = result[owner * rows : (owner + 1) * rows]
 
 
-def project_part(mixed, blocks, begin, end):
+def project(mixed, weight):
+    blocks = lax.all_gather(weight, "seq")
     owners = lax.axis_size("exp")
     tokens, depth = mixed.shape
+    count = blocks.shape[0]
+    group = SIDE
     rows = tokens // owners
-    count = end - begin
-    return pl.pallas_call(
+    views = [pl.BlockSpec((None, depth, LANES), lambda i, q=q: (group * i + q, 0, 0)) for q in range(group)]
+    terms = pl.pallas_call(
         project_kernel,
         name="project",
-        grid=(count // 2,),
+        grid=(count // group,),
         out_shape=jax.ShapeDtypeStruct((owners, rows, count * LANES), jnp.bfloat16),
-        in_specs=[VMEM, pl.BlockSpec((2, depth, LANES), lambda i: (i + begin // 2, 0, 0))],
-        out_specs=pl.BlockSpec((owners, rows, 2 * LANES), lambda i: (0, 0, i)),
+        in_specs=[VMEM] + views,
+        out_specs=pl.BlockSpec((owners, rows, group * LANES), lambda i: (0, 0, i)),
         compiler_params=pltpu.CompilerParams(vmem_limit_bytes=56 << 20),
         cost_estimate=pl.CostEstimate(
-            flops=2 * tokens * depth * count * LANES,
-            transcendentals=0,
-            bytes_accessed=2 * depth * count * LANES + 4 * tokens * depth,
+            flops=2 * tokens * depth * count * LANES, transcendentals=0, bytes_accessed=10_000_000
         ),
-    )(mixed, blocks)
-
-
-def project(mixed, weight):
-    blocks = lax.all_gather(weight, "seq")
-    count = blocks.shape[0]
-    begin = count * 7 // 16 // 2 * 2
-    first = project_part(mixed, blocks, 0, begin)
-    first = lax.psum_scatter(first, "exp", scatter_dimension=0, tiled=False)
-    second = project_part(mixed, blocks, begin, count)
-    second = lax.all_to_all(second, "exp", 0, 0, tiled=True)
-    second = added(*(second[k] for k in range(second.shape[0])))
-    return jnp.concatenate([first.astype(jnp.float32), second], axis=1)
+    )(mixed, *([blocks] * group))
+    terms = lax.all_to_all(terms, "exp", 0, 0, tiled=True)
+    return added(*(terms[k] for k in range(owners)))
 
 
 def shards(
@@ -426,13 +423,10 @@
         jnp.bfloat16
     )
     repeated = jnp.broadcast_to(normed[:, None, :], (rows, 2, model_width)).reshape(-1, model_width)
-    outgoing = (
-        jnp.dot(placing, repeated, preferred_element_type=jnp.float32)
-        .astype(jnp.bfloat16)
-        .reshape(experts, capacity, model_width)
-    )
+    outgoing = jnp.dot(placing, repeated, preferred_element_type=jnp.float32).astype(jnp.bfloat16)
+    outgoing = outgoing.reshape(experts, -1, LANES)
     arrived = lax.all_to_all(outgoing, "exp", split_axis=0, concat_axis=0, tiled=True)
-    flat_rows = arrived.reshape(-1, arrived.shape[2])
+    flat_rows = arrived.reshape(-1, model_width)
     summed_out = experts_of_rows(flat_rows, here, there)
     returned = lax.all_to_all(
         summed_out.reshape(arrived.shape), "exp", split_axis=0, concat_axis=0, tiled=True

time: 280 us -> 271 us (0.968)
  waiting for transfers between devices: 127 us -> 138 us
  starting transfers between devices: 58.3 us -> 51.1 us
  Pallas kernels: 43.8 us -> 38.3 us
  blocking collectives: 19.8 us -> 16.1 us
    all_to_all x1, waiting for transfers between devices: 0.01 us -> 28.8 us  [project(): terms = lax.all_to_all(terms, 'exp', 0, 0, tiled=True)]
    reduce_scatter x1 -> x0, waiting for transfers between devices: 24.5 us -> none  [project(): first = lax.psum_scatter(first, 'exp', scatter_dimension=0, tiled=False)]
    ppermute x18 -> x19, waiting for transfers between devices: 54.8 us -> 62.9 us  [around(): return lax.ppermute(block, 'seq', route)]
    ppermute x18 -> x19, starting transfers between devices: 34.3 us -> 27.2 us  [around(): return lax.ppermute(block, 'seq', route)]
    pallas_call x2 -> x1, Pallas kernels: 13.4 us -> 7.86 us  [project(): pl.pallas_call(project_kernel, name='project', grid=(count // group,), ou...]
    all_to_all x1, blocking collectives: 19.8 us -> 16.1 us  [shards(): lax.all_to_all(outgoing, 'exp', split_axis=0, concat_axis=0, tiled=True)]
  transfers between devices with their start and end apart: 33 -> 33, of which waited for: 23 -> 24; matrix products, arithmetic and copies ran while one was open for 3% -> 3% of each run, Pallas kernels for 7% -> 4%
where the time goes in v5:
time: 271 us; the launch traced here: 269 us
  waiting for transfers between devices  138 us (51%)
  starting transfers between devices  51.1 us (19%)
  Pallas kernels  38.3 us (14%)
  blocking collectives  16.1 us (6%)
  between operations  14.5 us (5%)
  local copies, waits for them, and re-layouts  6.24 us (2%)
  other arithmetic  5.17 us (2%)
    ppermute x19, waiting for transfers between devices, around(): return lax.ppermute(block, 'seq', route)  62.9 us
    all_to_all x1, waiting for transfers between devices, project(): terms = lax.all_to_all(terms, 'exp', 0, 0, tiled=True)  28.8 us
    ppermute x19, starting transfers between devices, around(): return lax.ppermute(block, 'seq', route)  27.2 us
    all_gather x1, waiting for transfers between devices, project(): blocks = lax.all_gather(weight, 'seq')  23.7 us
    pallas_call x1, Pallas kernels, expert(): pl.pallas_call(functools.partial(expert_kernel, steps), name='expert', gr...  19.3 us
    all_to_all x1, blocking collectives, shards(): lax.all_to_all(outgoing, 'exp', split_axis=0, concat_axis=0, tiled=True)  16.1 us
    ppermute x10, starting transfers between devices, moved(): return lax.ppermute(block, 'seq', route)  11 us
    all_to_all x1, waiting for transfers between devices, shards(): lax.all_to_all(summed_out.reshape(arrived.shape), 'exp', split_axis=0, co...  10.8 us
  transfers between devices with their start and end apart: 33, of which 24 were waited for; matrix products, arithmetic and copies ran while one was open for 3% of the time, Pallas kernels for 4%

profile of v5, /device:TPU:6, one launch (start us, length us, event | category | flops | bytes accessed | tf_op | source)
XLA Modules:
  0.0 269.5 jit_solution(16119006947790818548)
XLA Ops:
  9.3 2.3 collective-permute-start
  15.2 7.2 %local_scan.1 = (f32[1024,128]{1,0:T(8,128)}, f32[1024,128]{1,0:T(8,128)}, f32[136,128]{1,0:T(8,128)}, f32[128,128]{1,0:T(8,128)}) custom-call(bf16[128,1024]{1,0:T(8,128)(2,1)} %inp_hbm.1, bf16[128,1024]{1,0:T(8,128)(2,1)} %raw_hbm.1, f32[16,1024]{1,0:T(8,128)} %rate_hbm.1, f32[4,1024]{1,0:T(4,128)} %taps_hbm.1, f32[1,1024]{1,0:T(1,128)} %bitcast.224, ...), custom_call_target="tpu_custom_call" | custom-call | flops 8000000 | bytes 2000000 | tf_op jit(solution)/shard_map/local_scan/pallas_call | solution.py:130
  23.8 1.1 collective-permute-done.4
  25.6 0.9 bitcast_add_fusion.1
  27.1 2.7 %collective-permute-start.6 = (f32[136,128]{1,0:T(8,128)S(1)}, f32[136,128]{1,0:T(8,128)S(1)}, u32[]{:S(2)}, u32[]{:S(2)}) collective-permute-start(f32[136,128]{1,0:T(8,128)S(1)} %maximum_bitcast_fusion), channel_id=1, source_target_pairs={{0,32},{8,40},{16,48},{24,56},{32,0},{40,8},{48,16},{56,24},{64,96... | collective-permute-start | bytes 208904 | tf_op jit(solution)/shard_map/ppermute | solution.py:35
  30.6 4.3 %collective-permute-done.7 = f32[136,128]{1,0:T(8,128)S(1)} collective-permute-done((f32[136,128]{1,0:T(8,128)S(1)}, f32[136,128]{1,0:T(8,128)S(1)}, u32[]{:S(2)}, u32[]{:S(2)}) %collective-permute-start.7) | collective-permute-done | bytes 69664 | tf_op jit(solution)/shard_map/ppermute | solution.py:35
  35.0 0.9 collective-permute-done.5
  35.9 1.0 fusion.20
  36.9 1.8 collective-permute-start.8
  38.8 1.5 collective-permute-start.10
  40.2 2.1 collective-permute-start.9
  42.5 3.5 %collective-permute-done.9 = f32[136,128]{1,0:T(8,128)S(1)} collective-permute-done((f32[136,128]{1,0:T(8,128)S(1)}, f32[136,128]{1,0:T(8,128)S(1)}, u32[]{:S(2)}, u32[]{:S(2)}) %collective-permute-start.9) | collective-permute-done | bytes 69664 | tf_op jit(solution)/shard_map/ppermute | solution.py:35
  46.2 3.9 %finish_scan.1.mixed_ref = bf16[128,1024]{1,0:T(8,128)(2,1)} custom-call(f32[1024,128]{1,0:T(8,128)S(1)} %copy-done.4, f32[1024,128]{1,0:T(8,128)S(1)} %copy-done.5, f32[128,128]{1,0:T(8,128)S(1)} %fusion.9.start_ref, f32[128,128]{1,0:T(8,128)S(1)} %copy-done.1, bf16[128,1024]{1,0:T(8,128)(2,1)S(1)} %copy-done.3, f32[2048]{0:T(1024)S(1)} %copy-done.2), custom_call_target="tpu_custom_call" | custom-call | flops 8000000 | bytes 2000000 | tf_op jit(solution)/shard_map/finish_scan/pallas_call | solution.py:155
  50.1 23.7 %all-gather.3.cloned.1.call-done = bf16[32768,128]{1,0:T(8,128)(2,1)} async-done(((bf16[1024,128]{1,0:T(8,128)(2,1)}), bf16[32768,128]{1,0:T(8,128)(2,1)}) %all-gather.3.cloned.1.call-update) | async-done | bytes 8388624 | tf_op jit(solution)/shard_map/all_gather | solution.py:342
  73.8 7.9 %project.1 = bf16[8,16,4096]{2,1,0:T(8,128)(2,1)} custom-call(bf16[128,1024]{1,0:T(8,128)(2,1)} %finish_scan.1.mixed_ref, bf16[32,1024,128]{2,1,0:T(8,128)(2,1)} %bitcast.212, bf16[32,1024,128]{2,1,0:T(8,128)(2,1)} %bitcast.213, bf16[32,1024,128]{2,1,0:T(8,128)(2,1)} %bitcast.214, bf16[32,1024,128]{2,1,0:T(8,128)(2,1)} %bitcast.215), custom_call_target="tpu_custom_call" | custom-call | flops 1073741824 | bytes 10000000 | tf_op jit(solution)/shard_map/project/pallas_call | solution.py:349
  81.7 7.1 %all-to-all-start = ((bf16[8,16,4096]{2,1,0:T(8,128)(2,1)}), bf16[8,16,4096]{2,1,0:T(8,128)(2,1)S(1)}, u32[]{:S(2)}, u32[]{:S(2)}) async-start(bf16[8,16,4096]{2,1,0:T(8,128)(2,1)} %project.1), calls=%async_computation | async-start | bytes 2097152 | tf_op jit(solution)/shard_map/all_to_all | solution.py:361
  89.2 28.8 %all-to-all-done = bf16[8,16,4096]{2,1,0:T(8,128)(2,1)S(1)} async-done(((bf16[8,16,4096]{2,1,0:T(8,128)(2,1)}), bf16[8,16,4096]{2,1,0:T(8,128)(2,1)S(1)}, u32[]{:S(2)}, u32[]{:S(2)}) %all-to-all-start) | async-done | bytes 1048608 | tf_op jit(solution)/shard_map/all_to_all | solution.py:361
  119.1 16.1 %all_to_all.15 = bf16[8,160,128]{2,1,0:T(8,128)(2,1)S(1)} all-to-all(bf16[8,160,128]{2,1,0:T(8,128)(2,1)S(1)} %reshape.173), channel_id=1, replica_groups=mesh['seq'=32,'exp'=8] {'exp'}, dimensions={0} | all-to-all | bytes 655360 | tf_op jit(solution)/shard_map/all_to_all | solution.py:428
  135.4 0.9 collective-permute-start.15
  136.3 2.4 collective-permute-start.11
  138.7 5.0 %collective-permute-done.15 = bf16[40,4096]{1,0:T(8,128)(2,1)S(1)} collective-permute-done((bf16[40,4096]{1,0:T(8,128)(2,1)S(1)}, bf16[40,4096]{1,0:T(8,128)(2,1)S(1)}, u32[]{:S(2)}, u32[]{:S(2)}) %collective-permute-start.15) | collective-permute-done | bytes 327712 | tf_op jit(solution)/shard_map/ppermute | solution.py:235
  144.1 3.3 %collective-permute-start.14 = (bf16[40,2048]{1,0:T(8,128)(2,1)S(1)}, bf16[40,2048]{1,0:T(8,128)(2,1)S(1)}, u32[]{:S(2)}, u32[]{:S(2)}) collective-permute-start(bf16[40,2048]{1,0:T(8,128)(2,1)S(1)} %slice.184), channel_id=1, source_target_pairs={{0,16},{8,72},{16,32},{24,88},{32,48},{40,104},{48,0},{56,120},{64... | collective-permute-start | bytes 491528 | tf_op jit(solution)/shard_map/ppermute | solution.py:235
  147.6 3.0 %collective-permute-done.16 = bf16[40,2048]{1,0:T(8,128)(2,1)S(1)} collective-permute-done((bf16[40,2048]{1,0:T(8,128)(2,1)S(1)}, bf16[40,2048]{1,0:T(8,128)(2,1)S(1)}, u32[]{:S(2)}, u32[]{:S(2)}) %collective-permute-start.16) | collective-permute-done | bytes 163872 | tf_op jit(solution)/shard_map/ppermute | solution.py:235
  150.6 1.5 collective-permute-done.14
  152.1 0.8 collective-permute-start.17
  152.9 1.2 collective-permute-start.19
  154.1 0.8 collective-permute-start.20
  154.9 4.4 %collective-permute-done.12.refs_4_ = bf16[80,4096]{1,0:T(8,128)(2,1)S(1)} collective-permute-done((bf16[80,4096]{1,0:T(8,128)(2,1)S(1)}, bf16[80,4096]{1,0:T(8,128)(2,1)S(1)}, u32[]{:S(2)}, u32[]{:S(2)}) %collective-permute-start.12) | collective-permute-done | bytes 655392 | tf_op jit(solution)/shard_map/ppermute | solution.py:235
  159.3 3.5 %collective-permute-done.17.refs_5_ = bf16[80,4096]{1,0:T(8,128)(2,1)S(1)} collective-permute-done((bf16[80,4096]{1,0:T(8,128)(2,1)S(1)}, bf16[80,4096]{1,0:T(8,128)(2,1)S(1)}, u32[]{:S(2)}, u32[]{:S(2)}) %collective-permute-start.17) | collective-permute-done | bytes 655392 | tf_op jit(solution)/shard_map/ppermute | solution.py:235
  162.7 1.9 collective-permute-start.18
  164.7 5.1 %collective-permute-done.19.refs_6_ = bf16[80,4096]{1,0:T(8,128)(2,1)S(1)} collective-permute-done((bf16[80,4096]{1,0:T(8,128)(2,1)S(1)}, bf16[80,4096]{1,0:T(8,128)(2,1)S(1)}, u32[]{:S(2)}, u32[]{:S(2)}) %collective-permute-start.19) | collective-permute-done | bytes 655392 | tf_op jit(solution)/shard_map/ppermute | solution.py:235
  169.8 3.6 %collective-permute-done.13.refs_0_ = bf16[80,4096]{1,0:T(8,128)(2,1)S(1)} collective-permute-done((bf16[80,4096]{1,0:T(8,128)(2,1)S(1)}, bf16[80,4096]{1,0:T(8,128)(2,1)S(1)}, u32[]{:S(2)}, u32[]{:S(2)}) %collective-permute-start.13) | collective-permute-done | bytes 655392 | tf_op jit(solution)/shard_map/ppermute | solution.py:235
  173.3 3.5 %collective-permute-done.18.refs_1_ = bf16[80,4096]{1,0:T(8,128)(2,1)S(1)} collective-permute-done((bf16[80,4096]{1,0:T(8,128)(2,1)S(1)}, bf16[80,4096]{1,0:T(8,128)(2,1)S(1)}, u32[]{:S(2)}, u32[]{:S(2)}) %collective-permute-start.18) | collective-permute-done | bytes 655392 | tf_op jit(solution)/shard_map/ppermute | solution.py:235
  176.8 19.3 %expert.1 = (bf16[80,4096]{1,0:T(8,128)(2,1)S(1)}, bf16[80,4096]{1,0:T(8,128)(2,1)S(1)}, bf16[80,4096]{1,0:T(8,128)(2,1)S(1)}, bf16[80,4096]{1,0:T(8,128)(2,1)S(...) custom-call(bf16[80,4096]{1,0:T(8,128)(2,1)S(1)} %collective-permute, ...), custom_call_target="tpu_custom_call" | custom-call | flops 12079595520 | bytes 24000000 | tf_op jit(solution)/shard_map/expert/pallas_call | solution.py:282
  196.3 3.1 %collective-permute-start.21 = (bf16[80,4096]{1,0:T(8,128)(2,1)S(1)}, bf16[80,4096]{1,0:T(8,128)(2,1)S(1)}, u32[]{:S(2)}, u32[]{:S(2)}) collective-permute-start(bf16[80,4096]{1,0:T(8,128)(2,1)S(1)} %get-tuple-element.27), channel_id=1, source_target_pairs={{0,192},{8,56},{16,208},{24,8},{32,224},{40,24},{48,240},{56,40},{... | collective-permute-start | bytes 1966088 | tf_op jit(solution)/shard_map/ppermute | solution.py:235
  199.4 3.2 %collective-permute-start.26 = (bf16[80,4096]{1,0:T(8,128)(2,1)S(1)}, bf16[80,4096]{1,0:T(8,128)(2,1)S(1)}, u32[]{:S(2)}, u32[]{:S(2)}) collective-permute-start(bf16[80,4096]{1,0:T(8,128)(2,1)S(1)} %get-tuple-element.33), channel_id=1, source_target_pairs={{0,192},{8,56},{16,208},{24,8},{32,224},{40,24},{48,240},{56,40},{... | collective-permute-start | bytes 1966088 | tf_op jit(solution)/shard_map/ppermute | solution.py:235
  202.7 5.3 %collective-permute-done.22 = bf16[80,4096]{1,0:T(8,128)(2,1)S(1)} collective-permute-done((bf16[80,4096]{1,0:T(8,128)(2,1)S(1)}, bf16[80,4096]{1,0:T(8,128)(2,1)S(1)}, u32[]{:S(2)}, u32[]{:S(2)}) %collective-permute-start.22) | collective-permute-done | bytes 655392 | tf_op jit(solution)/shard_map/ppermute | solution.py:235
  208.2 6.3 %collective-permute-done.26 = bf16[80,4096]{1,0:T(8,128)(2,1)S(1)} collective-permute-done((bf16[80,4096]{1,0:T(8,128)(2,1)S(1)}, bf16[80,4096]{1,0:T(8,128)(2,1)S(1)}, u32[]{:S(2)}, u32[]{:S(2)}) %collective-permute-start.26) | collective-permute-done | bytes 655392 | tf_op jit(solution)/shard_map/ppermute | solution.py:235
  214.7 4.0 %collective-permute-start.27 = (bf16[80,4096]{1,0:T(8,128)(2,1)S(1)}, bf16[80,4096]{1,0:T(8,128)(2,1)S(1)}, u32[]{:S(2)}, u32[]{:S(2)}) collective-permute-start(bf16[80,4096]{1,0:T(8,128)(2,1)S(1)} %add_convert_fusion.1), channel_id=1, source_target_pairs={{0,192},{8,56},{16,208},{24,8},{32,224},{40,24},{48,240},{56,40},{... | collective-permute-start | bytes 1966088 | tf_op jit(solution)/shard_map/ppermute | solution.py:235
  218.7 3.3 %collective-permute-done.23 = bf16[80,4096]{1,0:T(8,128)(2,1)S(1)} collective-permute-done((bf16[80,4096]{1,0:T(8,128)(2,1)S(1)}, bf16[80,4096]{1,0:T(8,128)(2,1)S(1)}, u32[]{:S(2)}, u32[]{:S(2)}) %collective-permute-start.23) | collective-permute-done | bytes 655392 | tf_op jit(solution)/shard_map/ppermute | solution.py:235
  222.4 9.2 %collective-permute-done.27 = bf16[80,4096]{1,0:T(8,128)(2,1)S(1)} collective-permute-done((bf16[80,4096]{1,0:T(8,128)(2,1)S(1)}, bf16[80,4096]{1,0:T(8,128)(2,1)S(1)}, u32[]{:S(2)}, u32[]{:S(2)}) %collective-permute-start.27) | collective-permute-done | bytes 655392 | tf_op jit(solution)/shard_map/ppermute | solution.py:235
  231.9 2.9 %collective-permute-start.28 = (bf16[40,4096]{1,0:T(8,128)(2,1)S(1)}, bf16[40,4096]{1,0:T(8,128)(2,1)S(1)}, u32[]{:S(2)}, u32[]{:S(2)}) collective-permute-start(bf16[40,4096]{1,0:T(8,128)(2,1)S(1)} %get-tuple-element.49), channel_id=1, source_target_pairs={{0,32},{8,136},{16,48},{24,152},{32,0},{40,168},{48,16},{56,184},{... | collective-permute-start | bytes 983048 | tf_op jit(solution)/shard_map/ppermute | solution.py:235
  234.9 1.7 collective-permute-start.29
  236.6 4.0 %collective-permute-done.28 = bf16[40,4096]{1,0:T(8,128)(2,1)S(1)} collective-permute-done((bf16[40,4096]{1,0:T(8,128)(2,1)S(1)}, bf16[40,4096]{1,0:T(8,128)(2,1)S(1)}, u32[]{:S(2)}, u32[]{:S(2)}) %collective-permute-start.28) | collective-permute-done | bytes 327712 | tf_op jit(solution)/shard_map/ppermute | solution.py:235
  240.6 5.3 %collective-permute-done.29 = bf16[40,4096]{1,0:T(8,128)(2,1)S(1)} collective-permute-done((bf16[40,4096]{1,0:T(8,128)(2,1)S(1)}, bf16[40,4096]{1,0:T(8,128)(2,1)S(1)}, u32[]{:S(2)}, u32[]{:S(2)}) %collective-permute-start.29) | collective-permute-done | bytes 327712 | tf_op jit(solution)/shard_map/ppermute | solution.py:235
  246.1 0.9 reshape.175
  247.0 3.4 %all-to-all-start.2 = ((bf16[8,160,128]{2,1,0:T(8,128)(2,1)}), bf16[8,160,128]{2,1,0:T(8,128)(2,1)S(1)}, u32[]{:S(2)}, u32[]{:S(2)}) async-start(bf16[8,160,128]{2,1,0:T(8,128)(2,1)} %reshape.175), calls=%async_computation.2 | async-start | bytes 655360 | tf_op jit(solution)/shard_map/all_to_all | solution.py:431
  250.7 10.8 %all-to-all-done.2 = bf16[8,160,128]{2,1,0:T(8,128)(2,1)S(1)} async-done(((bf16[8,160,128]{2,1,0:T(8,128)(2,1)}), bf16[8,160,128]{2,1,0:T(8,128)(2,1)S(1)}, u32[]{:S(2)}, u32[]{:S(2)}) %all-to-all-start.2) | async-done | bytes 327712 | tf_op jit(solution)/shard_map/all_to_all | solution.py:431
  (91 shorter events, 14.4 us)
Async XLA Ops:
  7.2 243.4 %copy-start = (bf16[4096,8]{0,1:T(8,128)(2,1)S(1)}, bf16[4096,8]{0,1:T(8,128)(2,1)}, u32[]{:S(2)}) copy-start(bf16[4096,8]{0,1:T(8,128)(2,1)} %param.29) | copy-start | bytes 196612
  7.2 66.6 %all-gather.3.cloned.1.call-start = ((), (), s32[]{:S(2)}) async-start(), calls=%async_computation.3 | async-start | bytes 8650752 | tf_op jit(solution)/shard_map/all_gather | solution.py:342
  7.9 14.6 %collective-permute-start.1 = (bf16[4096,384]{1,0:T(8,128)(2,1)}, bf16[4096,384]{1,0:T(8,128)(2,1)}, u32[]{:S(2)}, u32[]{:S(2)}) collective-permute-start(bf16[4096,384]{1,0:T(8,128)(2,1)} %bitcast.218), channel_id=1, source_target_pairs={{0,8},{8,0},{16,24},{24,16},{32,40},{40,32},{48,56},{56,48},{64,72... | collective-permute-start | bytes 9437192 | tf_op jit(solution)/shard_map/ppermute | solution.py:35
  8.0 14.5 %collective-permute-start.2 = (bf16[4096,384]{1,0:T(8,128)(2,1)}, bf16[4096,384]{1,0:T(8,128)(2,1)}, u32[]{:S(2)}, u32[]{:S(2)}) collective-permute-start(bf16[4096,384]{1,0:T(8,128)(2,1)} %bitcast.220), channel_id=1, source_target_pairs={{0,8},{8,0},{16,24},{24,16},{32,40},{40,32},{48,56},{56,48},{64,72... | collective-permute-start | bytes 9437192 | tf_op jit(solution)/shard_map/ppermute | solution.py:35
  8.5 14.5 %collective-permute-start.3 = (bf16[384,4096]{1,0:T(8,128)(2,1)}, bf16[384,4096]{1,0:T(8,128)(2,1)}, u32[]{:S(2)}, u32[]{:S(2)}) collective-permute-start(bf16[384,4096]{1,0:T(8,128)(2,1)} %bitcast.222), channel_id=1, source_target_pairs={{0,8},{8,0},{16,24},{24,16},{32,40},{40,32},{48,56},{56,48},{64,72... | collective-permute-start | bytes 9437192 | tf_op jit(solution)/shard_map/ppermute | solution.py:35
  9.3 5.2 %collective-permute-start = (bf16[3,1024]{1,0:T(4,128)(2,1)S(1)}, bf16[3,1024]{1,0:T(4,128)(2,1)S(1)}, u32[]{:S(2)}, u32[]{:S(2)}) collective-permute-start(bf16[3,1024]{1,0:T(4,128)(2,1)S(1)} %slice.126), channel_id=1, source_target_pairs={{0,8},{8,16},{16,24},{24,32},{32,40},{40,48},{48,56},{56,64},{64,7... | collective-permute-start | bytes 18440 | tf_op jit(solution)/shard_map/ppermute | solution.py:225
  14.6 0.6 copy-start.9
  22.4 23.7 %copy-start.1 = (f32[128,128]{1,0:T(8,128)S(1)}, f32[128,128]{1,0:T(8,128)}, u32[]{:S(2)}) copy-start(f32[128,128]{1,0:T(8,128)} %get-tuple-element.22.scaled_ref) | copy-start | bytes 196612
  22.4 23.8 %copy-start.2 = (f32[2048]{0:T(1024)S(1)}, f32[2048]{0:T(1024)}, u32[]{:S(2)}) copy-start(f32[2048]{0:T(1024)} %reshape.180.out_ref) | copy-start | bytes 24580
  22.4 23.8 %copy-start.3 = (bf16[128,1024]{1,0:T(8,128)(2,1)S(1)}, bf16[128,1024]{1,0:T(8,128)(2,1)}, u32[]{:S(2)}) copy-start(bf16[128,1024]{1,0:T(8,128)(2,1)} %gate_hbm.1) | copy-start | bytes 786436
  22.4 23.8 %copy-start.4 = (f32[1024,128]{1,0:T(8,128)S(1)}, f32[1024,128]{1,0:T(8,128)}, u32[]{:S(2)}) copy-start(f32[1024,128]{1,0:T(8,128)} %get-tuple-element.18.y_ref) | copy-start | bytes 1572868
  22.5 23.8 %copy-start.5 = (f32[1024,128]{1,0:T(8,128)S(1)}, f32[1024,128]{1,0:T(8,128)}, u32[]{:S(2)}) copy-start(f32[1024,128]{1,0:T(8,128)} %get-tuple-element.19.sums_ref) | copy-start | bytes 1572868
  23.0 1.9 collective-permute-start.4
  26.5 8.4 %collective-permute-start.7 = (f32[136,128]{1,0:T(8,128)S(1)}, f32[136,128]{1,0:T(8,128)S(1)}, u32[]{:S(2)}, u32[]{:S(2)}) collective-permute-start(f32[136,128]{1,0:T(8,128)S(1)} %maximum_bitcast_fusion), channel_id=1, source_target_pairs={{0,48},{8,56},{16,0},{24,8},{32,16},{40,24},{48,32},{56,40},{64,11... | collective-permute-start | bytes 208904 | tf_op jit(solution)/shard_map/ppermute | solution.py:35
  27.1 7.8 %collective-permute-start.6 = (f32[136,128]{1,0:T(8,128)S(1)}, f32[136,128]{1,0:T(8,128)S(1)}, u32[]{:S(2)}, u32[]{:S(2)}) collective-permute-start(f32[136,128]{1,0:T(8,128)S(1)} %maximum_bitcast_fusion), channel_id=1, source_target_pairs={{0,32},{8,40},{16,48},{24,56},{32,0},{40,8},{48,16},{56,24},{64,96... | collective-permute-start | bytes 208904 | tf_op jit(solution)/shard_map/ppermute | solution.py:35
  29.9 6.0 %collective-permute-start.5 = (f32[136,128]{1,0:T(8,128)S(1)}, f32[136,128]{1,0:T(8,128)S(1)}, u32[]{:S(2)}, u32[]{:S(2)}) collective-permute-start(f32[136,128]{1,0:T(8,128)S(1)} %maximum_bitcast_fusion), channel_id=1, source_target_pairs={{0,16},{8,24},{16,32},{24,40},{32,48},{40,56},{48,0},{56,8},{64,80... | collective-permute-start | bytes 208904 | tf_op jit(solution)/shard_map/ppermute | solution.py:35
  36.9 5.6 %collective-permute-start.8 = (f32[136,128]{1,0:T(8,128)S(1)}, f32[136,128]{1,0:T(8,128)S(1)}, u32[]{:S(2)}, u32[]{:S(2)}) collective-permute-start(f32[136,128]{1,0:T(8,128)S(1)} %maximum_bitcast_fusion.1), channel_id=1, source_target_pairs={{0,64},{8,72},{16,80},{24,88},{32,96},{40,104},{48,112},{56,120},{... | collective-permute-start | bytes 208904 | tf_op jit(solution)/shard_map/ppermute | solution.py:35
  38.8 7.3 %collective-permute-start.10 = (f32[136,128]{1,0:T(8,128)S(1)}, f32[136,128]{1,0:T(8,128)S(1)}, u32[]{:S(2)}, u32[]{:S(2)}) collective-permute-start(f32[136,128]{1,0:T(8,128)S(1)} %maximum_bitcast_fusion.1), channel_id=1, source_target_pairs={{0,192},{8,200},{16,208},{24,216},{32,224},{40,232},{48,240},{56,2... | collective-permute-start | bytes 208904 | tf_op jit(solution)/shard_map/ppermute | solution.py:35
  40.2 5.8 %collective-permute-start.9 = (f32[136,128]{1,0:T(8,128)S(1)}, f32[136,128]{1,0:T(8,128)S(1)}, u32[]{:S(2)}, u32[]{:S(2)}) collective-permute-start(f32[136,128]{1,0:T(8,128)S(1)} %maximum_bitcast_fusion.1), channel_id=1, source_target_pairs={{0,128},{8,136},{16,144},{24,152},{32,160},{40,168},{48,176},{56,1... | collective-permute-start | bytes 208904 | tf_op jit(solution)/shard_map/ppermute | solution.py:35
  81.7 7.2 %copy-start.8 = (s32[16,2]{0,1:T(2,128)S(1)}, s32[16,2]{0,1:T(2,128)}, u32[]{:S(2)}) copy-start(s32[16,2]{0,1:T(2,128)} %param.30) | copy-start | bytes 388
  81.7 36.4 %copy-start.6 = (bf16[16,4096]{1,0:T(8,128)(2,1)S(1)}, bf16[16,4096]{1,0:T(8,128)(2,1)}, u32[]{:S(2)}) copy-start(bf16[16,4096]{1,0:T(8,128)(2,1)} %param.27) | copy-start | bytes 393220
  81.7 36.7 %copy-start.7 = (f32[4096]{0:T(1024)S(1)}, f32[4096]{0:T(1024)}, u32[]{:S(2)}) copy-start(f32[4096]{0:T(1024)} %param.28) | copy-start | bytes 49156
  81.7 36.4 %all-to-all-start = ((bf16[8,16,4096]{2,1,0:T(8,128)(2,1)}), bf16[8,16,4096]{2,1,0:T(8,128)(2,1)S(1)}, u32[]{:S(2)}, u32[]{:S(2)}) async-start(bf16[8,16,4096]{2,1,0:T(8,128)(2,1)} %project.1), calls=%async_computation | async-start | bytes 2097152 | tf_op jit(solution)/shard_map/all_to_all | solution.py:361
  135.4 8.4 %collective-permute-start.15 = (bf16[40,4096]{1,0:T(8,128)(2,1)S(1)}, bf16[40,4096]{1,0:T(8,128)(2,1)S(1)}, u32[]{:S(2)}, u32[]{:S(2)}) collective-permute-start(bf16[40,4096]{1,0:T(8,128)(2,1)S(1)} %reshape.174), channel_id=1, source_target_pairs={{0,48},{8,200},{16,0},{24,216},{32,16},{40,232},{48,32},{56,248},{... | collective-permute-start | bytes 983048 | tf_op jit(solution)/shard_map/ppermute | solution.py:235
  136.3 7.7 %collective-permute-start.11 = (bf16[40,4096]{1,0:T(8,128)(2,1)S(1)}, bf16[40,4096]{1,0:T(8,128)(2,1)S(1)}, u32[]{:S(2)}, u32[]{:S(2)}) collective-permute-start(bf16[40,4096]{1,0:T(8,128)(2,1)S(1)} %reshape.174), channel_id=1, source_target_pairs={{0,16},{8,72},{16,32},{24,88},{32,48},{40,104},{48,0},{56,120},{64... | collective-permute-start | bytes 983048 | tf_op jit(solution)/shard_map/ppermute | solution.py:235
  143.8 6.8 %collective-permute-start.16 = (bf16[40,2048]{1,0:T(8,128)(2,1)S(1)}, bf16[40,2048]{1,0:T(8,128)(2,1)S(1)}, u32[]{:S(2)}, u32[]{:S(2)}) collective-permute-start(bf16[40,2048]{1,0:T(8,128)(2,1)S(1)} %slice.185), channel_id=1, source_target_pairs={{0,48},{8,200},{16,0},{24,216},{32,16},{40,232},{48,32},{56,248},{... | collective-permute-start | bytes 491528 | tf_op jit(solution)/shard_map/ppermute | solution.py:235
  144.1 7.9 %collective-permute-start.14 = (bf16[40,2048]{1,0:T(8,128)(2,1)S(1)}, bf16[40,2048]{1,0:T(8,128)(2,1)S(1)}, u32[]{:S(2)}, u32[]{:S(2)}) collective-permute-start(bf16[40,2048]{1,0:T(8,128)(2,1)S(1)} %slice.184), channel_id=1, source_target_pairs={{0,16},{8,72},{16,32},{24,88},{32,48},{40,104},{48,0},{56,120},{64... | collective-permute-start | bytes 491528 | tf_op jit(solution)/shard_map/ppermute | solution.py:235
  147.4 11.9 %collective-permute-start.12 = (bf16[80,4096]{1,0:T(8,128)(2,1)S(1)}, bf16[80,4096]{1,0:T(8,128)(2,1)S(1)}, u32[]{:S(2)}, u32[]{:S(2)}) collective-permute-start(bf16[80,4096]{1,0:T(8,128)(2,1)S(1)} %constant_dynamic-update-slice_fusion.refs_2_), channel_id=1, source_target_pairs={{0,64},{8,24},{16,80},{24,40},{32,96},{40,56},{48,112},{56,8},{64,... | collective-permute-start | bytes 1966088 | tf_op jit(solution)/shard_map/ppermute | solution.py:235
  152.1 10.7 %collective-permute-start.17 = (bf16[80,4096]{1,0:T(8,128)(2,1)S(1)}, bf16[80,4096]{1,0:T(8,128)(2,1)S(1)}, u32[]{:S(2)}, u32[]{:S(2)}) collective-permute-start(bf16[80,4096]{1,0:T(8,128)(2,1)S(1)} %pad_maximum_fusion.refs_3_), channel_id=1, source_target_pairs={{0,192},{8,56},{16,208},{24,8},{32,224},{40,24},{48,240},{56,40},{... | collective-permute-start | bytes 1966088 | tf_op jit(solution)/shard_map/ppermute | solution.py:235
  152.9 16.9 %collective-permute-start.19 = (bf16[80,4096]{1,0:T(8,128)(2,1)S(1)}, bf16[80,4096]{1,0:T(8,128)(2,1)S(1)}, u32[]{:S(2)}, u32[]{:S(2)}) collective-permute-start(bf16[80,4096]{1,0:T(8,128)(2,1)S(1)} %constant_dynamic-update-slice_fusion.refs_2_), channel_id=1, source_target_pairs={{0,192},{8,56},{16,208},{24,8},{32,224},{40,24},{48,240},{56,40},{... | collective-permute-start | bytes 1966088 | tf_op jit(solution)/shard_map/ppermute | solution.py:235
  154.1 15.7 %collective-permute-start.20 = (bf16[80,4096]{1,0:T(8,128)(2,1)S(1)}, bf16[80,4096]{1,0:T(8,128)(2,1)S(1)}, u32[]{:S(2)}, u32[]{:S(2)}) collective-permute-start(bf16[80,4096]{1,0:T(8,128)(2,1)S(1)} %pad_maximum_fusion.refs_3_), channel_id=1, source_target_pairs={{0,64},{8,24},{16,80},{24,40},{32,96},{40,56},{48,112},{56,8},{64,... | collective-permute-start | bytes 1966088 | tf_op jit(solution)/shard_map/ppermute | solution.py:235
  159.3 14.0 %collective-permute-start.13 = (bf16[80,4096]{1,0:T(8,128)(2,1)S(1)}, bf16[80,4096]{1,0:T(8,128)(2,1)S(1)}, u32[]{:S(2)}, u32[]{:S(2)}) collective-permute-start(bf16[80,4096]{1,0:T(8,128)(2,1)S(1)} %collective-permute-done.12.refs_4_), channel_id=1, source_target_pairs={{0,64},{8,24},{16,80},{24,40},{32,96},{40,56},{48,112},{56,8},{64,... | collective-permute-start | bytes 1966088 | tf_op jit(solution)/shard_map/ppermute | solution.py:235
  162.7 14.0 %collective-permute-start.18 = (bf16[80,4096]{1,0:T(8,128)(2,1)S(1)}, bf16[80,4096]{1,0:T(8,128)(2,1)S(1)}, u32[]{:S(2)}, u32[]{:S(2)}) collective-permute-start(bf16[80,4096]{1,0:T(8,128)(2,1)S(1)} %collective-permute-done.17.refs_5_), channel_id=1, source_target_pairs={{0,192},{8,56},{16,208},{24,8},{32,224},{40,24},{48,240},{56,40},{... | collective-permute-start | bytes 1966088 | tf_op jit(solution)/shard_map/ppermute | solution.py:235
  196.1 11.9 %collective-permute-start.22 = (bf16[80,4096]{1,0:T(8,128)(2,1)S(1)}, bf16[80,4096]{1,0:T(8,128)(2,1)S(1)}, u32[]{:S(2)}, u32[]{:S(2)}) collective-permute-start(bf16[80,4096]{1,0:T(8,128)(2,1)S(1)} %get-tuple-element.29), channel_id=1, source_target_pairs={{0,64},{8,24},{16,80},{24,40},{32,96},{40,56},{48,112},{56,8},{64,... | collective-permute-start | bytes 1966088 | tf_op jit(solution)/shard_map/ppermute | solution.py:235
  196.3 22.4 %collective-permute-start.21 = (bf16[80,4096]{1,0:T(8,128)(2,1)S(1)}, bf16[80,4096]{1,0:T(8,128)(2,1)S(1)}, u32[]{:S(2)}, u32[]{:S(2)}) collective-permute-start(bf16[80,4096]{1,0:T(8,128)(2,1)S(1)} %get-tuple-element.27), channel_id=1, source_target_pairs={{0,192},{8,56},{16,208},{24,8},{32,224},{40,24},{48,240},{56,40},{... | collective-permute-start | bytes 1966088 | tf_op jit(solution)/shard_map/ppermute | solution.py:235
  199.4 23.0 %collective-permute-start.25 = (bf16[80,4096]{1,0:T(8,128)(2,1)S(1)}, bf16[80,4096]{1,0:T(8,128)(2,1)S(1)}, u32[]{:S(2)}, u32[]{:S(2)}) collective-permute-start(bf16[80,4096]{1,0:T(8,128)(2,1)S(1)} %get-tuple-element.31), channel_id=1, source_target_pairs={{0,64},{8,24},{16,80},{24,40},{32,96},{40,56},{48,112},{56,8},{64,... | collective-permute-start | bytes 1966088 | tf_op jit(solution)/shard_map/ppermute | solution.py:235
  199.4 15.1 %collective-permute-start.26 = (bf16[80,4096]{1,0:T(8,128)(2,1)S(1)}, bf16[80,4096]{1,0:T(8,128)(2,1)S(1)}, u32[]{:S(2)}, u32[]{:S(2)}) collective-permute-start(bf16[80,4096]{1,0:T(8,128)(2,1)S(1)} %get-tuple-element.33), channel_id=1, source_target_pairs={{0,192},{8,56},{16,208},{24,8},{32,224},{40,24},{48,240},{56,40},{... | collective-permute-start | bytes 1966088 | tf_op jit(solution)/shard_map/ppermute | solution.py:235
  208.2 13.9 %collective-permute-start.23 = (bf16[80,4096]{1,0:T(8,128)(2,1)S(1)}, bf16[80,4096]{1,0:T(8,128)(2,1)S(1)}, u32[]{:S(2)}, u32[]{:S(2)}) collective-permute-start(bf16[80,4096]{1,0:T(8,128)(2,1)S(1)} %add_convert_fusion.2), channel_id=1, source_target_pairs={{0,64},{8,24},{16,80},{24,40},{32,96},{40,56},{48,112},{56,8},{64,... | collective-permute-start | bytes 1966088 | tf_op jit(solution)/shard_map/ppermute | solution.py:235
  214.7 16.9 %collective-permute-start.27 = (bf16[80,4096]{1,0:T(8,128)(2,1)S(1)}, bf16[80,4096]{1,0:T(8,128)(2,1)S(1)}, u32[]{:S(2)}, u32[]{:S(2)}) collective-permute-start(bf16[80,4096]{1,0:T(8,128)(2,1)S(1)} %add_convert_fusion.1), channel_id=1, source_target_pairs={{0,192},{8,56},{16,208},{24,8},{32,224},{40,24},{48,240},{56,40},{... | collective-permute-start | bytes 1966088 | tf_op jit(solution)/shard_map/ppermute | solution.py:235
  222.3 14.3 %collective-permute-start.24 = (bf16[40,4096]{1,0:T(8,128)(2,1)S(1)}, bf16[40,4096]{1,0:T(8,128)(2,1)S(1)}, u32[]{:S(2)}, u32[]{:S(2)}) collective-permute-start(bf16[40,4096]{1,0:T(8,128)(2,1)S(1)} %slice.275), channel_id=1, source_target_pairs={{0,48},{8,200},{16,0},{24,216},{32,16},{40,232},{48,32},{56,248},{... | collective-permute-start | bytes 983048 | tf_op jit(solution)/shard_map/ppermute | solution.py:235
  231.9 8.7 %collective-permute-start.28 = (bf16[40,4096]{1,0:T(8,128)(2,1)S(1)}, bf16[40,4096]{1,0:T(8,128)(2,1)S(1)}, u32[]{:S(2)}, u32[]{:S(2)}) collective-permute-start(bf16[40,4096]{1,0:T(8,128)(2,1)S(1)} %get-tuple-element.49), channel_id=1, source_target_pairs={{0,32},{8,136},{16,48},{24,152},{32,0},{40,168},{48,16},{56,184},{... | collective-permute-start | bytes 983048 | tf_op jit(solution)/shard_map/ppermute | solution.py:235
  234.9 11.1 %collective-permute-start.29 = (bf16[40,4096]{1,0:T(8,128)(2,1)S(1)}, bf16[40,4096]{1,0:T(8,128)(2,1)S(1)}, u32[]{:S(2)}, u32[]{:S(2)}) collective-permute-start(bf16[40,4096]{1,0:T(8,128)(2,1)S(1)} %get-tuple-element.50), channel_id=1, source_target_pairs={{0,16},{8,72},{16,32},{24,88},{32,48},{40,104},{48,0},{56,120},{64... | collective-permute-start | bytes 983048 | tf_op jit(solution)/shard_map/ppermute | solution.py:235
  247.0 14.5 %all-to-all-start.2 = ((bf16[8,160,128]{2,1,0:T(8,128)(2,1)}), bf16[8,160,128]{2,1,0:T(8,128)(2,1)S(1)}, u32[]{:S(2)}, u32[]{:S(2)}) async-start(bf16[8,160,128]{2,1,0:T(8,128)(2,1)} %reshape.175), calls=%async_computation.2 | async-start | bytes 655360 | tf_op jit(solution)/shard_map/all_to_all | solution.py:431
Sparse Core Ops, SparseCore 0:
  10.6 63.1 all-gather.2

commit v6 on v5

--- a/solution.py
+++ b/solution.py
@@ -239,62 +239,80 @@
     return sum(t.astype(jnp.float32) for t in terms)
 
 
-def expert_kernel(steps, *refs):
-    count = (len(refs) - 8) // 2
-    pieces, outs = refs[:count], refs[count + 6 : -2]
-    gate_a, gate_b, up_a, up_b, down_a, down_b = refs[count : count + 6]
-    rows_ref, acts_ref = refs[-2:]
+def expert_in_kernel(*refs):
+    pieces, (gate_a, gate_b, up_a, up_b, act_a, act_b, rows_ref) = refs[:-7], refs[-7:]
     rows = pieces[0].shape[0]
-    half = acts_ref.shape[1] // 2
-    i = pl.program_id(0)
-
-    @pl.when(i == 0)
+
+    @pl.when(pl.program_id(0) == 0)
     def _():
         for k, piece in enumerate(pieces):
             rows_ref[k * rows : (k + 1) * rows, :] = piece[...]
 
-    @pl.when(i < steps)
-    def _():
-        for begin, gate, up in ((0, gate_a, up_a), (half, gate_b, up_b)):
-            both = jnp.concatenate([gate[...], up[...]], axis=1)
-            hidden = jnp.dot(rows_ref[...], both, preferred_element_type=jnp.float32)
-            gating, upward = hidden[:, :LANES], hidden[:, LANES:]
-            act = (gating * jax.nn.sigmoid(gating) * upward).astype(acts_ref.dtype)
-            acts_ref[:, pl.ds(pl.multiple_of(begin + i * LANES, LANES), LANES)] = act
-
-    @pl.when(i >= steps)
-    def _():
-        down = jnp.concatenate([down_a[...], down_b[...]], axis=0)
-        result = jnp.dot(acts_ref[...], down, preferred_element_type=jnp.float32)
-        for k, out in enumerate(outs):
-            out[...] = result[k * rows : (k + 1) * rows].astype(out.dtype)
-
-
-def expert(pieces, here, there):
+    for gate, up, act in ((gate_a, up_a, act_a), (gate_b, up_b, act_b)):
+        both = jnp.concatenate([gate[...], up[...]], axis=1)
+        hidden = jnp.dot(rows_ref[...], both, preferred_element_type=jnp.float32)
+        gating, upward = hidden[:, :LANES], hidden[:, LANES:]
+        act[...] = (gating * jax.nn.sigmoid(gating) * upward).astype(act.dtype)
+
+
+def expert_in(pieces, here, there):
     rows, width = pieces[0].shape
     count = len(pieces) * rows
     hidden = here[0].shape[1]
-    steps = hidden // LANES
-    tile = 4 * LANES
-    into = pl.BlockSpec((width, LANES), lambda i: (0, jnp.minimum(i, steps - 1)))
-    back = pl.BlockSpec((hidden, tile), lambda i: (0, jnp.maximum(i - steps, 0)))
-    piece = pl.BlockSpec((rows, tile), lambda i: (0, jnp.maximum(i - steps, 0)))
+    weight = pl.BlockSpec((width, LANES), lambda i: (0, i))
+    act = pl.BlockSpec((count, LANES), lambda i: (0, i))
     return pl.pallas_call(
-        functools.partial(expert_kernel, steps),
-        name="expert",
-        grid=(steps + width // tile,),
-        out_shape=(jax.ShapeDtypeStruct((rows, width), jnp.bfloat16),) * len(pieces),
-        in_specs=[VMEM] * len(pieces) + [into] * 4 + [back] * 2,
-        out_specs=(piece,) * len(pieces),
-        scratch_shapes=[
-            pltpu.VMEM((count, width), jnp.bfloat16),
-            pltpu.VMEM((count, 2 * hidden), jnp.bfloat16),
-        ],
+        expert_in_kernel,
+        name="expert_in",
+        grid=(hidden // LANES,),
+        out_shape=(jax.ShapeDtypeStruct((count, hidden), jnp.bfloat16),) * 2,
+        in_specs=[VMEM] * len(pieces) + [weight] * 4,
+        out_specs=(act, act),
+        scratch_shapes=[pltpu.VMEM((count, width), jnp.bfloat16)],
         compiler_params=pltpu.CompilerParams(vmem_limit_bytes=42 << 20),
         cost_estimate=pl.CostEstimate(
-            flops=12 * count * width * hidden, transcendentals=2 * count * hidden, bytes_accessed=24_000_000
+            flops=8 * count * width * hidden, transcendentals=2 * count * hidden, bytes_accessed=16_000_000
         ),
-    )(*pieces, here[0], there[0], here[1], there[1], here[2], there[2])
+    )(*pieces, here[0], there[0], here[1], there[1])
+
+
+def expert_out_kernel(places, rows, *refs):
+    acts, (down_a, down_b) = refs[:4], refs[4:6]
+    outs, acts_ref = refs[6:-1], refs[-1]
+    hidden = down_a.shape[0]
+
+    @pl.when(pl.program_id(0) == 0)
+    def _():
+        for k, (part, begin) in enumerate(places):
+            for side in range(2):
+                block = acts[2 * part + side][begin * rows : (begin + 1) * rows, :]
+                acts_ref[k * rows : (k + 1) * rows, side * hidden : (side + 1) * hidden] = block
+
+    down = jnp.concatenate([down_a[...], down_b[...]], axis=0)
+    result = jnp.dot(acts_ref[...], down, preferred_element_type=jnp.float32)
+    for k, out in enumerate(outs):
+        out[...] = result[k * rows : (k + 1) * rows].astype(out.dtype)
+
+
+def expert_out(places, rows, acts, here, there):
+    hidden, width = here[2].shape
+    count = len(places) * rows
+    tile = 8 * LANES
+    weight = pl.BlockSpec((hidden, tile), lambda i: (0, i))
+    piece = pl.BlockSpec((rows, tile), lambda i: (0, i))
+    return pl.pallas_call(
+        functools.partial(expert_out_kernel, places, rows),
+        name="expert_out",
+        grid=(width // tile,),
+        out_shape=(jax.ShapeDtypeStruct((rows, width), jnp.bfloat16),) * len(places),
+        in_specs=[VMEM] * 4 + [weight] * 2,
+        out_specs=(piece,) * len(places),
+        scratch_shapes=[pltpu.VMEM((count, 2 * hidden), jnp.bfloat16)],
+        compiler_params=pltpu.CompilerParams(vmem_limit_bytes=42 << 20),
+        cost_estimate=pl.CostEstimate(
+            flops=4 * count * width * hidden, transcendentals=0, bytes_accessed=9_000_000
+        ),
+    )(*acts, here[2], there[2])
 
 
 def experts_of_rows(block, here, there):
@@ -312,11 +330,13 @@
     low_down = around(low, "outer", -1)
     low_far = around(low_up, "outer", 1)
     high_far = around(high_down, "outer", -1)
-    low_far, high_far, low, high, low_up, high_down, low_down, high_up = expert(
-        [low_far, high_far, low, high, low_up, high_down, low_down, high_up], here, there
-    )
+    acts = expert_in([low, high, low_up, high_down], here, there)
+    acts = [*acts, *expert_in([low_far, high_far, low_down, high_up], here, there)]
+    rows = low.shape[0]
+    low_far, high_far, low_up, high_down = expert_out(((1, 0), (1, 1), (0, 2), (0, 3)), rows, acts, here, there)
     got_high_down = around(high_down, "outer", 1)
     got_low_up = around(low_up, "outer", -1)
+    low, high, low_down, high_up = expert_out(((0, 0), (0, 1), (1, 2), (1, 3)), rows, acts, here, there)
     low_relay = around(low_far, "outer", 1)
     high_relay = around(high_far, "outer", -1)
     got_low_down = around(added(low_down, low_relay).astype(dtype), "outer", 1)
@@ -403,22 +423,23 @@
     mixed = finish_scan(y, sums, start, scaled, gate_input, out_flat)
     rows = residual.shape[0]
     model_width = residual.shape[1]
-    projected = project(mixed, out_weight)
-    hidden_state = residual.astype(jnp.float32) + projected
-    scale = lax.rsqrt(jnp.mean(hidden_state * hidden_state, axis=1, keepdims=True) + 1e-06)
-    normed = (hidden_state * scale * norm_gain[None, :]).astype(jnp.bfloat16)
     experts = router_weight.shape[1]
     capacity = 2 * rows // experts + 1
-    logits = jnp.dot(normed, router_weight, preferred_element_type=jnp.float32)
     expert_range = jnp.arange(experts, dtype=jnp.int32)
-    matches = expert_ids[:, :, None] == expert_range[None, None, :]
-    chosen = jnp.sum(jnp.where(matches, logits[:, None, :], 0.0), axis=2)
-    first = jax.nn.sigmoid(chosen[:, 0] - chosen[:, 1])
     flat_ids = expert_ids.reshape(-1)
     position = jnp.arange(flat_ids.shape[0], dtype=jnp.int32)
     earlier = (flat_ids[:, None] == flat_ids[None, :]) & (position[None, :] < position[:, None])
     rank = jnp.sum(earlier.astype(jnp.int32), axis=1)
     target = flat_ids * capacity + rank
+    mixed, target = lax.optimization_barrier((mixed, target))
+    projected = project(mixed, out_weight)
+    hidden_state = residual.astype(jnp.float32) + projected
+    scale = lax.rsqrt(jnp.mean(hidden_state * hidden_state, axis=1, keepdims=True) + 1e-06)
+    normed = (hidden_state * scale * norm_gain[None, :]).astype(jnp.bfloat16)
+    logits = jnp.dot(normed, router_weight, preferred_element_type=jnp.float32)
+    matches = expert_ids[:, :, None] == expert_range[None, None, :]
+    chosen = jnp.sum(jnp.where(matches, logits[:, None, :], 0.0), axis=2)
+    first = jax.nn.sigmoid(chosen[:, 0] - chosen[:, 1])
     placing = (jnp.arange(experts * capacity, dtype=jnp.int32)[:, None] == target[None, :]).astype(
         jnp.bfloat16
     )

time: 271 us -> 270 us (level)
  waiting for transfers between devices: 138 us -> 87.1 us
  blocking collectives: 16.1 us -> 53.7 us
  local copies, waits for them, and re-layouts: 6.24 us -> 17.8 us
  starting transfers between devices: 51.1 us -> 40.3 us
  other arithmetic: 5.17 us -> 10.3 us
  Pallas kernels: 38.3 us -> 42.7 us
    all_to_all x0 -> x1, blocking collectives: none -> 36.3 us  [project(): terms = lax.all_to_all(terms, 'exp', 0, 0, tiled=True)]
    all_to_all x1 -> x0, waiting for transfers between devices: 28.8 us -> none  [project(): terms = lax.all_to_all(terms, 'exp', 0, 0, tiled=True)]
    ppermute x19, waiting for transfers between devices: 62.9 us -> 51.7 us  [around(): return lax.ppermute(block, 'seq', route)]
    all_gather x1, waiting for transfers between devices: 23.7 us -> 15 us  [project(): blocks = lax.all_gather(weight, 'seq')]
    all_to_all x1 -> x0, starting transfers between devices: 7.15 us -> none  [project(): terms = lax.all_to_all(terms, 'exp', 0, 0, tiled=True)]
    unnamed x22 -> x38, local copies, waits for them, and re-layouts: 0.75 us -> 5.91 us
    pallas_call x1 -> x4, Pallas kernels: 19.3 us -> 23.8 us  [the longest x2 14.3 us: expert_in(): pl.pallas_call(expert_in_kernel, name='expert_in', grid=(hidden // LANES,...]
    ppermute x19, starting transfers between devices: 27.2 us -> 24.2 us  [around(): return lax.ppermute(block, 'seq', route)]
  transfers between devices with their start and end apart: 33 -> 32, of which waited for: 24 -> 20; matrix products, arithmetic and copies ran while one was open for 3% -> 6% of each run, Pallas kernels for 4% -> 9%
where the time goes in v6:
time: 270 us; the launch traced here: 269 us
  waiting for transfers between devices  87.1 us (32%)
  blocking collectives  53.7 us (20%)
  Pallas kernels  42.7 us (16%)
  starting transfers between devices  40.3 us (15%)
  local copies, waits for them, and re-layouts  17.8 us (7%)
  between operations  14.5 us (5%)
  other arithmetic  10.3 us (4%)
    ppermute x19, waiting for transfers between devices, around(): return lax.ppermute(block, 'seq', route)  51.7 us
    all_to_all x1, blocking collectives, project(): terms = lax.all_to_all(terms, 'exp', 0, 0, tiled=True)  36.3 us
    ppermute x19, starting transfers between devices, around(): return lax.ppermute(block, 'seq', route)  24.2 us
    all_to_all x1, blocking collectives, shards(): lax.all_to_all(outgoing, 'exp', split_axis=0, concat_axis=0, tiled=True)  17.4 us
    all_gather x1, waiting for transfers between devices, project(): blocks = lax.all_gather(weight, 'seq')  15 us
    pallas_call x2, Pallas kernels, expert_in(): pl.pallas_call(expert_in_kernel, name='expert_in', grid=(hidden // LANES,...  14.3 us
    all_to_all x1, waiting for transfers between devices, shards(): lax.all_to_all(summed_out.reshape(arrived.shape), 'exp', split_axis=0, co...  10.8 us
    ppermute x10, starting transfers between devices, moved(): return lax.ppermute(block, 'seq', route)  10.3 us
  transfers between devices with their start and end apart: 32, of which 20 were waited for; matrix products, arithmetic and copies ran while one was open for 6% of the time, Pallas kernels for 9%

profile of v6, /device:TPU:6, one launch (start us, length us, event | category | flops | bytes accessed | tf_op | source)
XLA Modules:
  0.0 268.7 jit_solution(6190578213975791397)
XLA Ops:
  9.3 2.3 collective-permute-start
  15.2 7.3 %local_scan.1 = (f32[1024,128]{1,0:T(8,128)}, f32[1024,128]{1,0:T(8,128)}, f32[136,128]{1,0:T(8,128)}, f32[128,128]{1,0:T(8,128)}) custom-call(bf16[128,1024]{1,0:T(8,128)(2,1)} %inp_hbm.1, bf16[128,1024]{1,0:T(8,128)(2,1)} %raw_hbm.1, f32[16,1024]{1,0:T(8,128)} %rate_hbm.1, f32[4,1024]{1,0:T(4,128)} %taps_hbm.1, f32[1,1024]{1,0:T(1,128)} %bitcast.227, ...), custom_call_target="tpu_custom_call" | custom-call | flops 8000000 | bytes 2000000 | tf_op jit(solution)/shard_map/local_scan/pallas_call | solution.py:130
  26.9 1.7 collective-permute-start.5
  30.7 1.5 collective-permute-done.5
  32.2 3.7 %collective-permute-done.6 = f32[136,128]{1,0:T(8,128)S(1)} collective-permute-done((f32[136,128]{1,0:T(8,128)S(1)}, f32[136,128]{1,0:T(8,128)S(1)}, u32[]{:S(2)}, u32[]{:S(2)}) %collective-permute-start.6) | collective-permute-done | bytes 69664 | tf_op jit(solution)/shard_map/ppermute | solution.py:35
  36.0 1.3 collective-permute-done.7
  39.6 1.8 collective-permute-start.8
  41.4 1.2 multiply_add_fusion
  42.6 2.9 %collective-permute-start.9 = (f32[136,128]{1,0:T(8,128)}, f32[136,128]{1,0:T(8,128)S(1)}, u32[]{:S(2)}, u32[]{:S(2)}) collective-permute-start(f32[136,128]{1,0:T(8,128)} %maximum_bitcast_fusion.1), channel_id=1, source_target_pairs={{0,128},{8,136},{16,144},{24,152},{32,160},{40,168},{48,176},{56,1... | collective-permute-start | bytes 208904 | tf_op jit(solution)/shard_map/ppermute | solution.py:35
  45.5 1.3 collective-permute-start.10
  47.5 1.2 collective-permute-done.9
  50.0 1.2 fusion.9.start_ref
  53.4 3.8 %finish_scan.1.mixed_ref = bf16[128,1024]{1,0:T(8,128)(2,1)} custom-call(f32[1024,128]{1,0:T(8,128)S(1)} %copy-done.6, f32[1024,128]{1,0:T(8,128)S(1)} %copy-done.7, f32[128,128]{1,0:T(8,128)S(1)} %fusion.9.start_ref, f32[128,128]{1,0:T(8,128)S(1)} %copy-done.2, bf16[128,1024]{1,0:T(8,128)(2,1)S(1)} %copy-done.5, f32[2048]{0:T(1024)S(1)} %copy-done.3), custom_call_target="tpu_custom_call" | custom-call | flops 8000000 | bytes 2000000 | tf_op jit(solution)/shard_map/finish_scan/pallas_call | solution.py:155
  57.2 15.0 %all-gather.3.cloned.1.call-done = bf16[32768,128]{1,0:T(8,128)(2,1)} async-done(((bf16[1024,128]{1,0:T(8,128)(2,1)}), bf16[32768,128]{1,0:T(8,128)(2,1)}) %all-gather.3.cloned.1.call-update) | async-done | bytes 8388624 | tf_op jit(solution)/shard_map/all_gather | solution.py:362
  72.2 7.9 %project.1 = bf16[8,16,4096]{2,1,0:T(8,128)(2,1)} custom-call(bf16[128,1024]{1,0:T(8,128)(2,1)} %finish_scan.1.mixed_ref, bf16[32,1024,128]{2,1,0:T(8,128)(2,1)} %bitcast.218, bf16[32,1024,128]{2,1,0:T(8,128)(2,1)} %bitcast.219, bf16[32,1024,128]{2,1,0:T(8,128)(2,1)} %bitcast.220, bf16[32,1024,128]{2,1,0:T(8,128)(2,1)} %bitcast.221), custom_call_target="tpu_custom_call" | custom-call | flops 1073741824 | bytes 10000000 | tf_op jit(solution)/shard_map/project/pallas_call | solution.py:369
  80.0 36.3 %all_to_all.15 = bf16[8,16,4096]{2,1,0:T(8,128)(2,1)S(1)} all-to-all(bf16[8,16,4096]{2,1,0:T(8,128)(2,1)} %project.1), channel_id=1, replica_groups=mesh['seq'=32,'exp'=8] {'exp'}, dimensions={0} | all-to-all | bytes 2097152 | tf_op jit(solution)/shard_map/all_to_all | solution.py:381
  118.3 1.8 reshape.165
  120.1 1.9 convolution_convert_fusion
  122.0 1.9 reshape.166
  123.9 17.4 %all_to_all.16 = bf16[8,160,128]{2,1,0:T(8,128)(2,1)} all-to-all(bf16[8,160,128]{2,1,0:T(8,128)(2,1)} %reshape.166), channel_id=1, replica_groups=mesh['seq'=32,'exp'=8] {'exp'}, dimensions={0} | all-to-all | bytes 655360 | tf_op jit(solution)/shard_map/all_to_all | solution.py:449
  141.3 1.9 reshape.167
  143.7 1.5 collective-permute-start.13
  145.2 1.1 constant_dynamic-update-slice_fusion.1
  146.3 4.1 %collective-permute-done.11 = bf16[40,4096]{1,0:T(8,128)(2,1)S(1)} collective-permute-done((bf16[40,4096]{1,0:T(8,128)(2,1)}, bf16[40,4096]{1,0:T(8,128)(2,1)S(1)}, u32[]{:S(2)}, u32[]{:S(2)}) %collective-permute-start.11) | collective-permute-done | bytes 327712 | tf_op jit(solution)/shard_map/ppermute | solution.py:235
  150.4 2.0 collective-permute-start.12
  153.8 3.2 %collective-permute-done.12 = bf16[40,2048]{1,0:T(8,128)(2,1)S(1)} collective-permute-done((bf16[40,2048]{1,0:T(8,128)(2,1)S(1)}, bf16[40,2048]{1,0:T(8,128)(2,1)S(1)}, u32[]{:S(2)}, u32[]{:S(2)}) %collective-permute-start.12) | collective-permute-done | bytes 163872 | tf_op jit(solution)/shard_map/ppermute | solution.py:235
  157.0 2.2 collective-permute-done.14
  159.2 2.4 collective-permute-start.16
  161.6 1.8 collective-permute-start.19
  164.7 5.8 %collective-permute-done.16.refs_3_ = bf16[80,4096]{1,0:T(8,128)(2,1)S(1)} collective-permute-done((bf16[80,4096]{1,0:T(8,128)(2,1)S(1)}, bf16[80,4096]{1,0:T(8,128)(2,1)S(1)}, u32[]{:S(2)}, u32[]{:S(2)}) %collective-permute-start.16) | collective-permute-done | bytes 655392 | tf_op jit(solution)/shard_map/ppermute | solution.py:235
  170.5 2.8 %collective-permute-start.18 = (bf16[80,4096]{1,0:T(8,128)(2,1)S(1)}, bf16[80,4096]{1,0:T(8,128)(2,1)S(1)}, u32[]{:S(2)}, u32[]{:S(2)}) collective-permute-start(bf16[80,4096]{1,0:T(8,128)(2,1)S(1)} %collective-permute-done.16.refs_3_), channel_id=1, source_target_pairs={{0,192},{8,56},{16,208},{24,8},{32,224},{40,24},{48,240},{56,40},{... | collective-permute-start | bytes 1966088 | tf_op jit(solution)/shard_map/ppermute | solution.py:235
  173.4 7.2 %expert_in.2 = (bf16[320,384]{1,0:T(8,128)(2,1)S(1)}, bf16[320,384]{1,0:T(8,128)(2,1)S(1)}) custom-call(bf16[80,4096]{1,0:T(8,128)(2,1)S(1)} %constant_dynamic-update-slice_fusion.refs_0_, bf16[80,4096]{1,0:T(8,128)(2,1)S(1)} %pad_maximum_fusion.refs_1_, bf16[80,4096]{1,0:T(8,128)(2,1)S(1)} %collective-permute-done.15.refs_2_, ...), custom_call_target="tpu_custom_call" | custom-call | flops 4026531840 | bytes 16000000 | tf_op jit(solution)/shard_map/expert_in/pallas_call | solution.py:264
  180.6 1.6 collective-permute-done.17.refs_0_
  182.2 2.4 collective-permute-done.18.refs_1_
  184.6 7.2 %expert_in.3 = (bf16[320,384]{1,0:T(8,128)(2,1)S(1)}, bf16[320,384]{1,0:T(8,128)(2,1)S(1)}) custom-call(bf16[80,4096]{1,0:T(8,128)(2,1)S(1)} %collective-permute-done.17.refs_0_, bf16[80,4096]{1,0:T(8,128)(2,1)S(1)} %collective-permute-done.18.refs_1_, bf16[80,4096]{1,0:T(8,128)(2,1)S(1)} %collective-permute-done.19.refs_2_, ...), custom_call_target="tpu_custom_call" | custom-call | flops 4026531840 | bytes 16000000 | tf_op jit(solution)/shard_map/expert_in/pallas_call | solution.py:264
  191.8 4.7 %expert_out.3 = (bf16[80,4096]{1,0:T(8,128)(2,1)S(1)}, bf16[80,4096]{1,0:T(8,128)(2,1)S(1)}, bf16[80,4096]{1,0:T(8,128)(2,1)S(1)}, bf16[80,4096]{1,0:T(8,128)(2,1)S(1)}) custom-call(bf16[320,384]{1,0:T(8,128)(2,1)S(1)} %get-tuple-element.33.refs_0_, bf16[320,384]{1,0:T(8,128)(2,1)S(1)} %get-tuple-element.34.refs_1_, ...), custom_call_target="tpu_custom_call" | custom-call | flops 2013265920 | bytes 9000000 | tf_op jit(solution)/shard_map/expert_out/pallas_call | solution.py:303
  196.5 2.9 %collective-permute-start.26 = (bf16[80,4096]{1,0:T(8,128)(2,1)S(1)}, bf16[80,4096]{1,0:T(8,128)(2,1)S(1)}, u32[]{:S(2)}, u32[]{:S(2)}) collective-permute-start(bf16[80,4096]{1,0:T(8,128)(2,1)S(1)} %get-tuple-element.45), channel_id=1, source_target_pairs={{0,192},{8,56},{16,208},{24,8},{32,224},{40,24},{48,240},{56,40},{... | collective-permute-start | bytes 1966088 | tf_op jit(solution)/shard_map/ppermute | solution.py:235
  199.4 1.2 collective-permute-start.22
  200.6 2.0 collective-permute-start.21
  202.7 4.7 %expert_out.2 = (bf16[80,4096]{1,0:T(8,128)(2,1)S(1)}, bf16[80,4096]{1,0:T(8,128)(2,1)S(1)}, bf16[80,4096]{1,0:T(8,128)(2,1)S(1)}, bf16[80,4096]{1,0:T(8,128)(2,1)S(1)}) custom-call(bf16[320,384]{1,0:T(8,128)(2,1)S(1)} %get-tuple-element.33.refs_0_, bf16[320,384]{1,0:T(8,128)(2,1)S(1)} %get-tuple-element.34.refs_1_, ...), custom_call_target="tpu_custom_call" | custom-call | flops 2013265920 | bytes 9000000 | tf_op jit(solution)/shard_map/expert_out/pallas_call | solution.py:303
  207.7 3.8 %collective-permute-start.27 = (bf16[80,4096]{1,0:T(8,128)(2,1)S(1)}, bf16[80,4096]{1,0:T(8,128)(2,1)S(1)}, u32[]{:S(2)}, u32[]{:S(2)}) collective-permute-start(bf16[80,4096]{1,0:T(8,128)(2,1)S(1)} %add_convert_fusion.1), channel_id=1, source_target_pairs={{0,192},{8,56},{16,208},{24,8},{32,224},{40,24},{48,240},{56,40},{... | collective-permute-start | bytes 1966088 | tf_op jit(solution)/shard_map/ppermute | solution.py:235
  211.4 6.8 %collective-permute-done.22 = bf16[80,4096]{1,0:T(8,128)(2,1)S(1)} collective-permute-done((bf16[80,4096]{1,0:T(8,128)(2,1)S(1)}, bf16[80,4096]{1,0:T(8,128)(2,1)S(1)}, u32[]{:S(2)}, u32[]{:S(2)}) %collective-permute-start.22) | collective-permute-done | bytes 655392 | tf_op jit(solution)/shard_map/ppermute | solution.py:235
  218.5 6.9 %collective-permute-done.27 = bf16[80,4096]{1,0:T(8,128)(2,1)S(1)} collective-permute-done((bf16[80,4096]{1,0:T(8,128)(2,1)S(1)}, bf16[80,4096]{1,0:T(8,128)(2,1)S(1)}, u32[]{:S(2)}, u32[]{:S(2)}) %collective-permute-start.27) | collective-permute-done | bytes 655392 | tf_op jit(solution)/shard_map/ppermute | solution.py:235
  225.8 1.5 collective-permute-start.29
  227.3 9.2 %collective-permute-done.23 = bf16[80,4096]{1,0:T(8,128)(2,1)S(1)} collective-permute-done((bf16[80,4096]{1,0:T(8,128)(2,1)S(1)}, bf16[80,4096]{1,0:T(8,128)(2,1)S(1)}, u32[]{:S(2)}, u32[]{:S(2)}) %collective-permute-start.23) | collective-permute-done | bytes 655392 | tf_op jit(solution)/shard_map/ppermute | solution.py:235
  236.9 8.3 %collective-permute-done.24 = bf16[40,4096]{1,0:T(8,128)(2,1)S(1)} collective-permute-done((bf16[40,4096]{1,0:T(8,128)(2,1)S(1)}, bf16[40,4096]{1,0:T(8,128)(2,1)S(1)}, u32[]{:S(2)}, u32[]{:S(2)}) %collective-permute-start.24) | collective-permute-done | bytes 327712 | tf_op jit(solution)/shard_map/ppermute | solution.py:235
  246.2 3.4 %all-to-all-start.2 = ((bf16[8,160,128]{2,1,0:T(8,128)(2,1)}), bf16[8,160,128]{2,1,0:T(8,128)(2,1)S(1)}, u32[]{:S(2)}, u32[]{:S(2)}) async-start(bf16[8,160,128]{2,1,0:T(8,128)(2,1)} %reshape.168), calls=%async_computation.2 | async-start | bytes 655360 | tf_op jit(solution)/shard_map/all_to_all | solution.py:452
  249.9 10.8 %all-to-all-done.2 = bf16[8,160,128]{2,1,0:T(8,128)(2,1)S(1)} async-done(((bf16[8,160,128]{2,1,0:T(8,128)(2,1)}), bf16[8,160,128]{2,1,0:T(8,128)(2,1)S(1)}, u32[]{:S(2)}, u32[]{:S(2)}) %all-to-all-start.2) | async-done | bytes 327712 | tf_op jit(solution)/shard_map/all_to_all | solution.py:452
  (109 shorter events, 27.5 us)
Async XLA Ops:
  7.2 242.5 %copy-start = (bf16[4096,8]{0,1:T(8,128)(2,1)S(1)}, bf16[4096,8]{0,1:T(8,128)(2,1)}, u32[]{:S(2)}) copy-start(bf16[4096,8]{0,1:T(8,128)(2,1)} %param.29) | copy-start | bytes 196612
  7.2 65.0 %all-gather.3.cloned.1.call-start = ((), (), s32[]{:S(2)}) async-start(), calls=%async_computation.3 | async-start | bytes 8650752 | tf_op jit(solution)/shard_map/all_gather | solution.py:362
  7.9 14.6 %collective-permute-start.1 = (bf16[4096,384]{1,0:T(8,128)(2,1)}, bf16[4096,384]{1,0:T(8,128)(2,1)S(1)}, u32[]{:S(2)}, u32[]{:S(2)}) collective-permute-start(bf16[4096,384]{1,0:T(8,128)(2,1)} %bitcast.212), channel_id=1, source_target_pairs={{0,8},{8,0},{16,24},{24,16},{32,40},{40,32},{48,56},{56,48},{64,72... | collective-permute-start | bytes 9437192 | tf_op jit(solution)/shard_map/ppermute | solution.py:35
  8.0 14.5 %collective-permute-start.2 = (bf16[4096,384]{1,0:T(8,128)(2,1)}, bf16[4096,384]{1,0:T(8,128)(2,1)}, u32[]{:S(2)}, u32[]{:S(2)}) collective-permute-start(bf16[4096,384]{1,0:T(8,128)(2,1)} %bitcast.222), channel_id=1, source_target_pairs={{0,8},{8,0},{16,24},{24,16},{32,40},{40,32},{48,56},{56,48},{64,72... | collective-permute-start | bytes 9437192 | tf_op jit(solution)/shard_map/ppermute | solution.py:35
  8.5 14.5 %collective-permute-start.3 = (bf16[384,4096]{1,0:T(8,128)(2,1)}, bf16[384,4096]{1,0:T(8,128)(2,1)}, u32[]{:S(2)}, u32[]{:S(2)}) collective-permute-start(bf16[384,4096]{1,0:T(8,128)(2,1)} %bitcast.215), channel_id=1, source_target_pairs={{0,8},{8,0},{16,24},{24,16},{32,40},{40,32},{48,56},{56,48},{64,72... | collective-permute-start | bytes 9437192 | tf_op jit(solution)/shard_map/ppermute | solution.py:35
  9.3 5.3 %collective-permute-start = (bf16[3,1024]{1,0:T(4,128)(2,1)S(1)}, bf16[3,1024]{1,0:T(4,128)(2,1)S(1)}, u32[]{:S(2)}, u32[]{:S(2)}) collective-permute-start(bf16[3,1024]{1,0:T(4,128)(2,1)S(1)} %slice.126), channel_id=1, source_target_pairs={{0,8},{8,16},{16,24},{24,32},{32,40},{40,48},{48,56},{56,64},{64,7... | collective-permute-start | bytes 18440 | tf_op jit(solution)/shard_map/ppermute | solution.py:225
  22.4 27.6 %copy-start.2 = (f32[128,128]{1,0:T(8,128)S(1)}, f32[128,128]{1,0:T(8,128)}, u32[]{:S(2)}) copy-start(f32[128,128]{1,0:T(8,128)} %get-tuple-element.28.scaled_ref) | copy-start | bytes 196612
  22.5 28.8 %copy-start.3 = (f32[2048]{0:T(1024)S(1)}, f32[2048]{0:T(1024)}, u32[]{:S(2)}) copy-start(f32[2048]{0:T(1024)} %reshape.173.out_ref) | copy-start | bytes 24580
  22.5 28.8 %copy-start.5 = (bf16[128,1024]{1,0:T(8,128)(2,1)S(1)}, bf16[128,1024]{1,0:T(8,128)(2,1)}, u32[]{:S(2)}) copy-start(bf16[128,1024]{1,0:T(8,128)(2,1)} %gate_hbm.1) | copy-start | bytes 786436
  23.0 2.2 collective-permute-start.4
  26.9 5.4 %collective-permute-start.5 = (f32[136,128]{1,0:T(8,128)S(1)}, f32[136,128]{1,0:T(8,128)S(1)}, u32[]{:S(2)}, u32[]{:S(2)}) collective-permute-start(f32[136,128]{1,0:T(8,128)S(1)} %maximum_bitcast_fusion), channel_id=1, source_target_pairs={{0,16},{8,24},{16,32},{24,40},{32,48},{40,56},{48,0},{56,8},{64,80... | collective-permute-start | bytes 208904 | tf_op jit(solution)/shard_map/ppermute | solution.py:35
  28.5 7.4 %collective-permute-start.6 = (f32[136,128]{1,0:T(8,128)S(1)}, f32[136,128]{1,0:T(8,128)S(1)}, u32[]{:S(2)}, u32[]{:S(2)}) collective-permute-start(f32[136,128]{1,0:T(8,128)S(1)} %maximum_bitcast_fusion), channel_id=1, source_target_pairs={{0,32},{8,40},{16,48},{24,56},{32,0},{40,8},{48,16},{56,24},{64,96... | collective-permute-start | bytes 208904 | tf_op jit(solution)/shard_map/ppermute | solution.py:35
  29.6 7.7 %collective-permute-start.7 = (f32[136,128]{1,0:T(8,128)S(1)}, f32[136,128]{1,0:T(8,128)S(1)}, u32[]{:S(2)}, u32[]{:S(2)}) collective-permute-start(f32[136,128]{1,0:T(8,128)S(1)} %maximum_bitcast_fusion), channel_id=1, source_target_pairs={{0,48},{8,56},{16,0},{24,8},{32,16},{40,24},{48,32},{56,40},{64,11... | collective-permute-start | bytes 208904 | tf_op jit(solution)/shard_map/ppermute | solution.py:35
  32.2 6.7 %copy-start.11 = (f32[136,128]{1,0:T(8,128)}, f32[136,128]{1,0:T(8,128)S(1)}, u32[]{:S(2)}) copy-start(f32[136,128]{1,0:T(8,128)S(1)} %collective-permute-done.5) | copy-start | bytes 208900
  36.0 3.0 %copy-start.12 = (f32[136,128]{1,0:T(8,128)}, f32[136,128]{1,0:T(8,128)S(1)}, u32[]{:S(2)}) copy-start(f32[136,128]{1,0:T(8,128)S(1)} %collective-permute-done.6) | copy-start | bytes 208900
  39.6 7.2 %collective-permute-start.8 = (f32[136,128]{1,0:T(8,128)}, f32[136,128]{1,0:T(8,128)}, u32[]{:S(2)}, u32[]{:S(2)}) collective-permute-start(f32[136,128]{1,0:T(8,128)} %maximum_bitcast_fusion.1), channel_id=1, source_target_pairs={{0,64},{8,72},{16,80},{24,88},{32,96},{40,104},{48,112},{56,120},{... | collective-permute-start | bytes 208904 | tf_op jit(solution)/shard_map/ppermute | solution.py:35
  42.6 6.0 %collective-permute-start.9 = (f32[136,128]{1,0:T(8,128)}, f32[136,128]{1,0:T(8,128)S(1)}, u32[]{:S(2)}, u32[]{:S(2)}) collective-permute-start(f32[136,128]{1,0:T(8,128)} %maximum_bitcast_fusion.1), channel_id=1, source_target_pairs={{0,128},{8,136},{16,144},{24,152},{32,160},{40,168},{48,176},{56,1... | collective-permute-start | bytes 208904 | tf_op jit(solution)/shard_map/ppermute | solution.py:35
  45.5 4.5 %collective-permute-start.10 = (f32[136,128]{1,0:T(8,128)}, f32[136,128]{1,0:T(8,128)S(1)}, u32[]{:S(2)}, u32[]{:S(2)}) collective-permute-start(f32[136,128]{1,0:T(8,128)} %maximum_bitcast_fusion.1), channel_id=1, source_target_pairs={{0,192},{8,200},{16,208},{24,216},{32,224},{40,232},{48,240},{56,2... | collective-permute-start | bytes 208904 | tf_op jit(solution)/shard_map/ppermute | solution.py:35
  51.3 1.0 copy-start.6
  52.3 1.0 copy-start.7
  80.0 36.3 %copy-start.13 = (bf16[16,4096]{1,0:T(8,128)(2,1)S(1)}, bf16[16,4096]{1,0:T(8,128)(2,1)}, u32[]{:S(2)}) copy-start(bf16[16,4096]{1,0:T(8,128)(2,1)} %param.27) | copy-start | bytes 393220
  80.0 36.6 %copy-start.14 = (f32[4096]{0:T(1024)S(1)}, f32[4096]{0:T(1024)}, u32[]{:S(2)}) copy-start(f32[4096]{0:T(1024)} %param.28) | copy-start | bytes 49156
  116.4 3.7 %copy-start.16 = (s32[32]{0:T(128)S(1)}, s32[32]{0:T(128)}, u32[]{:S(2)}) copy-start(s32[32]{0:T(128)} %multiply_add_fusion) | copy-start | bytes 388
  116.8 0.7 copy-start.8
  143.1 7.3 %collective-permute-start.11 = (bf16[40,4096]{1,0:T(8,128)(2,1)}, bf16[40,4096]{1,0:T(8,128)(2,1)S(1)}, u32[]{:S(2)}, u32[]{:S(2)}) collective-permute-start(bf16[40,4096]{1,0:T(8,128)(2,1)} %reshape.167), channel_id=1, source_target_pairs={{0,16},{8,72},{16,32},{24,88},{32,48},{40,104},{48,0},{56,120},{64... | collective-permute-start | bytes 983048 | tf_op jit(solution)/shard_map/ppermute | solution.py:235
  143.7 8.8 %collective-permute-start.13 = (bf16[40,4096]{1,0:T(8,128)(2,1)}, bf16[40,4096]{1,0:T(8,128)(2,1)S(1)}, u32[]{:S(2)}, u32[]{:S(2)}) collective-permute-start(bf16[40,4096]{1,0:T(8,128)(2,1)} %reshape.167), channel_id=1, source_target_pairs={{0,48},{8,200},{16,0},{24,216},{32,16},{40,232},{48,32},{56,248},{... | collective-permute-start | bytes 983048 | tf_op jit(solution)/shard_map/ppermute | solution.py:235
  145.2 28.2 %copy-start.1 = (bf16[1,4096,384]{2,1,0:T(8,128)(2,1)S(1)}, bf16[1,4096,384]{2,1,0:T(8,128)(2,1)}, u32[]{:S(2)}) copy-start(bf16[1,4096,384]{2,1,0:T(8,128)(2,1)} %param.31) | copy-start | bytes 9437188
  150.4 6.5 %collective-permute-start.12 = (bf16[40,2048]{1,0:T(8,128)(2,1)S(1)}, bf16[40,2048]{1,0:T(8,128)(2,1)S(1)}, u32[]{:S(2)}, u32[]{:S(2)}) collective-permute-start(bf16[40,2048]{1,0:T(8,128)(2,1)S(1)} %slice.184), channel_id=1, source_target_pairs={{0,16},{8,72},{16,32},{24,88},{32,48},{40,104},{48,0},{56,120},{64... | collective-permute-start | bytes 491528 | tf_op jit(solution)/shard_map/ppermute | solution.py:235
  152.5 6.7 %collective-permute-start.14 = (bf16[40,2048]{1,0:T(8,128)(2,1)S(1)}, bf16[40,2048]{1,0:T(8,128)(2,1)S(1)}, u32[]{:S(2)}, u32[]{:S(2)}) collective-permute-start(bf16[40,2048]{1,0:T(8,128)(2,1)S(1)} %slice.185), channel_id=1, source_target_pairs={{0,48},{8,200},{16,0},{24,216},{32,16},{40,232},{48,32},{56,248},{... | collective-permute-start | bytes 491528 | tf_op jit(solution)/shard_map/ppermute | solution.py:235
  152.8 11.9 %collective-permute-start.15 = (bf16[80,4096]{1,0:T(8,128)(2,1)S(1)}, bf16[80,4096]{1,0:T(8,128)(2,1)S(1)}, u32[]{:S(2)}, u32[]{:S(2)}) collective-permute-start(bf16[80,4096]{1,0:T(8,128)(2,1)S(1)} %constant_dynamic-update-slice_fusion.refs_0_), channel_id=1, source_target_pairs={{0,64},{8,24},{16,80},{24,40},{32,96},{40,56},{48,112},{56,8},{64,... | collective-permute-start | bytes 1966088 | tf_op jit(solution)/shard_map/ppermute | solution.py:235
  159.2 11.3 %collective-permute-start.16 = (bf16[80,4096]{1,0:T(8,128)(2,1)S(1)}, bf16[80,4096]{1,0:T(8,128)(2,1)S(1)}, u32[]{:S(2)}, u32[]{:S(2)}) collective-permute-start(bf16[80,4096]{1,0:T(8,128)(2,1)S(1)} %pad_maximum_fusion.refs_1_), channel_id=1, source_target_pairs={{0,192},{8,56},{16,208},{24,8},{32,224},{40,24},{48,240},{56,40},{... | collective-permute-start | bytes 1966088 | tf_op jit(solution)/shard_map/ppermute | solution.py:235
  161.6 19.0 %collective-permute-start.19 = (bf16[80,4096]{1,0:T(8,128)(2,1)S(1)}, bf16[80,4096]{1,0:T(8,128)(2,1)S(1)}, u32[]{:S(2)}, u32[]{:S(2)}) collective-permute-start(bf16[80,4096]{1,0:T(8,128)(2,1)S(1)} %constant_dynamic-update-slice_fusion.refs_0_), channel_id=1, source_target_pairs={{0,192},{8,56},{16,208},{24,8},{32,224},{40,24},{48,240},{56,40},{... | collective-permute-start | bytes 1966088 | tf_op jit(solution)/shard_map/ppermute | solution.py:235
  163.4 17.2 %collective-permute-start.20 = (bf16[80,4096]{1,0:T(8,128)(2,1)S(1)}, bf16[80,4096]{1,0:T(8,128)(2,1)S(1)}, u32[]{:S(2)}, u32[]{:S(2)}) collective-permute-start(bf16[80,4096]{1,0:T(8,128)(2,1)S(1)} %pad_maximum_fusion.refs_1_), channel_id=1, source_target_pairs={{0,64},{8,24},{16,80},{24,40},{32,96},{40,56},{48,112},{56,8},{64,... | collective-permute-start | bytes 1966088 | tf_op jit(solution)/shard_map/ppermute | solution.py:235
  164.7 17.5 %collective-permute-start.17 = (bf16[80,4096]{1,0:T(8,128)(2,1)S(1)}, bf16[80,4096]{1,0:T(8,128)(2,1)S(1)}, u32[]{:S(2)}, u32[]{:S(2)}) collective-permute-start(bf16[80,4096]{1,0:T(8,128)(2,1)S(1)} %collective-permute-done.15.refs_2_), channel_id=1, source_target_pairs={{0,64},{8,24},{16,80},{24,40},{32,96},{40,56},{48,112},{56,8},{64,... | collective-permute-start | bytes 1966088 | tf_op jit(solution)/shard_map/ppermute | solution.py:235
  170.5 14.0 %collective-permute-start.18 = (bf16[80,4096]{1,0:T(8,128)(2,1)S(1)}, bf16[80,4096]{1,0:T(8,128)(2,1)S(1)}, u32[]{:S(2)}, u32[]{:S(2)}) collective-permute-start(bf16[80,4096]{1,0:T(8,128)(2,1)S(1)} %collective-permute-done.16.refs_3_), channel_id=1, source_target_pairs={{0,192},{8,56},{16,208},{24,8},{32,224},{40,24},{48,240},{56,40},{... | collective-permute-start | bytes 1966088 | tf_op jit(solution)/shard_map/ppermute | solution.py:235
  180.5 11.2 %copy-start.4 = (bf16[1,384,4096]{2,1,0:T(8,128)(2,1)S(1)}, bf16[1,384,4096]{2,1,0:T(8,128)(2,1)}, u32[]{:S(2)}) copy-start(bf16[1,384,4096]{2,1,0:T(8,128)(2,1)} %param.33) | copy-start | bytes 9437188
  196.5 11.0 %collective-permute-start.26 = (bf16[80,4096]{1,0:T(8,128)(2,1)S(1)}, bf16[80,4096]{1,0:T(8,128)(2,1)S(1)}, u32[]{:S(2)}, u32[]{:S(2)}) collective-permute-start(bf16[80,4096]{1,0:T(8,128)(2,1)S(1)} %get-tuple-element.45), channel_id=1, source_target_pairs={{0,192},{8,56},{16,208},{24,8},{32,224},{40,24},{48,240},{56,40},{... | collective-permute-start | bytes 1966088 | tf_op jit(solution)/shard_map/ppermute | solution.py:235
  199.4 19.1 %collective-permute-start.25 = (bf16[80,4096]{1,0:T(8,128)(2,1)S(1)}, bf16[80,4096]{1,0:T(8,128)(2,1)S(1)}, u32[]{:S(2)}, u32[]{:S(2)}) collective-permute-start(bf16[80,4096]{1,0:T(8,128)(2,1)S(1)} %get-tuple-element.43), channel_id=1, source_target_pairs={{0,64},{8,24},{16,80},{24,40},{32,96},{40,56},{48,112},{56,8},{64,... | collective-permute-start | bytes 1966088 | tf_op jit(solution)/shard_map/ppermute | solution.py:235
  199.4 18.8 %collective-permute-start.22 = (bf16[80,4096]{1,0:T(8,128)(2,1)S(1)}, bf16[80,4096]{1,0:T(8,128)(2,1)S(1)}, u32[]{:S(2)}, u32[]{:S(2)}) collective-permute-start(bf16[80,4096]{1,0:T(8,128)(2,1)S(1)} %get-tuple-element.41), channel_id=1, source_target_pairs={{0,64},{8,24},{16,80},{24,40},{32,96},{40,56},{48,112},{56,8},{64,... | collective-permute-start | bytes 1966088 | tf_op jit(solution)/shard_map/ppermute | solution.py:235
  200.6 26.6 %collective-permute-start.21 = (bf16[80,4096]{1,0:T(8,128)(2,1)S(1)}, bf16[80,4096]{1,0:T(8,128)(2,1)S(1)}, u32[]{:S(2)}, u32[]{:S(2)}) collective-permute-start(bf16[80,4096]{1,0:T(8,128)(2,1)S(1)} %get-tuple-element.39), channel_id=1, source_target_pairs={{0,192},{8,56},{16,208},{24,8},{32,224},{40,24},{48,240},{56,40},{... | collective-permute-start | bytes 1966088 | tf_op jit(solution)/shard_map/ppermute | solution.py:235
  207.7 17.7 %collective-permute-start.27 = (bf16[80,4096]{1,0:T(8,128)(2,1)S(1)}, bf16[80,4096]{1,0:T(8,128)(2,1)S(1)}, u32[]{:S(2)}, u32[]{:S(2)}) collective-permute-start(bf16[80,4096]{1,0:T(8,128)(2,1)S(1)} %add_convert_fusion.1), channel_id=1, source_target_pairs={{0,192},{8,56},{16,208},{24,8},{32,224},{40,24},{48,240},{56,40},{... | collective-permute-start | bytes 1966088 | tf_op jit(solution)/shard_map/ppermute | solution.py:235
  218.4 18.1 %collective-permute-start.23 = (bf16[80,4096]{1,0:T(8,128)(2,1)S(1)}, bf16[80,4096]{1,0:T(8,128)(2,1)S(1)}, u32[]{:S(2)}, u32[]{:S(2)}) collective-permute-start(bf16[80,4096]{1,0:T(8,128)(2,1)S(1)} %add_convert_fusion.2), channel_id=1, source_target_pairs={{0,64},{8,24},{16,80},{24,40},{32,96},{40,56},{48,112},{56,8},{64,... | collective-permute-start | bytes 1966088 | tf_op jit(solution)/shard_map/ppermute | solution.py:235
  225.7 11.2 %collective-permute-start.28 = (bf16[40,4096]{1,0:T(8,128)(2,1)S(1)}, bf16[40,4096]{1,0:T(8,128)(2,1)S(1)}, u32[]{:S(2)}, u32[]{:S(2)}) collective-permute-start(bf16[40,4096]{1,0:T(8,128)(2,1)S(1)} %get-tuple-element.61), channel_id=1, source_target_pairs={{0,32},{8,136},{16,48},{24,152},{32,0},{40,168},{48,16},{56,184},{... | collective-permute-start | bytes 983048 | tf_op jit(solution)/shard_map/ppermute | solution.py:235
  225.8 11.1 %collective-permute-start.29 = (bf16[40,4096]{1,0:T(8,128)(2,1)S(1)}, bf16[40,4096]{1,0:T(8,128)(2,1)S(1)}, u32[]{:S(2)}, u32[]{:S(2)}) collective-permute-start(bf16[40,4096]{1,0:T(8,128)(2,1)S(1)} %get-tuple-element.62), channel_id=1, source_target_pairs={{0,16},{8,72},{16,32},{24,88},{32,48},{40,104},{48,0},{56,120},{64... | collective-permute-start | bytes 983048 | tf_op jit(solution)/shard_map/ppermute | solution.py:235
  236.7 13.0 %copy-start.9 = (bf16[16,4096]{1,0:T(8,128)(2,1)S(1)}, bf16[16,4096]{1,0:T(8,128)(2,1)}, u32[]{:S(2)}) copy-start(bf16[16,4096]{1,0:T(8,128)(2,1)} %copy-done.8) | copy-start | bytes 393220
  236.8 13.1 %copy-start.15 = (s32[16,2]{0,1:T(2,128)S(1)}, s32[16,2]{0,1:T(2,128)}, u32[]{:S(2)}) copy-start(s32[16,2]{0,1:T(2,128)} %param.30) | copy-start | bytes 388
  236.8 8.4 %collective-permute-start.24 = (bf16[40,4096]{1,0:T(8,128)(2,1)S(1)}, bf16[40,4096]{1,0:T(8,128)(2,1)S(1)}, u32[]{:S(2)}, u32[]{:S(2)}) collective-permute-start(bf16[40,4096]{1,0:T(8,128)(2,1)S(1)} %slice.275), channel_id=1, source_target_pairs={{0,48},{8,200},{16,0},{24,216},{32,16},{40,232},{48,32},{56,248},{... | collective-permute-start | bytes 983048 | tf_op jit(solution)/shard_map/ppermute | solution.py:235
  246.2 14.5 %all-to-all-start.2 = ((bf16[8,160,128]{2,1,0:T(8,128)(2,1)}), bf16[8,160,128]{2,1,0:T(8,128)(2,1)S(1)}, u32[]{:S(2)}, u32[]{:S(2)}) async-start(bf16[8,160,128]{2,1,0:T(8,128)(2,1)} %reshape.168), calls=%async_computation.2 | async-start | bytes 655360 | tf_op jit(solution)/shard_map/all_to_all | solution.py:452
  (2 other events, 1.2 us)
Sparse Core Ops, SparseCore 0:
  10.6 61.5 all-gather.2

commit v7 on v6

--- a/solution.py
+++ b/solution.py
@@ -269,7 +269,7 @@
         in_specs=[VMEM] * len(pieces) + [weight] * 4,
         out_specs=(act, act),
         scratch_shapes=[pltpu.VMEM((count, width), jnp.bfloat16)],
-        compiler_params=pltpu.CompilerParams(vmem_limit_bytes=42 << 20),
+        compiler_params=pltpu.CompilerParams(vmem_limit_bytes=50 << 20),
         cost_estimate=pl.CostEstimate(
             flops=8 * count * width * hidden, transcendentals=2 * count * hidden, bytes_accessed=16_000_000
         ),
@@ -308,7 +308,7 @@
         in_specs=[VMEM] * 4 + [weight] * 2,
         out_specs=(piece,) * len(places),
         scratch_shapes=[pltpu.VMEM((count, 2 * hidden), jnp.bfloat16)],
-        compiler_params=pltpu.CompilerParams(vmem_limit_bytes=42 << 20),
+        compiler_params=pltpu.CompilerParams(vmem_limit_bytes=50 << 20),
         cost_estimate=pl.CostEstimate(
             flops=4 * count * width * hidden, transcendentals=0, bytes_accessed=9_000_000
         ),
@@ -423,23 +423,22 @@
     mixed = finish_scan(y, sums, start, scaled, gate_input, out_flat)
     rows = residual.shape[0]
     model_width = residual.shape[1]
+    projected = project(mixed, out_weight)
+    hidden_state = residual.astype(jnp.float32) + projected
+    scale = lax.rsqrt(jnp.mean(hidden_state * hidden_state, axis=1, keepdims=True) + 1e-06)
+    normed = (hidden_state * scale * norm_gain[None, :]).astype(jnp.bfloat16)
     experts = router_weight.shape[1]
     capacity = 2 * rows // experts + 1
+    logits = jnp.dot(normed, router_weight, preferred_element_type=jnp.float32)
     expert_range = jnp.arange(experts, dtype=jnp.int32)
+    matches = expert_ids[:, :, None] == expert_range[None, None, :]
+    chosen = jnp.sum(jnp.where(matches, logits[:, None, :], 0.0), axis=2)
+    first = jax.nn.sigmoid(chosen[:, 0] - chosen[:, 1])
     flat_ids = expert_ids.reshape(-1)
     position = jnp.arange(flat_ids.shape[0], dtype=jnp.int32)
     earlier = (flat_ids[:, None] == flat_ids[None, :]) & (position[None, :] < position[:, None])
     rank = jnp.sum(earlier.astype(jnp.int32), axis=1)
     target = flat_ids * capacity + rank
-    mixed, target = lax.optimization_barrier((mixed, target))
-    projected = project(mixed, out_weight)
-    hidden_state = residual.astype(jnp.float32) + projected
-    scale = lax.rsqrt(jnp.mean(hidden_state * hidden_state, axis=1, keepdims=True) + 1e-06)
-    normed = (hidden_state * scale * norm_gain[None, :]).astype(jnp.bfloat16)
-    logits = jnp.dot(normed, router_weight, preferred_element_type=jnp.float32)
-    matches = expert_ids[:, :, None] == expert_range[None, None, :]
-    chosen = jnp.sum(jnp.where(matches, logits[:, None, :], 0.0), axis=2)
-    first = jax.nn.sigmoid(chosen[:, 0] - chosen[:, 1])
     placing = (jnp.arange(experts * capacity, dtype=jnp.int32)[:, None] == target[None, :]).astype(
         jnp.bfloat16
     )

time: 270 us -> 262 us (0.970)
  blocking collectives: 53.7 us -> 16.1 us
  waiting for transfers between devices: 87.1 us -> 121 us
  starting transfers between devices: 40.3 us -> 52.8 us
  local copies, waits for them, and re-layouts: 17.8 us -> 6.25 us
  other arithmetic: 10.3 us -> 5.16 us
    all_to_all x1 -> x0, blocking collectives: 36.3 us -> none  [project(): terms = lax.all_to_all(terms, 'exp', 0, 0, tiled=True)]
    all_to_all x0 -> x1, waiting for transfers between devices: none -> 28.8 us  [project(): terms = lax.all_to_all(terms, 'exp', 0, 0, tiled=True)]
    all_to_all x0 -> x1, starting transfers between devices: none -> 7.15 us  [project(): terms = lax.all_to_all(terms, 'exp', 0, 0, tiled=True)]
    all_gather x1, waiting for transfers between devices: 15 us -> 21.3 us  [project(): blocks = lax.all_gather(weight, 'seq')]
    unnamed x38 -> x22, local copies, waits for them, and re-layouts: 5.91 us -> 0.75 us
    ppermute x19, starting transfers between devices: 24.2 us -> 29.2 us  [around(): return lax.ppermute(block, 'seq', route)]
    ppermute x19, waiting for transfers between devices: 51.7 us -> 47.3 us  [around(): return lax.ppermute(block, 'seq', route)]
    ppermute x10, waiting for transfers between devices: 8.95 us -> 11.9 us  [moved(): return lax.ppermute(block, 'seq', route)]
  transfers between devices with their start and end apart: 32 -> 33, of which waited for: 20 -> 21; matrix products, arithmetic and copies ran while one was open for 6% -> 3% of each run, Pallas kernels for 9% -> 9%
where the time goes in v7:
time: 262 us; the launch traced here: 261 us
  waiting for transfers between devices  121 us (46%)
  starting transfers between devices  52.8 us (20%)
  Pallas kernels  44.5 us (17%)
  blocking collectives  16.1 us (6%)
  between operations  14.5 us (6%)
  local copies, waits for them, and re-layouts  6.25 us (2%)
  other arithmetic  5.16 us (2%)
    ppermute x19, waiting for transfers between devices, around(): return lax.ppermute(block, 'seq', route)  47.3 us
    ppermute x19, starting transfers between devices, around(): return lax.ppermute(block, 'seq', route)  29.2 us
    all_to_all x1, waiting for transfers between devices, project(): terms = lax.all_to_all(terms, 'exp', 0, 0, tiled=True)  28.8 us
    all_gather x1, waiting for transfers between devices, project(): blocks = lax.all_gather(weight, 'seq')  21.3 us
    all_to_all x1, blocking collectives, shards(): lax.all_to_all(outgoing, 'exp', split_axis=0, concat_axis=0, tiled=True)  16.1 us
    pallas_call x2, Pallas kernels, expert_in(): pl.pallas_call(expert_in_kernel, name='expert_in', grid=(hidden // LANES,...  15.3 us
    ppermute x10, waiting for transfers between devices, moved(): return lax.ppermute(block, 'seq', route)  11.9 us
    all_to_all x1, waiting for transfers between devices, shards(): lax.all_to_all(summed_out.reshape(arrived.shape), 'exp', split_axis=0, co...  10.8 us
  transfers between devices with their start and end apart: 33, of which 21 were waited for; matrix products, arithmetic and copies ran while one was open for 3% of the time, Pallas kernels for 9%

profile of v7, /device:TPU:6, one launch (start us, length us, event | category | flops | bytes accessed | tf_op | source)
XLA Modules:
  0.0 260.8 jit_solution(4987227793188275304)
XLA Ops:
  9.3 2.3 collective-permute-start
  15.2 7.2 %local_scan.1 = (f32[1024,128]{1,0:T(8,128)}, f32[1024,128]{1,0:T(8,128)}, f32[136,128]{1,0:T(8,128)}, f32[128,128]{1,0:T(8,128)}) custom-call(bf16[128,1024]{1,0:T(8,128)(2,1)} %inp_hbm.1, bf16[128,1024]{1,0:T(8,128)(2,1)} %raw_hbm.1, f32[16,1024]{1,0:T(8,128)} %rate_hbm.1, f32[4,1024]{1,0:T(4,128)} %taps_hbm.1, f32[1,1024]{1,0:T(1,128)} %bitcast.227, ...), custom_call_target="tpu_custom_call" | custom-call | flops 8000000 | bytes 2000000 | tf_op jit(solution)/shard_map/local_scan/pallas_call | solution.py:130
  23.8 1.1 collective-permute-done.4
  25.6 0.9 bitcast_add_fusion.1
  26.6 1.8 collective-permute-start.5
  29.5 2.3 collective-permute-done.5
  31.8 3.9 %collective-permute-done.6 = f32[136,128]{1,0:T(8,128)S(1)} collective-permute-done((f32[136,128]{1,0:T(8,128)S(1)}, f32[136,128]{1,0:T(8,128)S(1)}, u32[]{:S(2)}, u32[]{:S(2)}) %collective-permute-start.6) | collective-permute-done | bytes 69664 | tf_op jit(solution)/shard_map/ppermute | solution.py:35
  35.7 1.1 collective-permute-done.7
  36.8 1.0 fusion.20
  37.8 2.0 collective-permute-start.8
  39.9 3.0 %collective-permute-start.9 = (f32[136,128]{1,0:T(8,128)S(1)}, f32[136,128]{1,0:T(8,128)S(1)}, u32[]{:S(2)}, u32[]{:S(2)}) collective-permute-start(f32[136,128]{1,0:T(8,128)S(1)} %maximum_bitcast_fusion.1), channel_id=1, source_target_pairs={{0,128},{8,136},{16,144},{24,152},{32,160},{40,168},{48,176},{56,1... | collective-permute-start | bytes 208904 | tf_op jit(solution)/shard_map/ppermute | solution.py:35
  42.8 1.3 collective-permute-start.10
  44.1 1.8 collective-permute-done.9
  46.0 1.1 collective-permute-done.10
  47.3 3.9 %finish_scan.1.mixed_ref = bf16[128,1024]{1,0:T(8,128)(2,1)} custom-call(f32[1024,128]{1,0:T(8,128)S(1)} %copy-done.4, f32[1024,128]{1,0:T(8,128)S(1)} %copy-done.5, f32[128,128]{1,0:T(8,128)S(1)} %fusion.9.start_ref, f32[128,128]{1,0:T(8,128)S(1)} %copy-done.1, bf16[128,1024]{1,0:T(8,128)(2,1)S(1)} %copy-done.3, f32[2048]{0:T(1024)S(1)} %copy-done.2), custom_call_target="tpu_custom_call" | custom-call | flops 8000000 | bytes 2000000 | tf_op jit(solution)/shard_map/finish_scan/pallas_call | solution.py:155
  51.1 21.3 %all-gather.3.cloned.1.call-done = bf16[32768,128]{1,0:T(8,128)(2,1)} async-done(((bf16[1024,128]{1,0:T(8,128)(2,1)}), bf16[32768,128]{1,0:T(8,128)(2,1)}) %all-gather.3.cloned.1.call-update) | async-done | bytes 8388624 | tf_op jit(solution)/shard_map/all_gather | solution.py:362
  72.4 7.9 %project.1 = bf16[8,16,4096]{2,1,0:T(8,128)(2,1)} custom-call(bf16[128,1024]{1,0:T(8,128)(2,1)} %finish_scan.1.mixed_ref, bf16[32,1024,128]{2,1,0:T(8,128)(2,1)} %bitcast.212, bf16[32,1024,128]{2,1,0:T(8,128)(2,1)} %bitcast.213, bf16[32,1024,128]{2,1,0:T(8,128)(2,1)} %bitcast.214, bf16[32,1024,128]{2,1,0:T(8,128)(2,1)} %bitcast.215), custom_call_target="tpu_custom_call" | custom-call | flops 1073741824 | bytes 10000000 | tf_op jit(solution)/shard_map/project/pallas_call | solution.py:369
  80.3 7.2 %all-to-all-start = ((bf16[8,16,4096]{2,1,0:T(8,128)(2,1)}), bf16[8,16,4096]{2,1,0:T(8,128)(2,1)S(1)}, u32[]{:S(2)}, u32[]{:S(2)}) async-start(bf16[8,16,4096]{2,1,0:T(8,128)(2,1)} %project.1), calls=%async_computation | async-start | bytes 2097152 | tf_op jit(solution)/shard_map/all_to_all | solution.py:381
  87.9 28.8 %all-to-all-done = bf16[8,16,4096]{2,1,0:T(8,128)(2,1)S(1)} async-done(((bf16[8,16,4096]{2,1,0:T(8,128)(2,1)}), bf16[8,16,4096]{2,1,0:T(8,128)(2,1)S(1)}, u32[]{:S(2)}, u32[]{:S(2)}) %all-to-all-start) | async-done | bytes 1048608 | tf_op jit(solution)/shard_map/all_to_all | solution.py:381
  117.8 16.1 %all_to_all.15 = bf16[8,160,128]{2,1,0:T(8,128)(2,1)S(1)} all-to-all(bf16[8,160,128]{2,1,0:T(8,128)(2,1)S(1)} %reshape.173), channel_id=1, replica_groups=mesh['seq'=32,'exp'=8] {'exp'}, dimensions={0} | all-to-all | bytes 655360 | tf_op jit(solution)/shard_map/all_to_all | solution.py:448
  134.7 1.5 collective-permute-start.13
  136.2 5.0 %collective-permute-done.11 = bf16[40,4096]{1,0:T(8,128)(2,1)S(1)} collective-permute-done((bf16[40,4096]{1,0:T(8,128)(2,1)S(1)}, bf16[40,4096]{1,0:T(8,128)(2,1)S(1)}, u32[]{:S(2)}, u32[]{:S(2)}) %collective-permute-start.11) | collective-permute-done | bytes 327712 | tf_op jit(solution)/shard_map/ppermute | solution.py:235
  141.2 2.0 collective-permute-start.12
  143.6 1.1 collective-permute-start.15
  144.7 2.8 %collective-permute-done.12 = bf16[40,2048]{1,0:T(8,128)(2,1)S(1)} collective-permute-done((bf16[40,2048]{1,0:T(8,128)(2,1)S(1)}, bf16[40,2048]{1,0:T(8,128)(2,1)S(1)}, u32[]{:S(2)}, u32[]{:S(2)}) %collective-permute-start.12) | collective-permute-done | bytes 163872 | tf_op jit(solution)/shard_map/ppermute | solution.py:235
  147.5 2.3 collective-permute-done.14
  149.9 2.6 collective-permute-start.16
  152.5 1.1 collective-permute-start.19
  153.6 1.0 collective-permute-start.20
  154.6 1.0 collective-permute-done.15.refs_2_
  155.5 5.6 %collective-permute-done.16.refs_3_ = bf16[80,4096]{1,0:T(8,128)(2,1)S(1)} collective-permute-done((bf16[80,4096]{1,0:T(8,128)(2,1)S(1)}, bf16[80,4096]{1,0:T(8,128)(2,1)S(1)}, u32[]{:S(2)}, u32[]{:S(2)}) %collective-permute-start.16) | collective-permute-done | bytes 655392 | tf_op jit(solution)/shard_map/ppermute | solution.py:235
  161.1 3.2 %collective-permute-start.18 = (bf16[80,4096]{1,0:T(8,128)(2,1)S(1)}, bf16[80,4096]{1,0:T(8,128)(2,1)S(1)}, u32[]{:S(2)}, u32[]{:S(2)}) collective-permute-start(bf16[80,4096]{1,0:T(8,128)(2,1)S(1)} %collective-permute-done.16.refs_3_), channel_id=1, source_target_pairs={{0,192},{8,56},{16,208},{24,8},{32,224},{40,24},{48,240},{56,40},{... | collective-permute-start | bytes 1966088 | tf_op jit(solution)/shard_map/ppermute | solution.py:235
  164.3 7.6 %expert_in.2 = (bf16[320,384]{1,0:T(8,128)(2,1)S(1)}, bf16[320,384]{1,0:T(8,128)(2,1)S(1)}) custom-call(bf16[80,4096]{1,0:T(8,128)(2,1)S(1)} %constant_dynamic-update-slice_fusion.refs_0_, bf16[80,4096]{1,0:T(8,128)(2,1)S(1)} %pad_maximum_fusion.refs_1_, bf16[80,4096]{1,0:T(8,128)(2,1)S(1)} %collective-permute-done.15.refs_2_, ...), custom_call_target="tpu_custom_call" | custom-call | flops 4026531840 | bytes 16000000 | tf_op jit(solution)/shard_map/expert_in/pallas_call | solution.py:264
  172.4 2.8 %collective-permute-done.18.refs_1_ = bf16[80,4096]{1,0:T(8,128)(2,1)S(1)} collective-permute-done((bf16[80,4096]{1,0:T(8,128)(2,1)S(1)}, bf16[80,4096]{1,0:T(8,128)(2,1)S(1)}, u32[]{:S(2)}, u32[]{:S(2)}) %collective-permute-start.18) | collective-permute-done | bytes 655392 | tf_op jit(solution)/shard_map/ppermute | solution.py:235
  175.2 7.6 %expert_in.3 = (bf16[320,384]{1,0:T(8,128)(2,1)S(1)}, bf16[320,384]{1,0:T(8,128)(2,1)S(1)}) custom-call(bf16[80,4096]{1,0:T(8,128)(2,1)S(1)} %collective-permute-done.17.refs_0_, bf16[80,4096]{1,0:T(8,128)(2,1)S(1)} %collective-permute-done.18.refs_1_, bf16[80,4096]{1,0:T(8,128)(2,1)S(1)} %collective-permute-done.19.refs_2_, ...), custom_call_target="tpu_custom_call" | custom-call | flops 4026531840 | bytes 16000000 | tf_op jit(solution)/shard_map/expert_in/pallas_call | solution.py:264
  182.8 5.1 %expert_out.3 = (bf16[80,4096]{1,0:T(8,128)(2,1)S(1)}, bf16[80,4096]{1,0:T(8,128)(2,1)S(1)}, bf16[80,4096]{1,0:T(8,128)(2,1)S(1)}, bf16[80,4096]{1,0:T(8,128)(2,1)S(1)}) custom-call(bf16[320,384]{1,0:T(8,128)(2,1)S(1)} %get-tuple-element.29.refs_0_, bf16[320,384]{1,0:T(8,128)(2,1)S(1)} %get-tuple-element.30.refs_1_, ...), custom_call_target="tpu_custom_call" | custom-call | flops 2013265920 | bytes 9000000 | tf_op jit(solution)/shard_map/expert_out/pallas_call | solution.py:303
  188.0 3.3 %collective-permute-start.26 = (bf16[80,4096]{1,0:T(8,128)(2,1)S(1)}, bf16[80,4096]{1,0:T(8,128)(2,1)S(1)}, u32[]{:S(2)}, u32[]{:S(2)}) collective-permute-start(bf16[80,4096]{1,0:T(8,128)(2,1)S(1)} %get-tuple-element.41), channel_id=1, source_target_pairs={{0,192},{8,56},{16,208},{24,8},{32,224},{40,24},{48,240},{56,40},{... | collective-permute-start | bytes 1966088 | tf_op jit(solution)/shard_map/ppermute | solution.py:235
  192.1 2.4 collective-permute-start.21
  194.5 5.1 %expert_out.2 = (bf16[80,4096]{1,0:T(8,128)(2,1)S(1)}, bf16[80,4096]{1,0:T(8,128)(2,1)S(1)}, bf16[80,4096]{1,0:T(8,128)(2,1)S(1)}, bf16[80,4096]{1,0:T(8,128)(2,1)S(1)}) custom-call(bf16[320,384]{1,0:T(8,128)(2,1)S(1)} %get-tuple-element.29.refs_0_, bf16[320,384]{1,0:T(8,128)(2,1)S(1)} %get-tuple-element.30.refs_1_, ...), custom_call_target="tpu_custom_call" | custom-call | flops 2013265920 | bytes 9000000 | tf_op jit(solution)/shard_map/expert_out/pallas_call | solution.py:303
  199.8 3.7 %collective-permute-start.27 = (bf16[80,4096]{1,0:T(8,128)(2,1)S(1)}, bf16[80,4096]{1,0:T(8,128)(2,1)S(1)}, u32[]{:S(2)}, u32[]{:S(2)}) collective-permute-start(bf16[80,4096]{1,0:T(8,128)(2,1)S(1)} %add_convert_fusion.1), channel_id=1, source_target_pairs={{0,192},{8,56},{16,208},{24,8},{32,224},{40,24},{48,240},{56,40},{... | collective-permute-start | bytes 1966088 | tf_op jit(solution)/shard_map/ppermute | solution.py:235
  203.5 6.6 %collective-permute-done.22 = bf16[80,4096]{1,0:T(8,128)(2,1)S(1)} collective-permute-done((bf16[80,4096]{1,0:T(8,128)(2,1)S(1)}, bf16[80,4096]{1,0:T(8,128)(2,1)S(1)}, u32[]{:S(2)}, u32[]{:S(2)}) %collective-permute-start.22) | collective-permute-done | bytes 655392 | tf_op jit(solution)/shard_map/ppermute | solution.py:235
  210.3 3.1 %collective-permute-done.27 = bf16[80,4096]{1,0:T(8,128)(2,1)S(1)} collective-permute-done((bf16[80,4096]{1,0:T(8,128)(2,1)S(1)}, bf16[80,4096]{1,0:T(8,128)(2,1)S(1)}, u32[]{:S(2)}, u32[]{:S(2)}) %collective-permute-start.27) | collective-permute-done | bytes 655392 | tf_op jit(solution)/shard_map/ppermute | solution.py:235
  213.7 3.5 %collective-permute-start.28 = (bf16[40,4096]{1,0:T(8,128)(2,1)S(1)}, bf16[40,4096]{1,0:T(8,128)(2,1)S(1)}, u32[]{:S(2)}, u32[]{:S(2)}) collective-permute-start(bf16[40,4096]{1,0:T(8,128)(2,1)S(1)} %get-tuple-element.57), channel_id=1, source_target_pairs={{0,32},{8,136},{16,48},{24,152},{32,0},{40,168},{48,16},{56,184},{... | collective-permute-start | bytes 983048 | tf_op jit(solution)/shard_map/ppermute | solution.py:235
  217.2 1.9 collective-permute-start.29
  219.1 9.5 %collective-permute-done.23 = bf16[80,4096]{1,0:T(8,128)(2,1)S(1)} collective-permute-done((bf16[80,4096]{1,0:T(8,128)(2,1)S(1)}, bf16[80,4096]{1,0:T(8,128)(2,1)S(1)}, u32[]{:S(2)}, u32[]{:S(2)}) %collective-permute-start.23) | collective-permute-done | bytes 655392 | tf_op jit(solution)/shard_map/ppermute | solution.py:235
  229.0 8.3 %collective-permute-done.24 = bf16[40,4096]{1,0:T(8,128)(2,1)S(1)} collective-permute-done((bf16[40,4096]{1,0:T(8,128)(2,1)S(1)}, bf16[40,4096]{1,0:T(8,128)(2,1)S(1)}, u32[]{:S(2)}, u32[]{:S(2)}) %collective-permute-start.24) | collective-permute-done | bytes 327712 | tf_op jit(solution)/shard_map/ppermute | solution.py:235
  238.3 3.4 %all-to-all-start.2 = ((bf16[8,160,128]{2,1,0:T(8,128)(2,1)}), bf16[8,160,128]{2,1,0:T(8,128)(2,1)S(1)}, u32[]{:S(2)}, u32[]{:S(2)}) async-start(bf16[8,160,128]{2,1,0:T(8,128)(2,1)} %reshape.175), calls=%async_computation.2 | async-start | bytes 655360 | tf_op jit(solution)/shard_map/all_to_all | solution.py:451
  242.0 10.8 %all-to-all-done.2 = bf16[8,160,128]{2,1,0:T(8,128)(2,1)S(1)} async-done(((bf16[8,160,128]{2,1,0:T(8,128)(2,1)}), bf16[8,160,128]{2,1,0:T(8,128)(2,1)S(1)}, u32[]{:S(2)}, u32[]{:S(2)}) %all-to-all-start.2) | async-done | bytes 327712 | tf_op jit(solution)/shard_map/all_to_all | solution.py:451
  (94 shorter events, 16.3 us)
Async XLA Ops:
  7.2 234.7 %copy-start = (bf16[4096,8]{0,1:T(8,128)(2,1)S(1)}, bf16[4096,8]{0,1:T(8,128)(2,1)}, u32[]{:S(2)}) copy-start(bf16[4096,8]{0,1:T(8,128)(2,1)} %param.29) | copy-start | bytes 196612
  7.2 65.3 %all-gather.3.cloned.1.call-start = ((), (), s32[]{:S(2)}) async-start(), calls=%async_computation.3 | async-start | bytes 8650752 | tf_op jit(solution)/shard_map/all_gather | solution.py:362
  7.9 14.6 %collective-permute-start.1 = (bf16[4096,384]{1,0:T(8,128)(2,1)}, bf16[4096,384]{1,0:T(8,128)(2,1)}, u32[]{:S(2)}, u32[]{:S(2)}) collective-permute-start(bf16[4096,384]{1,0:T(8,128)(2,1)} %bitcast.216), channel_id=1, source_target_pairs={{0,8},{8,0},{16,24},{24,16},{32,40},{40,32},{48,56},{56,48},{64,72... | collective-permute-start | bytes 9437192 | tf_op jit(solution)/shard_map/ppermute | solution.py:35
  8.0 14.5 %collective-permute-start.2 = (bf16[4096,384]{1,0:T(8,128)(2,1)}, bf16[4096,384]{1,0:T(8,128)(2,1)}, u32[]{:S(2)}, u32[]{:S(2)}) collective-permute-start(bf16[4096,384]{1,0:T(8,128)(2,1)} %bitcast.219), channel_id=1, source_target_pairs={{0,8},{8,0},{16,24},{24,16},{32,40},{40,32},{48,56},{56,48},{64,72... | collective-permute-start | bytes 9437192 | tf_op jit(solution)/shard_map/ppermute | solution.py:35
  8.5 14.5 %collective-permute-start.3 = (bf16[384,4096]{1,0:T(8,128)(2,1)}, bf16[384,4096]{1,0:T(8,128)(2,1)}, u32[]{:S(2)}, u32[]{:S(2)}) collective-permute-start(bf16[384,4096]{1,0:T(8,128)(2,1)} %bitcast.224), channel_id=1, source_target_pairs={{0,8},{8,0},{16,24},{24,16},{32,40},{40,32},{48,56},{56,48},{64,72... | collective-permute-start | bytes 9437192 | tf_op jit(solution)/shard_map/ppermute | solution.py:35
  9.3 5.3 %collective-permute-start = (bf16[3,1024]{1,0:T(4,128)(2,1)S(1)}, bf16[3,1024]{1,0:T(4,128)(2,1)S(1)}, u32[]{:S(2)}, u32[]{:S(2)}) collective-permute-start(bf16[3,1024]{1,0:T(4,128)(2,1)S(1)} %slice.126), channel_id=1, source_target_pairs={{0,8},{8,16},{16,24},{24,32},{32,40},{40,48},{48,56},{56,64},{64,7... | collective-permute-start | bytes 18440 | tf_op jit(solution)/shard_map/ppermute | solution.py:225
  14.6 0.6 copy-start.9
  22.4 24.7 %copy-start.1 = (f32[128,128]{1,0:T(8,128)S(1)}, f32[128,128]{1,0:T(8,128)}, u32[]{:S(2)}) copy-start(f32[128,128]{1,0:T(8,128)} %get-tuple-element.26.scaled_ref) | copy-start | bytes 196612
  22.5 24.8 %copy-start.2 = (f32[2048]{0:T(1024)S(1)}, f32[2048]{0:T(1024)}, u32[]{:S(2)}) copy-start(f32[2048]{0:T(1024)} %reshape.180.out_ref) | copy-start | bytes 24580
  22.5 24.8 %copy-start.3 = (bf16[128,1024]{1,0:T(8,128)(2,1)S(1)}, bf16[128,1024]{1,0:T(8,128)(2,1)}, u32[]{:S(2)}) copy-start(bf16[128,1024]{1,0:T(8,128)(2,1)} %gate_hbm.1) | copy-start | bytes 786436
  22.5 24.8 %copy-start.4 = (f32[1024,128]{1,0:T(8,128)S(1)}, f32[1024,128]{1,0:T(8,128)}, u32[]{:S(2)}) copy-start(f32[1024,128]{1,0:T(8,128)} %get-tuple-element.22.y_ref) | copy-start | bytes 1572868
  22.5 24.8 %copy-start.5 = (f32[1024,128]{1,0:T(8,128)S(1)}, f32[1024,128]{1,0:T(8,128)}, u32[]{:S(2)}) copy-start(f32[1024,128]{1,0:T(8,128)} %get-tuple-element.23.sums_ref) | copy-start | bytes 1572868
  23.0 1.9 collective-permute-start.4
  26.6 5.3 %collective-permute-start.5 = (f32[136,128]{1,0:T(8,128)S(1)}, f32[136,128]{1,0:T(8,128)S(1)}, u32[]{:S(2)}, u32[]{:S(2)}) collective-permute-start(f32[136,128]{1,0:T(8,128)S(1)} %maximum_bitcast_fusion), channel_id=1, source_target_pairs={{0,16},{8,24},{16,32},{24,40},{32,48},{40,56},{48,0},{56,8},{64,80... | collective-permute-start | bytes 208904 | tf_op jit(solution)/shard_map/ppermute | solution.py:35
  28.4 7.3 %collective-permute-start.6 = (f32[136,128]{1,0:T(8,128)S(1)}, f32[136,128]{1,0:T(8,128)S(1)}, u32[]{:S(2)}, u32[]{:S(2)}) collective-permute-start(f32[136,128]{1,0:T(8,128)S(1)} %maximum_bitcast_fusion), channel_id=1, source_target_pairs={{0,32},{8,40},{16,48},{24,56},{32,0},{40,8},{48,16},{56,24},{64,96... | collective-permute-start | bytes 208904 | tf_op jit(solution)/shard_map/ppermute | solution.py:35
  29.2 7.6 %collective-permute-start.7 = (f32[136,128]{1,0:T(8,128)S(1)}, f32[136,128]{1,0:T(8,128)S(1)}, u32[]{:S(2)}, u32[]{:S(2)}) collective-permute-start(f32[136,128]{1,0:T(8,128)S(1)} %maximum_bitcast_fusion), channel_id=1, source_target_pairs={{0,48},{8,56},{16,0},{24,8},{32,16},{40,24},{48,32},{56,40},{64,11... | collective-permute-start | bytes 208904 | tf_op jit(solution)/shard_map/ppermute | solution.py:35
  37.8 6.3 %collective-permute-start.8 = (f32[136,128]{1,0:T(8,128)S(1)}, f32[136,128]{1,0:T(8,128)S(1)}, u32[]{:S(2)}, u32[]{:S(2)}) collective-permute-start(f32[136,128]{1,0:T(8,128)S(1)} %maximum_bitcast_fusion.1), channel_id=1, source_target_pairs={{0,64},{8,72},{16,80},{24,88},{32,96},{40,104},{48,112},{56,120},{... | collective-permute-start | bytes 208904 | tf_op jit(solution)/shard_map/ppermute | solution.py:35
  39.9 6.1 %collective-permute-start.9 = (f32[136,128]{1,0:T(8,128)S(1)}, f32[136,128]{1,0:T(8,128)S(1)}, u32[]{:S(2)}, u32[]{:S(2)}) collective-permute-start(f32[136,128]{1,0:T(8,128)S(1)} %maximum_bitcast_fusion.1), channel_id=1, source_target_pairs={{0,128},{8,136},{16,144},{24,152},{32,160},{40,168},{48,176},{56,1... | collective-permute-start | bytes 208904 | tf_op jit(solution)/shard_map/ppermute | solution.py:35
  42.8 4.3 %collective-permute-start.10 = (f32[136,128]{1,0:T(8,128)S(1)}, f32[136,128]{1,0:T(8,128)S(1)}, u32[]{:S(2)}, u32[]{:S(2)}) collective-permute-start(f32[136,128]{1,0:T(8,128)S(1)} %maximum_bitcast_fusion.1), channel_id=1, source_target_pairs={{0,192},{8,200},{16,208},{24,216},{32,224},{40,232},{48,240},{56,2... | collective-permute-start | bytes 208904 | tf_op jit(solution)/shard_map/ppermute | solution.py:35
  80.3 7.2 %copy-start.8 = (s32[16,2]{0,1:T(2,128)S(1)}, s32[16,2]{0,1:T(2,128)}, u32[]{:S(2)}) copy-start(s32[16,2]{0,1:T(2,128)} %param.30) | copy-start | bytes 388
  80.3 36.4 %copy-start.6 = (bf16[16,4096]{1,0:T(8,128)(2,1)S(1)}, bf16[16,4096]{1,0:T(8,128)(2,1)}, u32[]{:S(2)}) copy-start(bf16[16,4096]{1,0:T(8,128)(2,1)} %param.27) | copy-start | bytes 393220
  80.3 36.7 %copy-start.7 = (f32[4096]{0:T(1024)S(1)}, f32[4096]{0:T(1024)}, u32[]{:S(2)}) copy-start(f32[4096]{0:T(1024)} %param.28) | copy-start | bytes 49156
  80.3 36.4 %all-to-all-start = ((bf16[8,16,4096]{2,1,0:T(8,128)(2,1)}), bf16[8,16,4096]{2,1,0:T(8,128)(2,1)S(1)}, u32[]{:S(2)}, u32[]{:S(2)}) async-start(bf16[8,16,4096]{2,1,0:T(8,128)(2,1)} %project.1), calls=%async_computation | async-start | bytes 2097152 | tf_op jit(solution)/shard_map/all_to_all | solution.py:381
  134.1 7.2 %collective-permute-start.11 = (bf16[40,4096]{1,0:T(8,128)(2,1)S(1)}, bf16[40,4096]{1,0:T(8,128)(2,1)S(1)}, u32[]{:S(2)}, u32[]{:S(2)}) collective-permute-start(bf16[40,4096]{1,0:T(8,128)(2,1)S(1)} %reshape.174), channel_id=1, source_target_pairs={{0,16},{8,72},{16,32},{24,88},{32,48},{40,104},{48,0},{56,120},{64... | collective-permute-start | bytes 983048 | tf_op jit(solution)/shard_map/ppermute | solution.py:235
  134.7 8.6 %collective-permute-start.13 = (bf16[40,4096]{1,0:T(8,128)(2,1)S(1)}, bf16[40,4096]{1,0:T(8,128)(2,1)S(1)}, u32[]{:S(2)}, u32[]{:S(2)}) collective-permute-start(bf16[40,4096]{1,0:T(8,128)(2,1)S(1)} %reshape.174), channel_id=1, source_target_pairs={{0,48},{8,200},{16,0},{24,216},{32,16},{40,232},{48,32},{56,248},{... | collective-permute-start | bytes 983048 | tf_op jit(solution)/shard_map/ppermute | solution.py:235
  141.2 6.3 %collective-permute-start.12 = (bf16[40,2048]{1,0:T(8,128)(2,1)S(1)}, bf16[40,2048]{1,0:T(8,128)(2,1)S(1)}, u32[]{:S(2)}, u32[]{:S(2)}) collective-permute-start(bf16[40,2048]{1,0:T(8,128)(2,1)S(1)} %slice.184), channel_id=1, source_target_pairs={{0,16},{8,72},{16,32},{24,88},{32,48},{40,104},{48,0},{56,120},{64... | collective-permute-start | bytes 491528 | tf_op jit(solution)/shard_map/ppermute | solution.py:235
  143.3 6.6 %collective-permute-start.14 = (bf16[40,2048]{1,0:T(8,128)(2,1)S(1)}, bf16[40,2048]{1,0:T(8,128)(2,1)S(1)}, u32[]{:S(2)}, u32[]{:S(2)}) collective-permute-start(bf16[40,2048]{1,0:T(8,128)(2,1)S(1)} %slice.185), channel_id=1, source_target_pairs={{0,48},{8,200},{16,0},{24,216},{32,16},{40,232},{48,32},{56,248},{... | collective-permute-start | bytes 491528 | tf_op jit(solution)/shard_map/ppermute | solution.py:235
  143.6 11.9 %collective-permute-start.15 = (bf16[80,4096]{1,0:T(8,128)(2,1)S(1)}, bf16[80,4096]{1,0:T(8,128)(2,1)S(1)}, u32[]{:S(2)}, u32[]{:S(2)}) collective-permute-start(bf16[80,4096]{1,0:T(8,128)(2,1)S(1)} %constant_dynamic-update-slice_fusion.refs_0_), channel_id=1, source_target_pairs={{0,64},{8,24},{16,80},{24,40},{32,96},{40,56},{48,112},{56,8},{64,... | collective-permute-start | bytes 1966088 | tf_op jit(solution)/shard_map/ppermute | solution.py:235
  149.9 11.2 %collective-permute-start.16 = (bf16[80,4096]{1,0:T(8,128)(2,1)S(1)}, bf16[80,4096]{1,0:T(8,128)(2,1)S(1)}, u32[]{:S(2)}, u32[]{:S(2)}) collective-permute-start(bf16[80,4096]{1,0:T(8,128)(2,1)S(1)} %pad_maximum_fusion.refs_1_), channel_id=1, source_target_pairs={{0,192},{8,56},{16,208},{24,8},{32,224},{40,24},{48,240},{56,40},{... | collective-permute-start | bytes 1966088 | tf_op jit(solution)/shard_map/ppermute | solution.py:235
  152.5 19.5 %collective-permute-start.19 = (bf16[80,4096]{1,0:T(8,128)(2,1)S(1)}, bf16[80,4096]{1,0:T(8,128)(2,1)S(1)}, u32[]{:S(2)}, u32[]{:S(2)}) collective-permute-start(bf16[80,4096]{1,0:T(8,128)(2,1)S(1)} %constant_dynamic-update-slice_fusion.refs_0_), channel_id=1, source_target_pairs={{0,192},{8,56},{16,208},{24,8},{32,224},{40,24},{48,240},{56,40},{... | collective-permute-start | bytes 1966088 | tf_op jit(solution)/shard_map/ppermute | solution.py:235
  153.6 18.4 %collective-permute-start.20 = (bf16[80,4096]{1,0:T(8,128)(2,1)S(1)}, bf16[80,4096]{1,0:T(8,128)(2,1)S(1)}, u32[]{:S(2)}, u32[]{:S(2)}) collective-permute-start(bf16[80,4096]{1,0:T(8,128)(2,1)S(1)} %pad_maximum_fusion.refs_1_), channel_id=1, source_target_pairs={{0,64},{8,24},{16,80},{24,40},{32,96},{40,56},{48,112},{56,8},{64,... | collective-permute-start | bytes 1966088 | tf_op jit(solution)/shard_map/ppermute | solution.py:235
  155.5 16.9 %collective-permute-start.17 = (bf16[80,4096]{1,0:T(8,128)(2,1)S(1)}, bf16[80,4096]{1,0:T(8,128)(2,1)S(1)}, u32[]{:S(2)}, u32[]{:S(2)}) collective-permute-start(bf16[80,4096]{1,0:T(8,128)(2,1)S(1)} %collective-permute-done.15.refs_2_), channel_id=1, source_target_pairs={{0,64},{8,24},{16,80},{24,40},{32,96},{40,56},{48,112},{56,8},{64,... | collective-permute-start | bytes 1966088 | tf_op jit(solution)/shard_map/ppermute | solution.py:235
  161.1 14.0 %collective-permute-start.18 = (bf16[80,4096]{1,0:T(8,128)(2,1)S(1)}, bf16[80,4096]{1,0:T(8,128)(2,1)S(1)}, u32[]{:S(2)}, u32[]{:S(2)}) collective-permute-start(bf16[80,4096]{1,0:T(8,128)(2,1)S(1)} %collective-permute-done.16.refs_3_), channel_id=1, source_target_pairs={{0,192},{8,56},{16,208},{24,8},{32,224},{40,24},{48,240},{56,40},{... | collective-permute-start | bytes 1966088 | tf_op jit(solution)/shard_map/ppermute | solution.py:235
  188.0 11.7 %collective-permute-start.26 = (bf16[80,4096]{1,0:T(8,128)(2,1)S(1)}, bf16[80,4096]{1,0:T(8,128)(2,1)S(1)}, u32[]{:S(2)}, u32[]{:S(2)}) collective-permute-start(bf16[80,4096]{1,0:T(8,128)(2,1)S(1)} %get-tuple-element.41), channel_id=1, source_target_pairs={{0,192},{8,56},{16,208},{24,8},{32,224},{40,24},{48,240},{56,40},{... | collective-permute-start | bytes 1966088 | tf_op jit(solution)/shard_map/ppermute | solution.py:235
  191.3 19.1 %collective-permute-start.25 = (bf16[80,4096]{1,0:T(8,128)(2,1)S(1)}, bf16[80,4096]{1,0:T(8,128)(2,1)S(1)}, u32[]{:S(2)}, u32[]{:S(2)}) collective-permute-start(bf16[80,4096]{1,0:T(8,128)(2,1)S(1)} %get-tuple-element.39), channel_id=1, source_target_pairs={{0,64},{8,24},{16,80},{24,40},{32,96},{40,56},{48,112},{56,8},{64,... | collective-permute-start | bytes 1966088 | tf_op jit(solution)/shard_map/ppermute | solution.py:235
  191.3 18.8 %collective-permute-start.22 = (bf16[80,4096]{1,0:T(8,128)(2,1)S(1)}, bf16[80,4096]{1,0:T(8,128)(2,1)S(1)}, u32[]{:S(2)}, u32[]{:S(2)}) collective-permute-start(bf16[80,4096]{1,0:T(8,128)(2,1)S(1)} %get-tuple-element.37), channel_id=1, source_target_pairs={{0,64},{8,24},{16,80},{24,40},{32,96},{40,56},{48,112},{56,8},{64,... | collective-permute-start | bytes 1966088 | tf_op jit(solution)/shard_map/ppermute | solution.py:235
  192.1 27.0 %collective-permute-start.21 = (bf16[80,4096]{1,0:T(8,128)(2,1)S(1)}, bf16[80,4096]{1,0:T(8,128)(2,1)S(1)}, u32[]{:S(2)}, u32[]{:S(2)}) collective-permute-start(bf16[80,4096]{1,0:T(8,128)(2,1)S(1)} %get-tuple-element.35), channel_id=1, source_target_pairs={{0,192},{8,56},{16,208},{24,8},{32,224},{40,24},{48,240},{56,40},{... | collective-permute-start | bytes 1966088 | tf_op jit(solution)/shard_map/ppermute | solution.py:235
  199.8 13.6 %collective-permute-start.27 = (bf16[80,4096]{1,0:T(8,128)(2,1)S(1)}, bf16[80,4096]{1,0:T(8,128)(2,1)S(1)}, u32[]{:S(2)}, u32[]{:S(2)}) collective-permute-start(bf16[80,4096]{1,0:T(8,128)(2,1)S(1)} %add_convert_fusion.1), channel_id=1, source_target_pairs={{0,192},{8,56},{16,208},{24,8},{32,224},{40,24},{48,240},{56,40},{... | collective-permute-start | bytes 1966088 | tf_op jit(solution)/shard_map/ppermute | solution.py:235
  210.2 18.4 %collective-permute-start.23 = (bf16[80,4096]{1,0:T(8,128)(2,1)S(1)}, bf16[80,4096]{1,0:T(8,128)(2,1)S(1)}, u32[]{:S(2)}, u32[]{:S(2)}) collective-permute-start(bf16[80,4096]{1,0:T(8,128)(2,1)S(1)} %add_convert_fusion.2), channel_id=1, source_target_pairs={{0,64},{8,24},{16,80},{24,40},{32,96},{40,56},{48,112},{56,8},{64,... | collective-permute-start | bytes 1966088 | tf_op jit(solution)/shard_map/ppermute | solution.py:235
  213.7 15.3 %collective-permute-start.28 = (bf16[40,4096]{1,0:T(8,128)(2,1)S(1)}, bf16[40,4096]{1,0:T(8,128)(2,1)S(1)}, u32[]{:S(2)}, u32[]{:S(2)}) collective-permute-start(bf16[40,4096]{1,0:T(8,128)(2,1)S(1)} %get-tuple-element.57), channel_id=1, source_target_pairs={{0,32},{8,136},{16,48},{24,152},{32,0},{40,168},{48,16},{56,184},{... | collective-permute-start | bytes 983048 | tf_op jit(solution)/shard_map/ppermute | solution.py:235
  217.2 11.8 %collective-permute-start.29 = (bf16[40,4096]{1,0:T(8,128)(2,1)S(1)}, bf16[40,4096]{1,0:T(8,128)(2,1)S(1)}, u32[]{:S(2)}, u32[]{:S(2)}) collective-permute-start(bf16[40,4096]{1,0:T(8,128)(2,1)S(1)} %get-tuple-element.58), channel_id=1, source_target_pairs={{0,16},{8,72},{16,32},{24,88},{32,48},{40,104},{48,0},{56,120},{64... | collective-permute-start | bytes 983048 | tf_op jit(solution)/shard_map/ppermute | solution.py:235
  228.9 8.4 %collective-permute-start.24 = (bf16[40,4096]{1,0:T(8,128)(2,1)S(1)}, bf16[40,4096]{1,0:T(8,128)(2,1)S(1)}, u32[]{:S(2)}, u32[]{:S(2)}) collective-permute-start(bf16[40,4096]{1,0:T(8,128)(2,1)S(1)} %slice.275), channel_id=1, source_target_pairs={{0,48},{8,200},{16,0},{24,216},{32,16},{40,232},{48,32},{56,248},{... | collective-permute-start | bytes 983048 | tf_op jit(solution)/shard_map/ppermute | solution.py:235
  238.3 14.5 %all-to-all-start.2 = ((bf16[8,160,128]{2,1,0:T(8,128)(2,1)}), bf16[8,160,128]{2,1,0:T(8,128)(2,1)S(1)}, u32[]{:S(2)}, u32[]{:S(2)}) async-start(bf16[8,160,128]{2,1,0:T(8,128)(2,1)} %reshape.175), calls=%async_computation.2 | async-start | bytes 655360 | tf_op jit(solution)/shard_map/all_to_all | solution.py:451
Sparse Core Ops, SparseCore 0:
  10.6 61.8 all-gather.2

commit v8 on v7

--- a/solution.py
+++ b/solution.py
@@ -277,9 +277,9 @@
 
 
 def expert_out_kernel(places, rows, *refs):
-    acts, (down_a, down_b) = refs[:4], refs[4:6]
-    outs, acts_ref = refs[6:-1], refs[-1]
-    hidden = down_a.shape[0]
+    acts, downs = refs[:4], refs[4:8]
+    outs, acts_ref = refs[8:-1], refs[-1]
+    hidden = acts_ref.shape[1] // 2
 
     @pl.when(pl.program_id(0) == 0)
     def _():
@@ -288,7 +288,7 @@
                 block = acts[2 * part + side][begin * rows : (begin + 1) * rows, :]
                 acts_ref[k * rows : (k + 1) * rows, side * hidden : (side + 1) * hidden] = block
 
-    down = jnp.concatenate([down_a[...], down_b[...]], axis=0)
+    down = jnp.concatenate([d[...] for d in downs], axis=0)
     result = jnp.dot(acts_ref[...], down, preferred_element_type=jnp.float32)
     for k, out in enumerate(outs):
         out[...] = result[k * rows : (k + 1) * rows].astype(out.dtype)
@@ -298,21 +298,21 @@
     hidden, width = here[2].shape
     count = len(places) * rows
     tile = 8 * LANES
-    weight = pl.BlockSpec((hidden, tile), lambda i: (0, i))
+    weights = [pl.BlockSpec((hidden // 2, tile), lambda i, h=h: (h, i)) for h in range(2)]
     piece = pl.BlockSpec((rows, tile), lambda i: (0, i))
     return pl.pallas_call(
         functools.partial(expert_out_kernel, places, rows),
         name="expert_out",
         grid=(width // tile,),
         out_shape=(jax.ShapeDtypeStruct((rows, width), jnp.bfloat16),) * len(places),
-        in_specs=[VMEM] * 4 + [weight] * 2,
+        in_specs=[VMEM] * 4 + weights * 2,
         out_specs=(piece,) * len(places),
         scratch_shapes=[pltpu.VMEM((count, 2 * hidden), jnp.bfloat16)],
         compiler_params=pltpu.CompilerParams(vmem_limit_bytes=50 << 20),
         cost_estimate=pl.CostEstimate(
             flops=4 * count * width * hidden, transcendentals=0, bytes_accessed=9_000_000
         ),
-    )(*acts, here[2], there[2])
+    )(*acts, here[2], here[2], there[2], there[2])
 
 
 def experts_of_rows(block, here, there):
@@ -363,7 +363,7 @@
     owners = lax.axis_size("exp")
     tokens, depth = mixed.shape
     count = blocks.shape[0]
-    group = SIDE
+    group = 2 * SIDE
     rows = tokens // owners
     views = [pl.BlockSpec((None, depth, LANES), lambda i, q=q: (group * i + q, 0, 0)) for q in range(group)]
     terms = pl.pallas_call(

time: 262 us -> 260 us (level)
  no operation moved by 1% of the time
where the time goes in v8:
time: 260 us; the launch traced here: 259 us
  waiting for transfers between devices  121 us (47%)
  starting transfers between devices  52.8 us (20%)
  Pallas kernels  42.6 us (16%)
  blocking collectives  16.1 us (6%)
  between operations  14.5 us (6%)
  local copies, waits for them, and re-layouts  6.25 us (2%)
  other arithmetic  5.16 us (2%)
    ppermute x19, waiting for transfers between devices, around(): return lax.ppermute(block, 'seq', route)  47.4 us
    ppermute x19, starting transfers between devices, around(): return lax.ppermute(block, 'seq', route)  29.1 us
    all_to_all x1, waiting for transfers between devices, project(): terms = lax.all_to_all(terms, 'exp', 0, 0, tiled=True)  28.8 us
    all_gather x1, waiting for transfers between devices, project(): blocks = lax.all_gather(weight, 'seq')  21.3 us
    all_to_all x1, blocking collectives, shards(): lax.all_to_all(outgoing, 'exp', split_axis=0, concat_axis=0, tiled=True)  16.1 us
    pallas_call x2, Pallas kernels, expert_in(): pl.pallas_call(expert_in_kernel, name='expert_in', grid=(hidden // LANES,...  15.3 us
    ppermute x10, waiting for transfers between devices, moved(): return lax.ppermute(block, 'seq', route)  11.9 us
    all_to_all x1, waiting for transfers between devices, shards(): lax.all_to_all(summed_out.reshape(arrived.shape), 'exp', split_axis=0, co...  10.8 us
  transfers between devices with their start and end apart: 33, of which 21 were waited for; matrix products, arithmetic and copies ran while one was open for 3% of the time, Pallas kernels for 9%

profile of v8, /device:TPU:6, one launch (start us, length us, event | category | flops | bytes accessed | tf_op | source)
XLA Modules:
  0.0 258.8 jit_solution(323728883816042316)
XLA Ops:
  9.3 2.3 collective-permute-start
  15.2 7.2 %local_scan.1 = (f32[1024,128]{1,0:T(8,128)}, f32[1024,128]{1,0:T(8,128)}, f32[136,128]{1,0:T(8,128)}, f32[128,128]{1,0:T(8,128)}) custom-call(bf16[128,1024]{1,0:T(8,128)(2,1)} %inp_hbm.1, bf16[128,1024]{1,0:T(8,128)(2,1)} %raw_hbm.1, f32[16,1024]{1,0:T(8,128)} %rate_hbm.1, f32[4,1024]{1,0:T(4,128)} %taps_hbm.1, f32[1,1024]{1,0:T(1,128)} %bitcast.233, ...), custom_call_target="tpu_custom_call" | custom-call | flops 8000000 | bytes 2000000 | tf_op jit(solution)/shard_map/local_scan/pallas_call | solution.py:130
  23.8 1.1 collective-permute-done.4
  25.6 0.9 bitcast_add_fusion.1
  26.6 1.8 collective-permute-start.5
  29.5 2.3 collective-permute-done.5
  31.8 3.9 %collective-permute-done.6 = f32[136,128]{1,0:T(8,128)S(1)} collective-permute-done((f32[136,128]{1,0:T(8,128)S(1)}, f32[136,128]{1,0:T(8,128)S(1)}, u32[]{:S(2)}, u32[]{:S(2)}) %collective-permute-start.6) | collective-permute-done | bytes 69664 | tf_op jit(solution)/shard_map/ppermute | solution.py:35
  35.7 1.1 collective-permute-done.7
  36.8 1.0 fusion.20
  37.8 2.0 collective-permute-start.8
  39.9 3.0 %collective-permute-start.9 = (f32[136,128]{1,0:T(8,128)S(1)}, f32[136,128]{1,0:T(8,128)S(1)}, u32[]{:S(2)}, u32[]{:S(2)}) collective-permute-start(f32[136,128]{1,0:T(8,128)S(1)} %maximum_bitcast_fusion.1), channel_id=1, source_target_pairs={{0,128},{8,136},{16,144},{24,152},{32,160},{40,168},{48,176},{56,1... | collective-permute-start | bytes 208904 | tf_op jit(solution)/shard_map/ppermute | solution.py:35
  42.8 1.3 collective-permute-start.10
  44.1 1.8 collective-permute-done.9
  46.0 1.1 collective-permute-done.10
  47.3 3.9 %finish_scan.1.mixed_ref = bf16[128,1024]{1,0:T(8,128)(2,1)} custom-call(f32[1024,128]{1,0:T(8,128)S(1)} %copy-done.4, f32[1024,128]{1,0:T(8,128)S(1)} %copy-done.5, f32[128,128]{1,0:T(8,128)S(1)} %fusion.9.start_ref, f32[128,128]{1,0:T(8,128)S(1)} %copy-done.1, bf16[128,1024]{1,0:T(8,128)(2,1)S(1)} %copy-done.3, f32[2048]{0:T(1024)S(1)} %copy-done.2), custom_call_target="tpu_custom_call" | custom-call | flops 8000000 | bytes 2000000 | tf_op jit(solution)/shard_map/finish_scan/pallas_call | solution.py:155
  51.1 21.3 %all-gather.3.cloned.1.call-done = bf16[32768,128]{1,0:T(8,128)(2,1)} async-done(((bf16[1024,128]{1,0:T(8,128)(2,1)}), bf16[32768,128]{1,0:T(8,128)(2,1)}) %all-gather.3.cloned.1.call-update) | async-done | bytes 8388624 | tf_op jit(solution)/shard_map/all_gather | solution.py:362
  72.4 5.9 %project.1 = bf16[8,16,4096]{2,1,0:T(8,128)(2,1)} custom-call(bf16[128,1024]{1,0:T(8,128)(2,1)} %finish_scan.1.mixed_ref, bf16[32,1024,128]{2,1,0:T(8,128)(2,1)} %bitcast.212, bf16[32,1024,128]{2,1,0:T(8,128)(2,1)} %bitcast.213, bf16[32,1024,128]{2,1,0:T(8,128)(2,1)} %bitcast.214, bf16[32,1024,128]{2,1,0:T(8,128)(2,1)} %bitcast.215, ...), custom_call_target="tpu_custom_call" | custom-call | flops 1073741824 | bytes 10000000 | tf_op jit(solution)/shard_map/project/pallas_call | solution.py:369
  78.4 7.2 %all-to-all-start = ((bf16[8,16,4096]{2,1,0:T(8,128)(2,1)}), bf16[8,16,4096]{2,1,0:T(8,128)(2,1)S(1)}, u32[]{:S(2)}, u32[]{:S(2)}) async-start(bf16[8,16,4096]{2,1,0:T(8,128)(2,1)} %project.1), calls=%async_computation | async-start | bytes 2097152 | tf_op jit(solution)/shard_map/all_to_all | solution.py:381
  85.9 28.8 %all-to-all-done = bf16[8,16,4096]{2,1,0:T(8,128)(2,1)S(1)} async-done(((bf16[8,16,4096]{2,1,0:T(8,128)(2,1)}), bf16[8,16,4096]{2,1,0:T(8,128)(2,1)S(1)}, u32[]{:S(2)}, u32[]{:S(2)}) %all-to-all-start) | async-done | bytes 1048608 | tf_op jit(solution)/shard_map/all_to_all | solution.py:381
  115.9 16.1 %all_to_all.15 = bf16[8,160,128]{2,1,0:T(8,128)(2,1)S(1)} all-to-all(bf16[8,160,128]{2,1,0:T(8,128)(2,1)S(1)} %reshape.173), channel_id=1, replica_groups=mesh['seq'=32,'exp'=8] {'exp'}, dimensions={0} | all-to-all | bytes 655360 | tf_op jit(solution)/shard_map/all_to_all | solution.py:448
  132.8 1.5 collective-permute-start.13
  134.3 5.0 %collective-permute-done.11 = bf16[40,4096]{1,0:T(8,128)(2,1)S(1)} collective-permute-done((bf16[40,4096]{1,0:T(8,128)(2,1)S(1)}, bf16[40,4096]{1,0:T(8,128)(2,1)S(1)}, u32[]{:S(2)}, u32[]{:S(2)}) %collective-permute-start.11) | collective-permute-done | bytes 327712 | tf_op jit(solution)/shard_map/ppermute | solution.py:235
  139.3 2.0 collective-permute-start.12
  141.7 1.1 collective-permute-start.15
  142.8 2.8 %collective-permute-done.12 = bf16[40,2048]{1,0:T(8,128)(2,1)S(1)} collective-permute-done((bf16[40,2048]{1,0:T(8,128)(2,1)S(1)}, bf16[40,2048]{1,0:T(8,128)(2,1)S(1)}, u32[]{:S(2)}, u32[]{:S(2)}) %collective-permute-start.12) | collective-permute-done | bytes 163872 | tf_op jit(solution)/shard_map/ppermute | solution.py:235
  145.6 2.4 collective-permute-done.14
  148.0 2.6 %collective-permute-start.16 = (bf16[80,4096]{1,0:T(8,128)(2,1)S(1)}, bf16[80,4096]{1,0:T(8,128)(2,1)S(1)}, u32[]{:S(2)}, u32[]{:S(2)}) collective-permute-start(bf16[80,4096]{1,0:T(8,128)(2,1)S(1)} %pad_maximum_fusion.refs_1_), channel_id=1, source_target_pairs={{0,192},{8,56},{16,208},{24,8},{32,224},{40,24},{48,240},{56,40},{... | collective-permute-start | bytes 1966088 | tf_op jit(solution)/shard_map/ppermute | solution.py:235
  150.6 1.1 collective-permute-start.19
  151.6 1.0 collective-permute-start.20
  152.6 1.0 collective-permute-done.15.refs_2_
  153.6 5.6 %collective-permute-done.16.refs_3_ = bf16[80,4096]{1,0:T(8,128)(2,1)S(1)} collective-permute-done((bf16[80,4096]{1,0:T(8,128)(2,1)S(1)}, bf16[80,4096]{1,0:T(8,128)(2,1)S(1)}, u32[]{:S(2)}, u32[]{:S(2)}) %collective-permute-start.16) | collective-permute-done | bytes 655392 | tf_op jit(solution)/shard_map/ppermute | solution.py:235
  159.2 3.2 %collective-permute-start.18 = (bf16[80,4096]{1,0:T(8,128)(2,1)S(1)}, bf16[80,4096]{1,0:T(8,128)(2,1)S(1)}, u32[]{:S(2)}, u32[]{:S(2)}) collective-permute-start(bf16[80,4096]{1,0:T(8,128)(2,1)S(1)} %collective-permute-done.16.refs_3_), channel_id=1, source_target_pairs={{0,192},{8,56},{16,208},{24,8},{32,224},{40,24},{48,240},{56,40},{... | collective-permute-start | bytes 1966088 | tf_op jit(solution)/shard_map/ppermute | solution.py:235
  162.4 7.6 %expert_in.2 = (bf16[320,384]{1,0:T(8,128)(2,1)S(1)}, bf16[320,384]{1,0:T(8,128)(2,1)S(1)}) custom-call(bf16[80,4096]{1,0:T(8,128)(2,1)S(1)} %constant_dynamic-update-slice_fusion.refs_0_, bf16[80,4096]{1,0:T(8,128)(2,1)S(1)} %pad_maximum_fusion.refs_1_, bf16[80,4096]{1,0:T(8,128)(2,1)S(1)} %collective-permute-done.15.refs_2_, ...), custom_call_target="tpu_custom_call" | custom-call | flops 4026531840 | bytes 16000000 | tf_op jit(solution)/shard_map/expert_in/pallas_call | solution.py:264
  170.5 2.8 %collective-permute-done.18.refs_1_ = bf16[80,4096]{1,0:T(8,128)(2,1)S(1)} collective-permute-done((bf16[80,4096]{1,0:T(8,128)(2,1)S(1)}, bf16[80,4096]{1,0:T(8,128)(2,1)S(1)}, u32[]{:S(2)}, u32[]{:S(2)}) %collective-permute-start.18) | collective-permute-done | bytes 655392 | tf_op jit(solution)/shard_map/ppermute | solution.py:235
  173.2 7.6 %expert_in.3 = (bf16[320,384]{1,0:T(8,128)(2,1)S(1)}, bf16[320,384]{1,0:T(8,128)(2,1)S(1)}) custom-call(bf16[80,4096]{1,0:T(8,128)(2,1)S(1)} %collective-permute-done.17.refs_0_, bf16[80,4096]{1,0:T(8,128)(2,1)S(1)} %collective-permute-done.18.refs_1_, bf16[80,4096]{1,0:T(8,128)(2,1)S(1)} %collective-permute-done.19.refs_2_, ...), custom_call_target="tpu_custom_call" | custom-call | flops 4026531840 | bytes 16000000 | tf_op jit(solution)/shard_map/expert_in/pallas_call | solution.py:264
  180.9 5.1 %expert_out.3 = (bf16[80,4096]{1,0:T(8,128)(2,1)S(1)}, bf16[80,4096]{1,0:T(8,128)(2,1)S(1)}, bf16[80,4096]{1,0:T(8,128)(2,1)S(1)}, bf16[80,4096]{1,0:T(8,128)(2,1)S(1)}) custom-call(bf16[320,384]{1,0:T(8,128)(2,1)S(1)} %get-tuple-element.29.refs_0_, bf16[320,384]{1,0:T(8,128)(2,1)S(1)} %get-tuple-element.30.refs_1_, ...), custom_call_target="tpu_custom_call" | custom-call | flops 2013265920 | bytes 9000000 | tf_op jit(solution)/shard_map/expert_out/pallas_call | solution.py:303
  186.0 3.3 %collective-permute-start.26 = (bf16[80,4096]{1,0:T(8,128)(2,1)S(1)}, bf16[80,4096]{1,0:T(8,128)(2,1)S(1)}, u32[]{:S(2)}, u32[]{:S(2)}) collective-permute-start(bf16[80,4096]{1,0:T(8,128)(2,1)S(1)} %get-tuple-element.41), channel_id=1, source_target_pairs={{0,192},{8,56},{16,208},{24,8},{32,224},{40,24},{48,240},{56,40},{... | collective-permute-start | bytes 1966088 | tf_op jit(solution)/shard_map/ppermute | solution.py:235
  190.2 2.4 collective-permute-start.21
  192.6 5.1 %expert_out.2 = (bf16[80,4096]{1,0:T(8,128)(2,1)S(1)}, bf16[80,4096]{1,0:T(8,128)(2,1)S(1)}, bf16[80,4096]{1,0:T(8,128)(2,1)S(1)}, bf16[80,4096]{1,0:T(8,128)(2,1)S(1)}) custom-call(bf16[320,384]{1,0:T(8,128)(2,1)S(1)} %get-tuple-element.29.refs_0_, bf16[320,384]{1,0:T(8,128)(2,1)S(1)} %get-tuple-element.30.refs_1_, ...), custom_call_target="tpu_custom_call" | custom-call | flops 2013265920 | bytes 9000000 | tf_op jit(solution)/shard_map/expert_out/pallas_call | solution.py:303
  197.9 3.7 %collective-permute-start.27 = (bf16[80,4096]{1,0:T(8,128)(2,1)S(1)}, bf16[80,4096]{1,0:T(8,128)(2,1)S(1)}, u32[]{:S(2)}, u32[]{:S(2)}) collective-permute-start(bf16[80,4096]{1,0:T(8,128)(2,1)S(1)} %add_convert_fusion.1), channel_id=1, source_target_pairs={{0,192},{8,56},{16,208},{24,8},{32,224},{40,24},{48,240},{56,40},{... | collective-permute-start | bytes 1966088 | tf_op jit(solution)/shard_map/ppermute | solution.py:235
  201.5 6.6 %collective-permute-done.22 = bf16[80,4096]{1,0:T(8,128)(2,1)S(1)} collective-permute-done((bf16[80,4096]{1,0:T(8,128)(2,1)S(1)}, bf16[80,4096]{1,0:T(8,128)(2,1)S(1)}, u32[]{:S(2)}, u32[]{:S(2)}) %collective-permute-start.22) | collective-permute-done | bytes 655392 | tf_op jit(solution)/shard_map/ppermute | solution.py:235
  208.4 3.1 %collective-permute-done.27 = bf16[80,4096]{1,0:T(8,128)(2,1)S(1)} collective-permute-done((bf16[80,4096]{1,0:T(8,128)(2,1)S(1)}, bf16[80,4096]{1,0:T(8,128)(2,1)S(1)}, u32[]{:S(2)}, u32[]{:S(2)}) %collective-permute-start.27) | collective-permute-done | bytes 655392 | tf_op jit(solution)/shard_map/ppermute | solution.py:235
  211.7 3.5 %collective-permute-start.28 = (bf16[40,4096]{1,0:T(8,128)(2,1)S(1)}, bf16[40,4096]{1,0:T(8,128)(2,1)S(1)}, u32[]{:S(2)}, u32[]{:S(2)}) collective-permute-start(bf16[40,4096]{1,0:T(8,128)(2,1)S(1)} %get-tuple-element.57), channel_id=1, source_target_pairs={{0,32},{8,136},{16,48},{24,152},{32,0},{40,168},{48,16},{56,184},{... | collective-permute-start | bytes 983048 | tf_op jit(solution)/shard_map/ppermute | solution.py:235
  215.2 1.9 collective-permute-start.29
  217.2 9.5 %collective-permute-done.23 = bf16[80,4096]{1,0:T(8,128)(2,1)S(1)} collective-permute-done((bf16[80,4096]{1,0:T(8,128)(2,1)S(1)}, bf16[80,4096]{1,0:T(8,128)(2,1)S(1)}, u32[]{:S(2)}, u32[]{:S(2)}) %collective-permute-start.23) | collective-permute-done | bytes 655392 | tf_op jit(solution)/shard_map/ppermute | solution.py:235
  227.0 8.3 %collective-permute-done.24 = bf16[40,4096]{1,0:T(8,128)(2,1)S(1)} collective-permute-done((bf16[40,4096]{1,0:T(8,128)(2,1)S(1)}, bf16[40,4096]{1,0:T(8,128)(2,1)S(1)}, u32[]{:S(2)}, u32[]{:S(2)}) %collective-permute-start.24) | collective-permute-done | bytes 327712 | tf_op jit(solution)/shard_map/ppermute | solution.py:235
  236.3 3.4 %all-to-all-start.2 = ((bf16[8,160,128]{2,1,0:T(8,128)(2,1)}), bf16[8,160,128]{2,1,0:T(8,128)(2,1)S(1)}, u32[]{:S(2)}, u32[]{:S(2)}) async-start(bf16[8,160,128]{2,1,0:T(8,128)(2,1)} %reshape.175), calls=%async_computation.2 | async-start | bytes 655360 | tf_op jit(solution)/shard_map/all_to_all | solution.py:451
  240.1 10.8 %all-to-all-done.2 = bf16[8,160,128]{2,1,0:T(8,128)(2,1)S(1)} async-done(((bf16[8,160,128]{2,1,0:T(8,128)(2,1)}), bf16[8,160,128]{2,1,0:T(8,128)(2,1)S(1)}, u32[]{:S(2)}, u32[]{:S(2)}) %all-to-all-start.2) | async-done | bytes 327712 | tf_op jit(solution)/shard_map/all_to_all | solution.py:451
  (94 shorter events, 16.3 us)
Async XLA Ops:
  7.2 232.7 %copy-start = (bf16[4096,8]{0,1:T(8,128)(2,1)S(1)}, bf16[4096,8]{0,1:T(8,128)(2,1)}, u32[]{:S(2)}) copy-start(bf16[4096,8]{0,1:T(8,128)(2,1)} %param.29) | copy-start | bytes 196612
  7.2 65.3 %all-gather.3.cloned.1.call-start = ((), (), s32[]{:S(2)}) async-start(), calls=%async_computation.3 | async-start | bytes 8650752 | tf_op jit(solution)/shard_map/all_gather | solution.py:362
  7.9 14.6 %collective-permute-start.1 = (bf16[4096,384]{1,0:T(8,128)(2,1)}, bf16[4096,384]{1,0:T(8,128)(2,1)}, u32[]{:S(2)}, u32[]{:S(2)}) collective-permute-start(bf16[4096,384]{1,0:T(8,128)(2,1)} %bitcast.225), channel_id=1, source_target_pairs={{0,8},{8,0},{16,24},{24,16},{32,40},{40,32},{48,56},{56,48},{64,72... | collective-permute-start | bytes 9437192 | tf_op jit(solution)/shard_map/ppermute | solution.py:35
  8.0 14.5 %collective-permute-start.2 = (bf16[4096,384]{1,0:T(8,128)(2,1)}, bf16[4096,384]{1,0:T(8,128)(2,1)}, u32[]{:S(2)}, u32[]{:S(2)}) collective-permute-start(bf16[4096,384]{1,0:T(8,128)(2,1)} %bitcast.228), channel_id=1, source_target_pairs={{0,8},{8,0},{16,24},{24,16},{32,40},{40,32},{48,56},{56,48},{64,72... | collective-permute-start | bytes 9437192 | tf_op jit(solution)/shard_map/ppermute | solution.py:35
  8.5 14.5 %collective-permute-start.3 = (bf16[384,4096]{1,0:T(8,128)(2,1)}, bf16[384,4096]{1,0:T(8,128)(2,1)}, u32[]{:S(2)}, u32[]{:S(2)}) collective-permute-start(bf16[384,4096]{1,0:T(8,128)(2,1)} %bitcast.220), channel_id=1, source_target_pairs={{0,8},{8,0},{16,24},{24,16},{32,40},{40,32},{48,56},{56,48},{64,72... | collective-permute-start | bytes 9437192 | tf_op jit(solution)/shard_map/ppermute | solution.py:35
  9.3 5.3 %collective-permute-start = (bf16[3,1024]{1,0:T(4,128)(2,1)S(1)}, bf16[3,1024]{1,0:T(4,128)(2,1)S(1)}, u32[]{:S(2)}, u32[]{:S(2)}) collective-permute-start(bf16[3,1024]{1,0:T(4,128)(2,1)S(1)} %slice.126), channel_id=1, source_target_pairs={{0,8},{8,16},{16,24},{24,32},{32,40},{40,48},{48,56},{56,64},{64,7... | collective-permute-start | bytes 18440 | tf_op jit(solution)/shard_map/ppermute | solution.py:225
  14.6 0.6 copy-start.9
  22.4 24.7 %copy-start.1 = (f32[128,128]{1,0:T(8,128)S(1)}, f32[128,128]{1,0:T(8,128)}, u32[]{:S(2)}) copy-start(f32[128,128]{1,0:T(8,128)} %get-tuple-element.26.scaled_ref) | copy-start | bytes 196612
  22.5 24.8 %copy-start.2 = (f32[2048]{0:T(1024)S(1)}, f32[2048]{0:T(1024)}, u32[]{:S(2)}) copy-start(f32[2048]{0:T(1024)} %reshape.180.out_ref) | copy-start | bytes 24580
  22.5 24.8 %copy-start.3 = (bf16[128,1024]{1,0:T(8,128)(2,1)S(1)}, bf16[128,1024]{1,0:T(8,128)(2,1)}, u32[]{:S(2)}) copy-start(bf16[128,1024]{1,0:T(8,128)(2,1)} %gate_hbm.1) | copy-start | bytes 786436
  22.5 24.8 %copy-start.4 = (f32[1024,128]{1,0:T(8,128)S(1)}, f32[1024,128]{1,0:T(8,128)}, u32[]{:S(2)}) copy-start(f32[1024,128]{1,0:T(8,128)} %get-tuple-element.22.y_ref) | copy-start | bytes 1572868
  22.5 24.8 %copy-start.5 = (f32[1024,128]{1,0:T(8,128)S(1)}, f32[1024,128]{1,0:T(8,128)}, u32[]{:S(2)}) copy-start(f32[1024,128]{1,0:T(8,128)} %get-tuple-element.23.sums_ref) | copy-start | bytes 1572868
  23.0 1.9 collective-permute-start.4
  26.6 5.3 %collective-permute-start.5 = (f32[136,128]{1,0:T(8,128)S(1)}, f32[136,128]{1,0:T(8,128)S(1)}, u32[]{:S(2)}, u32[]{:S(2)}) collective-permute-start(f32[136,128]{1,0:T(8,128)S(1)} %maximum_bitcast_fusion), channel_id=1, source_target_pairs={{0,16},{8,24},{16,32},{24,40},{32,48},{40,56},{48,0},{56,8},{64,80... | collective-permute-start | bytes 208904 | tf_op jit(solution)/shard_map/ppermute | solution.py:35
  28.4 7.3 %collective-permute-start.6 = (f32[136,128]{1,0:T(8,128)S(1)}, f32[136,128]{1,0:T(8,128)S(1)}, u32[]{:S(2)}, u32[]{:S(2)}) collective-permute-start(f32[136,128]{1,0:T(8,128)S(1)} %maximum_bitcast_fusion), channel_id=1, source_target_pairs={{0,32},{8,40},{16,48},{24,56},{32,0},{40,8},{48,16},{56,24},{64,96... | collective-permute-start | bytes 208904 | tf_op jit(solution)/shard_map/ppermute | solution.py:35
  29.2 7.6 %collective-permute-start.7 = (f32[136,128]{1,0:T(8,128)S(1)}, f32[136,128]{1,0:T(8,128)S(1)}, u32[]{:S(2)}, u32[]{:S(2)}) collective-permute-start(f32[136,128]{1,0:T(8,128)S(1)} %maximum_bitcast_fusion), channel_id=1, source_target_pairs={{0,48},{8,56},{16,0},{24,8},{32,16},{40,24},{48,32},{56,40},{64,11... | collective-permute-start | bytes 208904 | tf_op jit(solution)/shard_map/ppermute | solution.py:35
  37.8 6.3 %collective-permute-start.8 = (f32[136,128]{1,0:T(8,128)S(1)}, f32[136,128]{1,0:T(8,128)S(1)}, u32[]{:S(2)}, u32[]{:S(2)}) collective-permute-start(f32[136,128]{1,0:T(8,128)S(1)} %maximum_bitcast_fusion.1), channel_id=1, source_target_pairs={{0,64},{8,72},{16,80},{24,88},{32,96},{40,104},{48,112},{56,120},{... | collective-permute-start | bytes 208904 | tf_op jit(solution)/shard_map/ppermute | solution.py:35
  39.9 6.1 %collective-permute-start.9 = (f32[136,128]{1,0:T(8,128)S(1)}, f32[136,128]{1,0:T(8,128)S(1)}, u32[]{:S(2)}, u32[]{:S(2)}) collective-permute-start(f32[136,128]{1,0:T(8,128)S(1)} %maximum_bitcast_fusion.1), channel_id=1, source_target_pairs={{0,128},{8,136},{16,144},{24,152},{32,160},{40,168},{48,176},{56,1... | collective-permute-start | bytes 208904 | tf_op jit(solution)/shard_map/ppermute | solution.py:35
  42.8 4.3 %collective-permute-start.10 = (f32[136,128]{1,0:T(8,128)S(1)}, f32[136,128]{1,0:T(8,128)S(1)}, u32[]{:S(2)}, u32[]{:S(2)}) collective-permute-start(f32[136,128]{1,0:T(8,128)S(1)} %maximum_bitcast_fusion.1), channel_id=1, source_target_pairs={{0,192},{8,200},{16,208},{24,216},{32,224},{40,232},{48,240},{56,2... | collective-permute-start | bytes 208904 | tf_op jit(solution)/shard_map/ppermute | solution.py:35
  78.4 7.2 %copy-start.8 = (s32[16,2]{0,1:T(2,128)S(1)}, s32[16,2]{0,1:T(2,128)}, u32[]{:S(2)}) copy-start(s32[16,2]{0,1:T(2,128)} %param.30) | copy-start | bytes 388
  78.4 36.4 %copy-start.6 = (bf16[16,4096]{1,0:T(8,128)(2,1)S(1)}, bf16[16,4096]{1,0:T(8,128)(2,1)}, u32[]{:S(2)}) copy-start(bf16[16,4096]{1,0:T(8,128)(2,1)} %param.27) | copy-start | bytes 393220
  78.4 36.7 %copy-start.7 = (f32[4096]{0:T(1024)S(1)}, f32[4096]{0:T(1024)}, u32[]{:S(2)}) copy-start(f32[4096]{0:T(1024)} %param.28) | copy-start | bytes 49156
  78.4 36.4 %all-to-all-start = ((bf16[8,16,4096]{2,1,0:T(8,128)(2,1)}), bf16[8,16,4096]{2,1,0:T(8,128)(2,1)S(1)}, u32[]{:S(2)}, u32[]{:S(2)}) async-start(bf16[8,16,4096]{2,1,0:T(8,128)(2,1)} %project.1), calls=%async_computation | async-start | bytes 2097152 | tf_op jit(solution)/shard_map/all_to_all | solution.py:381
  132.1 7.2 %collective-permute-start.11 = (bf16[40,4096]{1,0:T(8,128)(2,1)S(1)}, bf16[40,4096]{1,0:T(8,128)(2,1)S(1)}, u32[]{:S(2)}, u32[]{:S(2)}) collective-permute-start(bf16[40,4096]{1,0:T(8,128)(2,1)S(1)} %reshape.174), channel_id=1, source_target_pairs={{0,16},{8,72},{16,32},{24,88},{32,48},{40,104},{48,0},{56,120},{64... | collective-permute-start | bytes 983048 | tf_op jit(solution)/shard_map/ppermute | solution.py:235
  132.8 8.6 %collective-permute-start.13 = (bf16[40,4096]{1,0:T(8,128)(2,1)S(1)}, bf16[40,4096]{1,0:T(8,128)(2,1)S(1)}, u32[]{:S(2)}, u32[]{:S(2)}) collective-permute-start(bf16[40,4096]{1,0:T(8,128)(2,1)S(1)} %reshape.174), channel_id=1, source_target_pairs={{0,48},{8,200},{16,0},{24,216},{32,16},{40,232},{48,32},{56,248},{... | collective-permute-start | bytes 983048 | tf_op jit(solution)/shard_map/ppermute | solution.py:235
  139.3 6.3 %collective-permute-start.12 = (bf16[40,2048]{1,0:T(8,128)(2,1)S(1)}, bf16[40,2048]{1,0:T(8,128)(2,1)S(1)}, u32[]{:S(2)}, u32[]{:S(2)}) collective-permute-start(bf16[40,2048]{1,0:T(8,128)(2,1)S(1)} %slice.184), channel_id=1, source_target_pairs={{0,16},{8,72},{16,32},{24,88},{32,48},{40,104},{48,0},{56,120},{64... | collective-permute-start | bytes 491528 | tf_op jit(solution)/shard_map/ppermute | solution.py:235
  141.3 6.6 %collective-permute-start.14 = (bf16[40,2048]{1,0:T(8,128)(2,1)S(1)}, bf16[40,2048]{1,0:T(8,128)(2,1)S(1)}, u32[]{:S(2)}, u32[]{:S(2)}) collective-permute-start(bf16[40,2048]{1,0:T(8,128)(2,1)S(1)} %slice.185), channel_id=1, source_target_pairs={{0,48},{8,200},{16,0},{24,216},{32,16},{40,232},{48,32},{56,248},{... | collective-permute-start | bytes 491528 | tf_op jit(solution)/shard_map/ppermute | solution.py:235
  141.7 11.9 %collective-permute-start.15 = (bf16[80,4096]{1,0:T(8,128)(2,1)S(1)}, bf16[80,4096]{1,0:T(8,128)(2,1)S(1)}, u32[]{:S(2)}, u32[]{:S(2)}) collective-permute-start(bf16[80,4096]{1,0:T(8,128)(2,1)S(1)} %constant_dynamic-update-slice_fusion.refs_0_), channel_id=1, source_target_pairs={{0,64},{8,24},{16,80},{24,40},{32,96},{40,56},{48,112},{56,8},{64,... | collective-permute-start | bytes 1966088 | tf_op jit(solution)/shard_map/ppermute | solution.py:235
  148.0 11.2 %collective-permute-start.16 = (bf16[80,4096]{1,0:T(8,128)(2,1)S(1)}, bf16[80,4096]{1,0:T(8,128)(2,1)S(1)}, u32[]{:S(2)}, u32[]{:S(2)}) collective-permute-start(bf16[80,4096]{1,0:T(8,128)(2,1)S(1)} %pad_maximum_fusion.refs_1_), channel_id=1, source_target_pairs={{0,192},{8,56},{16,208},{24,8},{32,224},{40,24},{48,240},{56,40},{... | collective-permute-start | bytes 1966088 | tf_op jit(solution)/shard_map/ppermute | solution.py:235
  150.6 19.5 %collective-permute-start.19 = (bf16[80,4096]{1,0:T(8,128)(2,1)S(1)}, bf16[80,4096]{1,0:T(8,128)(2,1)S(1)}, u32[]{:S(2)}, u32[]{:S(2)}) collective-permute-start(bf16[80,4096]{1,0:T(8,128)(2,1)S(1)} %constant_dynamic-update-slice_fusion.refs_0_), channel_id=1, source_target_pairs={{0,192},{8,56},{16,208},{24,8},{32,224},{40,24},{48,240},{56,40},{... | collective-permute-start | bytes 1966088 | tf_op jit(solution)/shard_map/ppermute | solution.py:235
  151.6 18.4 %collective-permute-start.20 = (bf16[80,4096]{1,0:T(8,128)(2,1)S(1)}, bf16[80,4096]{1,0:T(8,128)(2,1)S(1)}, u32[]{:S(2)}, u32[]{:S(2)}) collective-permute-start(bf16[80,4096]{1,0:T(8,128)(2,1)S(1)} %pad_maximum_fusion.refs_1_), channel_id=1, source_target_pairs={{0,64},{8,24},{16,80},{24,40},{32,96},{40,56},{48,112},{56,8},{64,... | collective-permute-start | bytes 1966088 | tf_op jit(solution)/shard_map/ppermute | solution.py:235
  153.6 16.9 %collective-permute-start.17 = (bf16[80,4096]{1,0:T(8,128)(2,1)S(1)}, bf16[80,4096]{1,0:T(8,128)(2,1)S(1)}, u32[]{:S(2)}, u32[]{:S(2)}) collective-permute-start(bf16[80,4096]{1,0:T(8,128)(2,1)S(1)} %collective-permute-done.15.refs_2_), channel_id=1, source_target_pairs={{0,64},{8,24},{16,80},{24,40},{32,96},{40,56},{48,112},{56,8},{64,... | collective-permute-start | bytes 1966088 | tf_op jit(solution)/shard_map/ppermute | solution.py:235
  159.2 14.0 %collective-permute-start.18 = (bf16[80,4096]{1,0:T(8,128)(2,1)S(1)}, bf16[80,4096]{1,0:T(8,128)(2,1)S(1)}, u32[]{:S(2)}, u32[]{:S(2)}) collective-permute-start(bf16[80,4096]{1,0:T(8,128)(2,1)S(1)} %collective-permute-done.16.refs_3_), channel_id=1, source_target_pairs={{0,192},{8,56},{16,208},{24,8},{32,224},{40,24},{48,240},{56,40},{... | collective-permute-start | bytes 1966088 | tf_op jit(solution)/shard_map/ppermute | solution.py:235
  186.0 11.6 %collective-permute-start.26 = (bf16[80,4096]{1,0:T(8,128)(2,1)S(1)}, bf16[80,4096]{1,0:T(8,128)(2,1)S(1)}, u32[]{:S(2)}, u32[]{:S(2)}) collective-permute-start(bf16[80,4096]{1,0:T(8,128)(2,1)S(1)} %get-tuple-element.41), channel_id=1, source_target_pairs={{0,192},{8,56},{16,208},{24,8},{32,224},{40,24},{48,240},{56,40},{... | collective-permute-start | bytes 1966088 | tf_op jit(solution)/shard_map/ppermute | solution.py:235
  189.3 19.1 %collective-permute-start.25 = (bf16[80,4096]{1,0:T(8,128)(2,1)S(1)}, bf16[80,4096]{1,0:T(8,128)(2,1)S(1)}, u32[]{:S(2)}, u32[]{:S(2)}) collective-permute-start(bf16[80,4096]{1,0:T(8,128)(2,1)S(1)} %get-tuple-element.39), channel_id=1, source_target_pairs={{0,64},{8,24},{16,80},{24,40},{32,96},{40,56},{48,112},{56,8},{64,... | collective-permute-start | bytes 1966088 | tf_op jit(solution)/shard_map/ppermute | solution.py:235
  189.3 18.8 %collective-permute-start.22 = (bf16[80,4096]{1,0:T(8,128)(2,1)S(1)}, bf16[80,4096]{1,0:T(8,128)(2,1)S(1)}, u32[]{:S(2)}, u32[]{:S(2)}) collective-permute-start(bf16[80,4096]{1,0:T(8,128)(2,1)S(1)} %get-tuple-element.37), channel_id=1, source_target_pairs={{0,64},{8,24},{16,80},{24,40},{32,96},{40,56},{48,112},{56,8},{64,... | collective-permute-start | bytes 1966088 | tf_op jit(solution)/shard_map/ppermute | solution.py:235
  190.2 27.0 %collective-permute-start.21 = (bf16[80,4096]{1,0:T(8,128)(2,1)S(1)}, bf16[80,4096]{1,0:T(8,128)(2,1)S(1)}, u32[]{:S(2)}, u32[]{:S(2)}) collective-permute-start(bf16[80,4096]{1,0:T(8,128)(2,1)S(1)} %get-tuple-element.35), channel_id=1, source_target_pairs={{0,192},{8,56},{16,208},{24,8},{32,224},{40,24},{48,240},{56,40},{... | collective-permute-start | bytes 1966088 | tf_op jit(solution)/shard_map/ppermute | solution.py:235
  197.9 13.6 %collective-permute-start.27 = (bf16[80,4096]{1,0:T(8,128)(2,1)S(1)}, bf16[80,4096]{1,0:T(8,128)(2,1)S(1)}, u32[]{:S(2)}, u32[]{:S(2)}) collective-permute-start(bf16[80,4096]{1,0:T(8,128)(2,1)S(1)} %add_convert_fusion.1), channel_id=1, source_target_pairs={{0,192},{8,56},{16,208},{24,8},{32,224},{40,24},{48,240},{56,40},{... | collective-permute-start | bytes 1966088 | tf_op jit(solution)/shard_map/ppermute | solution.py:235
  208.3 18.4 %collective-permute-start.23 = (bf16[80,4096]{1,0:T(8,128)(2,1)S(1)}, bf16[80,4096]{1,0:T(8,128)(2,1)S(1)}, u32[]{:S(2)}, u32[]{:S(2)}) collective-permute-start(bf16[80,4096]{1,0:T(8,128)(2,1)S(1)} %add_convert_fusion.2), channel_id=1, source_target_pairs={{0,64},{8,24},{16,80},{24,40},{32,96},{40,56},{48,112},{56,8},{64,... | collective-permute-start | bytes 1966088 | tf_op jit(solution)/shard_map/ppermute | solution.py:235
  211.7 15.3 %collective-permute-start.28 = (bf16[40,4096]{1,0:T(8,128)(2,1)S(1)}, bf16[40,4096]{1,0:T(8,128)(2,1)S(1)}, u32[]{:S(2)}, u32[]{:S(2)}) collective-permute-start(bf16[40,4096]{1,0:T(8,128)(2,1)S(1)} %get-tuple-element.57), channel_id=1, source_target_pairs={{0,32},{8,136},{16,48},{24,152},{32,0},{40,168},{48,16},{56,184},{... | collective-permute-start | bytes 983048 | tf_op jit(solution)/shard_map/ppermute | solution.py:235
  215.2 11.8 %collective-permute-start.29 = (bf16[40,4096]{1,0:T(8,128)(2,1)S(1)}, bf16[40,4096]{1,0:T(8,128)(2,1)S(1)}, u32[]{:S(2)}, u32[]{:S(2)}) collective-permute-start(bf16[40,4096]{1,0:T(8,128)(2,1)S(1)} %get-tuple-element.58), channel_id=1, source_target_pairs={{0,16},{8,72},{16,32},{24,88},{32,48},{40,104},{48,0},{56,120},{64... | collective-permute-start | bytes 983048 | tf_op jit(solution)/shard_map/ppermute | solution.py:235
  226.9 8.4 %collective-permute-start.24 = (bf16[40,4096]{1,0:T(8,128)(2,1)S(1)}, bf16[40,4096]{1,0:T(8,128)(2,1)S(1)}, u32[]{:S(2)}, u32[]{:S(2)}) collective-permute-start(bf16[40,4096]{1,0:T(8,128)(2,1)S(1)} %slice.275), channel_id=1, source_target_pairs={{0,48},{8,200},{16,0},{24,216},{32,16},{40,232},{48,32},{56,248},{... | collective-permute-start | bytes 983048 | tf_op jit(solution)/shard_map/ppermute | solution.py:235
  236.3 14.5 %all-to-all-start.2 = ((bf16[8,160,128]{2,1,0:T(8,128)(2,1)}), bf16[8,160,128]{2,1,0:T(8,128)(2,1)S(1)}, u32[]{:S(2)}, u32[]{:S(2)}) async-start(bf16[8,160,128]{2,1,0:T(8,128)(2,1)} %reshape.175), calls=%async_computation.2 | async-start | bytes 655360 | tf_op jit(solution)/shard_map/all_to_all | solution.py:451
Sparse Core Ops, SparseCore 0:
  10.6 61.8 all-gather.2
